TPU v7x, 32 devices: a whole 2x2x4 slice. The times are simulated.
32 devices in a mesh: seq: 16 (over z, y, core), fsdp: 2 (over x).
Axes of the slice: x: 2, y: 2, z: 4, core: 2. Of those that a mesh axis runs over, the one named last changes fastest.
Arguments:
- patches: bfloat16 [2, 8192, 1024], P('fsdp', 'seq'), may hold values from -6 to 6
- pos_embed: bfloat16 [2, 8192, 1024], P('fsdp', 'seq'), may hold values from -4 to 4
- lengths: int32 [2, 8], P('fsdp'), may hold values from 1 to 2304, 8192 in all within a row
- out_grad: bfloat16 [2, 8192, 1024], P('fsdp', 'seq'), may hold values from -6 to 6
- ln1_gain: bfloat16 [1024], P('fsdp'), may hold values from 0.5 to 1.5
- ln1_bias: bfloat16 [1024], P('fsdp'), may hold values from -1 to 1
- w_qkv: bfloat16 [1024, 3072], P('fsdp'), may hold values from -0.1875 to 0.1875
- b_qv: bfloat16 [2048], P('fsdp'), may hold values from -1 to 1
- w_out: bfloat16 [1024, 1024], P('fsdp'), may hold values from -3 to 3
- b_out: bfloat16 [1024], P('fsdp'), may hold values from -1 to 1
- ln2_gain: bfloat16 [1024], P('fsdp'), may hold values from 0.5 to 1.5
- ln2_bias: bfloat16 [1024], P('fsdp'), may hold values from -1 to 1
- w_fc1: bfloat16 [1024, 4096], P('fsdp'), may hold values from -0.1875 to 0.1875
- b_fc1: bfloat16 [4096], P('fsdp'), may hold values from -1 to 1
- w_fc2: bfloat16 [4096, 1024], P('fsdp'), may hold values from -0.09375 to 0.09375
- b_fc2: bfloat16 [1024], P('fsdp'), may hold values from -1 to 1
Outputs:
- block_out: bfloat16 [2, 8192, 1024], P('fsdp', 'seq')
- patch_grad: float32 [2, 8192, 1024], P('fsdp', 'seq')
- ln1_gain_grad: float32 [1024], P('fsdp')
- ln1_bias_grad: float32 [1024], P('fsdp')
- w_qkv_grad: float32 [1024, 3072], P('fsdp')
- b_qv_grad: float32 [2048], P('fsdp')
- w_out_grad: float32 [1024, 1024], P('fsdp')
- b_out_grad: float32 [1024], P('fsdp')
- ln2_gain_grad: float32 [1024], P('fsdp')
- ln2_bias_grad: float32 [1024], P('fsdp')
- w_fc1_grad: float32 [1024, 4096], P('fsdp')
- b_fc1_grad: float32 [4096], P('fsdp')
- w_fc2_grad: float32 [4096, 1024], P('fsdp')
- b_fc2_grad: float32 [1024], P('fsdp')
Inputs may be any that keep to these rules, and one draw needn't show every extreme that they name: The patches of pack b are its 8 images one after another in the order of lengths[b]; they add up to 8192, and in every pack one image has exactly 2304 patches.
All inputs are finite; a program needn't handle non-finite values.
Results may differ from a plain program's by a relative error of at most 0.0099.
Values may be sent and summed in bfloat16 or wider, within the bound.
No kernel may reach another device: no remote copies, remote signals or barrier semaphores. Data moves between devices by JAX's collectives and lax.ppermute only.
A program may use at most 320 MiB of HBM per device.

v0:
```python
from functools import partial
import math

import jax
import jax.numpy as jnp
from jax import lax
from jax.sharding import PartitionSpec as P

HEADS = 16
HEAD_DIM = 64
LONG = 2304


NORM_EPS = 1e-06
MASKED = -1e30


def shifted(value, axis, steps):
    count = lax.axis_size(axis)
    leading, last = (max(0, -steps), min(count, count - steps))
    return lax.ppermute(value, axis, [(source, source + steps) for source in range(leading, last)])


def norm_forward(hidden, gain_vec, offset_vec):
    centre = hidden - jnp.mean(hidden, axis=-1, keepdims=True)
    spread = jnp.mean(centre * centre, axis=-1, keepdims=True)
    inv_std = lax.rsqrt(spread + NORM_EPS)
    scaled = centre * inv_std
    return (scaled * gain_vec + offset_vec, scaled, inv_std)


def norm_backward(grad_out, scaled, inv_std, gain_vec):
    gain_grad = jnp.sum(grad_out * scaled, axis=0)
    offset_grad = jnp.sum(grad_out, axis=0)
    grad_scaled = grad_out * gain_vec
    grad_in = inv_std * (
        grad_scaled
        - jnp.mean(grad_scaled, axis=-1, keepdims=True)
        - scaled * jnp.mean(grad_scaled * scaled, axis=-1, keepdims=True)
    )
    return (gain_grad, offset_grad, grad_in)


def inner_rows(first_mat, second_mat):
    return lax.dot_general(
        first_mat, second_mat, (((0,), (0,)), ((), ())), preferred_element_type=jnp.float32
    )


def times_transposed(first_mat, second_mat):
    return lax.dot_general(
        first_mat, second_mat, (((1,), (1,)), ((), ())), preferred_element_type=jnp.float32
    )


def segment_rows(image_ends, block_pos, row_count, block_count):
    places = block_pos * row_count + jnp.arange(row_count, dtype=jnp.int32)
    inside = jnp.logical_and(block_pos >= 0, block_pos < block_count)
    labels = jnp.sum((places[:, None] >= image_ends[None, :]).astype(jnp.int32), axis=1)
    return jnp.where(inside, labels, -1)


def body(
    patches,
    pos_embed,
    lengths,
    out_grad,
    ln1_gain,
    ln1_bias,
    w_qkv,
    b_qv,
    w_out,
    b_out,
    ln2_gain,
    ln2_bias,
    w_fc1,
    b_fc1,
    w_fc2,
    b_fc2,
):
    shards = (
        ln1_gain,
        ln1_bias,
        w_qkv,
        b_qv,
        w_out,
        b_out,
        ln2_gain,
        ln2_bias,
        w_fc1,
        b_fc1,
        w_fc2,
        b_fc2,
    )
    gathered = (
        lax.all_gather(shards[0], "fsdp", axis=0, tiled=True),
        lax.all_gather(shards[1], "fsdp", axis=0, tiled=True),
        lax.all_gather(shards[2], "fsdp", axis=0, tiled=True),
        lax.all_gather(shards[3], "fsdp", axis=0, tiled=True),
        lax.all_gather(shards[4], "fsdp", axis=0, tiled=True),
        lax.all_gather(shards[5], "fsdp", axis=0, tiled=True),
        lax.all_gather(shards[6], "fsdp", axis=0, tiled=True),
        lax.all_gather(shards[7], "fsdp", axis=0, tiled=True),
        lax.all_gather(shards[8], "fsdp", axis=0, tiled=True),
        lax.all_gather(shards[9], "fsdp", axis=0, tiled=True),
        lax.all_gather(shards[10], "fsdp", axis=0, tiled=True),
        lax.all_gather(shards[11], "fsdp", axis=0, tiled=True),
    )
    (
        gain_one,
        bias_one,
        qkv_full,
        qv_bias,
        out_full,
        out_bias,
        gain_two,
        bias_two,
        fc1_full,
        fc1_bias,
        fc2_full,
        fc2_bias,
    ) = gathered
    row_count = patches.shape[1]
    model_width = patches.shape[2]
    seq_count = lax.axis_size("seq")
    seq_pos = lax.axis_index("seq")
    image_ends = jnp.cumsum(lengths[0])
    key_reach = (LONG + row_count - 2) // row_count
    hidden = patches[0].astype(jnp.float32) + pos_embed[0].astype(jnp.float32)
    normed_pre, scaled_one, inv_one = norm_forward(
        hidden, gain_one.astype(jnp.float32), bias_one.astype(jnp.float32)
    )
    normed = normed_pre.astype(jnp.bfloat16)
    joined = jnp.dot(normed, qkv_full, preferred_element_type=jnp.float32)
    queries = (joined[:, :model_width] + qv_bias[:model_width].astype(jnp.float32)).astype(
        jnp.bfloat16
    )
    key_vals = jnp.concatenate(
        [
            joined[:, model_width : 2 * model_width],
            joined[:, 2 * model_width :] + qv_bias[model_width:].astype(jnp.float32),
        ],
        axis=1,
    ).astype(jnp.bfloat16)
    blocks = []
    seg_blocks = []
    for offset in range(-key_reach, key_reach + 1):
        if offset == 0:
            blocks.append(key_vals)
        else:
            blocks.append(shifted(key_vals, "seq", -offset))
        seg_blocks.append(segment_rows(image_ends, seq_pos + offset, row_count, seq_count))
    window = jnp.concatenate(blocks, axis=0)
    own_segs = segment_rows(image_ends, seq_pos, row_count, seq_count)
    same_image = own_segs[:, None] == jnp.concatenate(seg_blocks)[None, :]
    pair_count = HEADS // 2
    score_scale = HEAD_DIM ** (-0.5)

    def to_pairs(rows_mat):
        return rows_mat.reshape(rows_mat.shape[0], pair_count, 2, HEAD_DIM).transpose(1, 0, 2, 3)

    def from_pairs(pair_mat):
        return pair_mat.transpose(1, 0, 2, 3).reshape(pair_mat.shape[1], model_width)

    query_pairs = to_pairs(queries)
    key_pairs = to_pairs(window[:, :model_width])
    value_pairs = to_pairs(window[:, model_width:])

    def pair_scores(query_part, key_part):
        scores = (
            jnp.einsum("qhd,khd->hqk", query_part, key_part, preferred_element_type=jnp.float32)
            * score_scale
        )
        return jnp.where(same_image[None], scores, MASKED)

    def pair_forward(pair_item):
        query_part, key_part, value_part = pair_item
        scores = pair_scores(query_part, key_part)
        row_max = jnp.max(scores, axis=-1, keepdims=True)
        exp_scores = jnp.exp(scores - row_max)
        row_total = jnp.sum(exp_scores, axis=-1, keepdims=True)
        prob_rows = exp_scores / row_total
        attended = jnp.einsum(
            "hqk,khd->qhd",
            prob_rows.astype(jnp.bfloat16),
            value_part,
            preferred_element_type=jnp.float32,
        )
        return (attended, row_max + jnp.log(row_total))

    attended, log_total = lax.map(pair_forward, (query_pairs, key_pairs, value_pairs))
    mixed_low = attended.transpose(1, 0, 2, 3).reshape(row_count, model_width).astype(jnp.bfloat16)
    branch = jnp.dot(mixed_low, out_full, preferred_element_type=jnp.float32) + out_bias.astype(
        jnp.float32
    )
    middle = hidden + branch
    normed_two_pre, scaled_two, inv_two = norm_forward(
        middle, gain_two.astype(jnp.float32), bias_two.astype(jnp.float32)
    )
    normed_two = normed_two_pre.astype(jnp.bfloat16)
    inner_sum = jnp.dot(normed_two, fc1_full, preferred_element_type=jnp.float32) + fc1_bias.astype(
        jnp.float32
    )
    active, gelu_pull = jax.vjp(partial(jax.nn.gelu, approximate=True), inner_sum)
    active_low = active.astype(jnp.bfloat16)
    block_out = middle + (
        jnp.dot(active_low, fc2_full, preferred_element_type=jnp.float32)
        + fc2_bias.astype(jnp.float32)
    )
    back_set = (
        lax.all_gather(shards[0], "fsdp", axis=0, tiled=True),
        lax.all_gather(shards[1], "fsdp", axis=0, tiled=True),
        lax.all_gather(shards[2], "fsdp", axis=0, tiled=True),
        lax.all_gather(shards[3], "fsdp", axis=0, tiled=True),
        lax.all_gather(shards[4], "fsdp", axis=0, tiled=True),
        lax.all_gather(shards[5], "fsdp", axis=0, tiled=True),
        lax.all_gather(shards[6], "fsdp", axis=0, tiled=True),
        lax.all_gather(shards[7], "fsdp", axis=0, tiled=True),
        lax.all_gather(shards[8], "fsdp", axis=0, tiled=True),
        lax.all_gather(shards[9], "fsdp", axis=0, tiled=True),
        lax.all_gather(shards[10], "fsdp", axis=0, tiled=True),
        lax.all_gather(shards[11], "fsdp", axis=0, tiled=True),
    )
    gain_one_back = back_set[0].astype(jnp.float32)
    qkv_back = back_set[2]
    out_back = back_set[4]
    gain_two_back = back_set[6].astype(jnp.float32)
    fc1_back = back_set[8]
    fc2_back = back_set[10]
    out_cot = out_grad[0]
    cot_full = out_cot.astype(jnp.float32)
    fc2_grad = inner_rows(active_low, out_cot)
    fc2_bias_grad = jnp.sum(cot_full, axis=0)
    active_grad = times_transposed(out_cot, fc2_back)
    inner_grad = gelu_pull(active_grad)[0].astype(jnp.bfloat16)
    fc1_grad = inner_rows(normed_two, inner_grad)
    fc1_bias_grad = jnp.sum(inner_grad.astype(jnp.float32), axis=0)
    norm_two_grad = times_transposed(inner_grad, fc1_back)
    gain_two_grad, bias_two_grad, middle_from_norm = norm_backward(
        norm_two_grad, scaled_two, inv_two, gain_two_back
    )
    middle_grad = cot_full + middle_from_norm
    branch_grad = middle_grad.astype(jnp.bfloat16)
    out_weight_grad = inner_rows(mixed_low, branch_grad)
    out_bias_grad = jnp.sum(branch_grad.astype(jnp.float32), axis=0)
    mixed_grad = times_transposed(branch_grad, out_back).astype(jnp.bfloat16)
    grad_pairs = to_pairs(mixed_grad)

    def pair_backward(pair_item):
        query_part, key_part, value_part, grad_part, log_part = pair_item
        scores = pair_scores(query_part, key_part)
        prob_rows = jnp.exp(scores - log_part)
        prob_grad = jnp.einsum(
            "qhd,khd->hqk", grad_part, value_part, preferred_element_type=jnp.float32
        )
        row_dot = jnp.sum(prob_rows * prob_grad, axis=-1, keepdims=True)
        score_grad = (prob_rows * (prob_grad - row_dot)).astype(jnp.bfloat16)
        query_grad = (
            jnp.einsum("hqk,khd->qhd", score_grad, key_part, preferred_element_type=jnp.float32)
            * score_scale
        )
        key_grad = (
            jnp.einsum("hqk,qhd->khd", score_grad, query_part, preferred_element_type=jnp.float32)
            * score_scale
        )
        value_grad = jnp.einsum(
            "hqk,qhd->khd",
            prob_rows.astype(jnp.bfloat16),
            grad_part,
            preferred_element_type=jnp.float32,
        )
        return (query_grad, key_grad, value_grad)

    query_all, key_all, value_all = lax.map(
        pair_backward, (query_pairs, key_pairs, value_pairs, grad_pairs, log_total)
    )
    query_grad = from_pairs(query_all).astype(jnp.bfloat16)
    window_grad = jnp.concatenate([from_pairs(key_all), from_pairs(value_all)], axis=1)
    kv_grad = window_grad[key_reach * row_count : (key_reach + 1) * row_count]
    for offset in range(-key_reach, key_reach + 1):
        if offset != 0:
            grad_piece = window_grad[
                (offset + key_reach) * row_count : (offset + key_reach + 1) * row_count
            ]
            kv_grad = kv_grad + shifted(grad_piece, "seq", offset)
    kv_low = kv_grad.astype(jnp.bfloat16)
    qkv_grad = jnp.concatenate([query_grad, kv_low], axis=1)
    qv_bias_grad = jnp.concatenate(
        [
            jnp.sum(query_grad.astype(jnp.float32), axis=0),
            jnp.sum(kv_low[:, model_width:].astype(jnp.float32), axis=0),
        ]
    )
    qkv_weight_grad = inner_rows(normed, qkv_grad)
    norm_one_grad = times_transposed(qkv_grad, qkv_back)
    gain_one_grad, bias_one_grad, hidden_from_norm = norm_backward(
        norm_one_grad, scaled_one, inv_one, gain_one_back
    )
    patch_grad = middle_grad + hidden_from_norm
    grad_list = (
        gain_one_grad,
        bias_one_grad,
        qkv_weight_grad,
        qv_bias_grad,
        out_weight_grad,
        out_bias_grad,
        gain_two_grad,
        bias_two_grad,
        fc1_grad,
        fc1_bias_grad,
        fc2_grad,
        fc2_bias_grad,
    )
    grad_shards = (
        lax.psum_scatter(grad_list[0], "fsdp", scatter_dimension=0, tiled=True),
        lax.psum_scatter(grad_list[1], "fsdp", scatter_dimension=0, tiled=True),
        lax.psum_scatter(grad_list[2], "fsdp", scatter_dimension=0, tiled=True),
        lax.psum_scatter(grad_list[3], "fsdp", scatter_dimension=0, tiled=True),
        lax.psum_scatter(grad_list[4], "fsdp", scatter_dimension=0, tiled=True),
        lax.psum_scatter(grad_list[5], "fsdp", scatter_dimension=0, tiled=True),
        lax.psum_scatter(grad_list[6], "fsdp", scatter_dimension=0, tiled=True),
        lax.psum_scatter(grad_list[7], "fsdp", scatter_dimension=0, tiled=True),
        lax.psum_scatter(grad_list[8], "fsdp", scatter_dimension=0, tiled=True),
        lax.psum_scatter(grad_list[9], "fsdp", scatter_dimension=0, tiled=True),
        lax.psum_scatter(grad_list[10], "fsdp", scatter_dimension=0, tiled=True),
        lax.psum_scatter(grad_list[11], "fsdp", scatter_dimension=0, tiled=True),
    )
    grad_totals = lax.psum(
        (
            grad_shards[0],
            grad_shards[1],
            grad_shards[2],
            grad_shards[3],
            grad_shards[4],
            grad_shards[5],
            grad_shards[6],
            grad_shards[7],
            grad_shards[8],
            grad_shards[9],
            grad_shards[10],
            grad_shards[11],
        ),
        "seq",
    )
    grad_scale = 1.0 / (lax.axis_size("fsdp") * math.sqrt(row_count * seq_count))
    return (
        block_out.astype(jnp.bfloat16)[None],
        patch_grad[None],
        grad_totals[0] * grad_scale,
        grad_totals[1] * grad_scale,
        grad_totals[2] * grad_scale,
        grad_totals[3] * grad_scale,
        grad_totals[4] * grad_scale,
        grad_totals[5] * grad_scale,
        grad_totals[6] * grad_scale,
        grad_totals[7] * grad_scale,
        grad_totals[8] * grad_scale,
        grad_totals[9] * grad_scale,
        grad_totals[10] * grad_scale,
        grad_totals[11] * grad_scale,
    )


def solution(mesh):
    in_specs = (
        P("fsdp", "seq", None),
        P("fsdp", "seq", None),
        P("fsdp", None),
        P("fsdp", "seq", None),
        P("fsdp"),
        P("fsdp"),
        P("fsdp", None),
        P("fsdp"),
        P("fsdp", None),
        P("fsdp"),
        P("fsdp"),
        P("fsdp"),
        P("fsdp", None),
        P("fsdp"),
        P("fsdp", None),
        P("fsdp"),
    )
    out_specs = (
        P("fsdp", "seq", None),
        P("fsdp", "seq", None),
        P("fsdp"),
        P("fsdp"),
        P("fsdp", None),
        P("fsdp"),
        P("fsdp", None),
        P("fsdp"),
        P("fsdp"),
        P("fsdp"),
        P("fsdp", None),
        P("fsdp"),
        P("fsdp", None),
        P("fsdp"),
    )
    return jax.shard_map(body, mesh=mesh, in_specs=in_specs, out_specs=out_specs, check_vma=False)
```

profile of v0, /device:TPU:0, one launch (start us, length us, event | category | flops | bytes accessed | tf_op | source)
XLA Modules:
  0.0 2991.3 jit_solution(12100147011240098556)
XLA Ops:
  25.2 67.4 %all-gather.11.cloned.1.call-done = bf16[1024,3072]{1,0:T(8,128)(2,1)} async-done(((bf16[512,3072]{1,0:T(8,128)(2,1)}), bf16[1024,3072]{1,0:T(8,128)(2,1)}) %all-gather.11.cloned.1.call-update) | async-done | bytes 6291472 | tf_op jit(solution)/shard_map/all_gather | solution.py:98
  150.4 43.6 %collective-permute-done.1 = bf16[512,2048]{1,0:T(8,128)(2,1)} collective-permute-done((bf16[512,2048]{1,0:T(8,128)(2,1)}, bf16[512,2048]{1,0:T(8,128)(2,1)}, u32[]{:S(2)}, u32[]{:S(2)}) %collective-permute-start.1) | collective-permute-done | bytes 2097184 | tf_op jit(solution)/shard_map/ppermute | solution.py:21
  199.7 92.8 %collective-permute-done.3 = bf16[512,2048]{1,0:T(8,128)(2,1)} collective-permute-done((bf16[512,2048]{1,0:T(8,128)(2,1)}, bf16[512,2048]{1,0:T(8,128)(2,1)}, u32[]{:S(2)}, u32[]{:S(2)}) %collective-permute-start.3) | collective-permute-done | bytes 2097184 | tf_op jit(solution)/shard_map/ppermute | solution.py:21
  306.1 51.2 %collective-permute-done.8 = bf16[512,2048]{1,0:T(8,128)(2,1)S(1)} collective-permute-done((bf16[512,2048]{1,0:T(8,128)(2,1)}, bf16[512,2048]{1,0:T(8,128)(2,1)S(1)}, u32[]{:S(2)}, u32[]{:S(2)}) %collective-permute-start.8) | collective-permute-done | bytes 2097184 | tf_op jit(solution)/shard_map/ppermute | solution.py:21
  397.2 287.6 %while.28 = (s32[]{:T(128)}, bf16[8,512,2,64]{1,3,2,0:T(8,128)(2,1)S(1)}, f32[8,2,512,1]{2,1,3,0:T(2,128)S(1)}, bf16[8,5632,2,64]{1,3,2,0:T(8,128)(2,1)}, bf16[8...) while((s32[]{:T(128)}, ...), condition=%wide.region_17.18_spmd.clone, body=%wide.region_14.17_spmd.clone.sunk | while | flops 1548483584 | bytes 84076640 | solution.py:191
  727.4 531.1 %while.29 = (s32[]{:T(128)}, bf16[8,512,2,64]{1,3,2,0:T(8,128)(2,1)}, f32[8,5632,2,64]{1,3,2,0:T(8,128)}, f32[8,5632,2,64]{1,3,2,0:T(8,128)}, bf16[8,5632,2,64]{...) while((s32[]{:T(128)}, ...), condition=%wide.region_24.25_spmd.clone, body=%wide.region_22.24_spmd.clone.sunk | while | flops 3746561024 | bytes 206488816 | solution.py:274
  740.3 17.3 multiply_reduce_fusion.10
  873.0 17.3 multiply_reduce_fusion.10
  939.3 17.3 multiply_reduce_fusion.10
  1005.7 17.3 multiply_reduce_fusion.10
  1072.1 17.3 multiply_reduce_fusion.10
  1204.7 17.3 multiply_reduce_fusion.10
  1258.6 26.0 fusion.83
  1284.6 49.5 %collective-permute-start.19 = (f32[512,2048]{0,1:T(8,128)}, f32[512,2048]{0,1:T(8,128)}, u32[]{:S(2)}, u32[]{:S(2)}) collective-permute-start(f32[512,2048]{0,1:T(8,128)} %get-tuple-element.250), channel_id=1, source_target_pairs={{0,10},{2,12},{4,14},{6,16},{8,18},{10,20},{12,22},{14,24},{16,26}... | collective-permute-start | bytes 12582920 | tf_op jit(solution)/shard_map/ppermute | solution.py:21
  1338.7 27.0 collective-permute-start.18
  1379.6 43.8 %collective-permute-done.19 = f32[512,2048]{0,1:T(8,128)} collective-permute-done((f32[512,2048]{0,1:T(8,128)}, f32[512,2048]{0,1:T(8,128)}, u32[]{:S(2)}, u32[]{:S(2)}) %collective-permute-start.19) | collective-permute-done | bytes 4194336 | tf_op jit(solution)/shard_map/ppermute | solution.py:21
  1424.7 88.6 %collective-permute-done.18 = f32[512,2048]{0,1:T(8,128)} collective-permute-done((f32[512,2048]{0,1:T(8,128)}, f32[512,2048]{0,1:T(8,128)}, u32[]{:S(2)}, u32[]{:S(2)}) %collective-permute-start.18) | collective-permute-done | bytes 4194336 | tf_op jit(solution)/shard_map/ppermute | solution.py:21
  1515.9 211.4 %collective-permute-done.16 = f32[512,2048]{0,1:T(8,128)} collective-permute-done((f32[512,2048]{0,1:T(8,128)}, f32[512,2048]{0,1:T(8,128)}, u32[]{:S(2)}, u32[]{:S(2)}) %collective-permute-start.16) | collective-permute-done | bytes 4194336 | tf_op jit(solution)/shard_map/ppermute | solution.py:21
  1730.1 116.7 %collective-permute-done.11 = f32[512,2048]{0,1:T(8,128)} collective-permute-done((f32[512,2048]{0,1:T(8,128)}, f32[512,2048]{0,1:T(8,128)}, u32[]{:S(2)}, u32[]{:S(2)}) %collective-permute-start.11) | collective-permute-done | bytes 4194336 | tf_op jit(solution)/shard_map/ppermute | solution.py:21
  1912.5 222.1 %reduce-scatter.5.cloned.1.call-done = f32[512,3072]{1,0:T(8,128)} async-done(((f32[1024,3072]{1,0:T(8,128)}), f32[512,3072]{1,0:T(8,128)}) %reduce-scatter.5.cloned.1.call-update) | async-done | bytes 6291472 | tf_op jit(solution)/shard_map/reduce_scatter | solution.py:317
  2134.7 191.6 %reduce-scatter.9.cloned.1.call-done = f32[512,4096]{1,0:T(8,128)} async-done(((f32[1024,4096]{1,0:T(8,128)}), f32[512,4096]{1,0:T(8,128)}) %reduce-scatter.9.cloned.1.call-update) | async-done | bytes 8388624 | tf_op jit(solution)/shard_map/reduce_scatter | solution.py:323
  2326.3 191.4 %reduce-scatter.11.cloned.1.call-done = f32[2048,1024]{1,0:T(8,128)} async-done(((f32[4096,1024]{1,0:T(8,128)}), f32[2048,1024]{1,0:T(8,128)}) %reduce-scatter.11.cloned.1.call-update) | async-done | bytes 8388624 | tf_op jit(solution)/shard_map/reduce_scatter | solution.py:325
  2557.5 63.1 %all-reduce.8 = (f32[512]{0:T(512)S(1)}, f32[512]{0:T(512)S(1)}, f32[1024]{0:T(1024)S(1)}, f32[512]{0:T(512)S(1)}, f32[512]{0:T(512)S(1)}, /*index=5*/f32[512]{0:T(512)S(1)}, f32[2048]{0:T(1024)S(1)}, f32[512]{0:T(512)S(1)}) all-reduce(f32[512]{0:T(512)S(1)} %dynamic-slice.1, ...), channel_id=1, replica_groups=mesh['seq'=16,'fsdp'=2] {'seq'}, use_global_device_ids=true, to_apply=%region_29.30 | all-reduce | flops 6144 | bytes 49152 | tf_op jit(solution)/shard_map/psum | solution.py:328
  2629.4 337.4 %all-reduce.13.cloned.1.call-done = (f32[512,3072]{1,0:T(8,128)}, f32[512,1024]{1,0:T(8,128)}, f32[512,4096]{1,0:T(8,128)}, f32[2048,1024]{1,0:T(8,128)}) async-done(((f32[512,3072]{1,0:T(8,128)}, f32[512,1024]{1,0:T(8,128)}, f32[512,4096]{1,0:T(8,128)}, f32[2048,1024]{1,0:T(8,128)}), (f32[512,3072]{1,0:T(8,128)}, f32[512,1024]{1,0:T(8,128)}, f32[512,4096]{1,0:T(8,128)}, ...) | async-done | bytes 25165840 | tf_op jit(solution)/shard_map/psum | solution.py:328
  (450 shorter events, 1045.4 us)
Async XLA Ops:
  7.9 677.0 %all-gather.13.cloned.1.call-start = ((), (), s32[]{:S(2)}) async-start(), calls=%async_computation.5 | async-start | bytes 3145728 | tf_op jit(solution)/shard_map/all_gather | solution.py:100
  8.7 681.3 %all-gather.15.cloned.1.call-start = ((), (), s32[]{:S(2)}) async-start(), calls=%async_computation.6 | async-start | bytes 12582912 | tf_op jit(solution)/shard_map/all_gather | solution.py:104
  9.5 692.7 %all-gather.17.cloned.1.call-start = ((), (), s32[]{:S(2)}) async-start(), calls=%async_computation.7 | async-start | bytes 12582912 | tf_op jit(solution)/shard_map/all_gather | solution.py:106
  10.0 1902.5 %reduce-scatter.7.cloned.1.call-start = ((), (), s32[]{:S(2)}) async-start(), calls=%async_computation.9 | async-start | bytes 6291456 | tf_op jit(solution)/shard_map/reduce_scatter | solution.py:319
  105.1 88.9 %collective-permute-start.1 = (bf16[512,2048]{1,0:T(8,128)(2,1)}, bf16[512,2048]{1,0:T(8,128)(2,1)}, u32[]{:S(2)}, u32[]{:S(2)}) collective-permute-start(bf16[512,2048]{1,0:T(8,128)(2,1)} %pad_maximum_fusion.2), channel_id=1, source_target_pairs={{0,8},{2,10},{4,12},{6,14},{8,16},{10,18},{12,20},{14,22},{16,24},... | collective-permute-start | bytes 6291464 | tf_op jit(solution)/shard_map/ppermute | solution.py:21
  114.1 178.4 %collective-permute-start.3 = (bf16[512,2048]{1,0:T(8,128)(2,1)}, bf16[512,2048]{1,0:T(8,128)(2,1)}, u32[]{:S(2)}, u32[]{:S(2)}) collective-permute-start(bf16[512,2048]{1,0:T(8,128)(2,1)} %pad_maximum_fusion.2), channel_id=1, source_target_pairs={{0,4},{2,6},{4,8},{6,10},{8,12},{10,14},{12,16},{14,18},{16,20},{1... | collective-permute-start | bytes 6291464 | tf_op jit(solution)/shard_map/ppermute | solution.py:21
  137.4 158.1 %collective-permute-start.4 = (bf16[512,2048]{1,0:T(8,128)(2,1)}, bf16[512,2048]{1,0:T(8,128)(2,1)}, u32[]{:S(2)}, u32[]{:S(2)}) collective-permute-start(bf16[512,2048]{1,0:T(8,128)(2,1)} %pad_maximum_fusion.2), channel_id=1, source_target_pairs={{0,2},{2,4},{4,6},{6,8},{8,10},{10,12},{12,14},{14,16},{16,18},{18... | collective-permute-start | bytes 6291464 | tf_op jit(solution)/shard_map/ppermute | solution.py:21
  149.1 153.4 %collective-permute-start.5 = (bf16[512,2048]{1,0:T(8,128)(2,1)}, bf16[512,2048]{1,0:T(8,128)(2,1)}, u32[]{:S(2)}, u32[]{:S(2)}) collective-permute-start(bf16[512,2048]{1,0:T(8,128)(2,1)} %pad_maximum_fusion.2), channel_id=1, source_target_pairs={{2,0},{4,2},{6,4},{8,6},{10,8},{12,10},{14,12},{16,14},{18,16},{20... | collective-permute-start | bytes 6291464 | tf_op jit(solution)/shard_map/ppermute | solution.py:21
  194.0 110.2 %collective-permute-start.6 = (bf16[512,2048]{1,0:T(8,128)(2,1)}, bf16[512,2048]{1,0:T(8,128)(2,1)}, u32[]{:S(2)}, u32[]{:S(2)}) collective-permute-start(bf16[512,2048]{1,0:T(8,128)(2,1)} %pad_maximum_fusion.2), channel_id=1, source_target_pairs={{4,0},{6,2},{8,4},{10,6},{12,8},{14,10},{16,12},{18,14},{20,16},{2... | collective-permute-start | bytes 6291464 | tf_op jit(solution)/shard_map/ppermute | solution.py:21
  196.6 109.3 %collective-permute-start.7 = (bf16[512,2048]{1,0:T(8,128)(2,1)}, bf16[512,2048]{1,0:T(8,128)(2,1)S(1)}, u32[]{:S(2)}, u32[]{:S(2)}) collective-permute-start(bf16[512,2048]{1,0:T(8,128)(2,1)} %pad_maximum_fusion.2), channel_id=1, source_target_pairs={{6,0},{8,2},{10,4},{12,6},{14,8},{16,10},{18,12},{20,14},{22,16},{... | collective-permute-start | bytes 6291464 | tf_op jit(solution)/shard_map/ppermute | solution.py:21
  1284.6 138.8 %collective-permute-start.19 = (f32[512,2048]{0,1:T(8,128)}, f32[512,2048]{0,1:T(8,128)}, u32[]{:S(2)}, u32[]{:S(2)}) collective-permute-start(f32[512,2048]{0,1:T(8,128)} %get-tuple-element.250), channel_id=1, source_target_pairs={{0,10},{2,12},{4,14},{6,16},{8,18},{10,20},{12,22},{14,24},{16,26}... | collective-permute-start | bytes 12582920 | tf_op jit(solution)/shard_map/ppermute | solution.py:21
  1338.7 174.6 %collective-permute-start.18 = (f32[512,2048]{0,1:T(8,128)}, f32[512,2048]{0,1:T(8,128)}, u32[]{:S(2)}, u32[]{:S(2)}) collective-permute-start(f32[512,2048]{0,1:T(8,128)} %fusion.71), channel_id=1, source_target_pairs={{0,8},{2,10},{4,12},{6,14},{8,16},{10,18},{12,20},{14,22},{16,24},... | collective-permute-start | bytes 12582920 | tf_op jit(solution)/shard_map/ppermute | solution.py:21
  1365.7 148.9 %collective-permute-start.17 = (f32[512,2048]{0,1:T(8,128)}, f32[512,2048]{0,1:T(8,128)}, u32[]{:S(2)}, u32[]{:S(2)}) collective-permute-start(f32[512,2048]{0,1:T(8,128)} %get-tuple-element.249), channel_id=1, source_target_pairs={{0,6},{2,8},{4,10},{6,12},{8,14},{10,16},{12,18},{14,20},{16,22},{... | collective-permute-start | bytes 12582920 | tf_op jit(solution)/shard_map/ppermute | solution.py:21
  1369.7 357.5 %collective-permute-start.16 = (f32[512,2048]{0,1:T(8,128)}, f32[512,2048]{0,1:T(8,128)}, u32[]{:S(2)}, u32[]{:S(2)}) collective-permute-start(f32[512,2048]{0,1:T(8,128)} %get-tuple-element.248), channel_id=1, source_target_pairs={{0,4},{2,6},{4,8},{6,10},{8,12},{10,14},{12,16},{14,18},{16,20},{1... | collective-permute-start | bytes 12582920 | tf_op jit(solution)/shard_map/ppermute | solution.py:21
  1373.0 355.6 %collective-permute-start.15 = (f32[512,2048]{0,1:T(8,128)}, f32[512,2048]{0,1:T(8,128)}, u32[]{:S(2)}, u32[]{:S(2)}) collective-permute-start(f32[512,2048]{0,1:T(8,128)} %get-tuple-element.247), channel_id=1, source_target_pairs={{0,2},{2,4},{4,6},{6,8},{8,10},{10,12},{12,14},{14,16},{16,18},{18... | collective-permute-start | bytes 12582920 | tf_op jit(solution)/shard_map/ppermute | solution.py:21
  1379.6 755.1 %reduce-scatter.5.cloned.1.call-start = ((), (), s32[]{:S(2)}) async-start(), calls=%async_computation.8 | async-start | bytes 18874368 | tf_op jit(solution)/shard_map/reduce_scatter | solution.py:317
  1423.4 306.6 %collective-permute-start.14 = (f32[512,2048]{0,1:T(8,128)}, f32[512,2048]{0,1:T(8,128)}, u32[]{:S(2)}, u32[]{:S(2)}) collective-permute-start(f32[512,2048]{0,1:T(8,128)} %get-tuple-element.246), channel_id=1, source_target_pairs={{2,0},{4,2},{6,4},{8,6},{10,8},{12,10},{14,12},{16,14},{18,16},{20... | collective-permute-start | bytes 12582920 | tf_op jit(solution)/shard_map/ppermute | solution.py:21
  1513.3 216.8 %collective-permute-start.13 = (f32[512,2048]{0,1:T(8,128)}, f32[512,2048]{0,1:T(8,128)}, u32[]{:S(2)}, u32[]{:S(2)}) collective-permute-start(f32[512,2048]{0,1:T(8,128)} %get-tuple-element.245), channel_id=1, source_target_pairs={{4,0},{6,2},{8,4},{10,6},{12,8},{14,10},{16,12},{18,14},{20,16},{2... | collective-permute-start | bytes 12582920 | tf_op jit(solution)/shard_map/ppermute | solution.py:21
  1514.6 215.5 %collective-permute-start.12 = (f32[512,2048]{0,1:T(8,128)}, f32[512,2048]{0,1:T(8,128)}, u32[]{:S(2)}, u32[]{:S(2)}) collective-permute-start(f32[512,2048]{0,1:T(8,128)} %get-tuple-element.244), channel_id=1, source_target_pairs={{6,0},{8,2},{10,4},{12,6},{14,8},{16,10},{18,12},{20,14},{22,16},{... | collective-permute-start | bytes 12582920 | tf_op jit(solution)/shard_map/ppermute | solution.py:21
  1727.3 119.5 %collective-permute-start.11 = (f32[512,2048]{0,1:T(8,128)}, f32[512,2048]{0,1:T(8,128)}, u32[]{:S(2)}, u32[]{:S(2)}) collective-permute-start(f32[512,2048]{0,1:T(8,128)} %get-tuple-element.243), channel_id=1, source_target_pairs={{8,0},{10,2},{12,4},{14,6},{16,8},{18,10},{20,12},{22,14},{24,16},... | collective-permute-start | bytes 12582920 | tf_op jit(solution)/shard_map/ppermute | solution.py:21
  1728.6 126.1 %collective-permute-start.10 = (f32[512,2048]{0,1:T(8,128)}, f32[512,2048]{0,1:T(8,128)}, u32[]{:S(2)}, u32[]{:S(2)}) collective-permute-start(f32[512,2048]{0,1:T(8,128)} %get-tuple-element.242), channel_id=1, source_target_pairs={{10,0},{12,2},{14,4},{16,6},{18,8},{20,10},{22,12},{24,14},{26,16}... | collective-permute-start | bytes 12582920 | tf_op jit(solution)/shard_map/ppermute | solution.py:21
  1882.0 444.2 %reduce-scatter.9.cloned.1.call-start = ((), (), s32[]{:S(2)}) async-start(), calls=%async_computation.10 | async-start | bytes 25165824 | tf_op jit(solution)/shard_map/reduce_scatter | solution.py:323
  1896.0 621.7 %reduce-scatter.11.cloned.1.call-start = ((), (), s32[]{:S(2)}) async-start(), calls=%async_computation.11 | async-start | bytes 25165824 | tf_op jit(solution)/shard_map/reduce_scatter | solution.py:325
  1912.4 1054.3 %all-reduce.13.cloned.1.call-start = ((), (), s32[]{:S(2)}) async-start(), calls=%async_computation.12 | async-start | bytes 50331648 | tf_op jit(solution)/shard_map/psum | solution.py:328
  (94 other events, 3148.6 us)
Sparse Core Ops, SparseCore 0:
  9.6 83.0 all-gather.10
  94.2 33.2 all-gather.12
  129.0 104.1 all-gather.14
  234.6 103.9 all-gather.16
  1379.7 50.6 reduce-scatter.6
  1882.2 252.4 reduce-scatter.4
  2137.1 189.1 reduce-scatter.8
  2328.5 189.0 reduce-scatter.10
  2523.3 443.3 all-reduce.12
where the time goes:
time: 3000 us; the launch traced here: 2990 us
  waiting for transfers between devices  1680 us (56%)
  matrix products  684 us (23%)
  other arithmetic  323 us (11%)
  starting transfers between devices  120 us (4%)
  blocking collectives  106 us (4%)
  local copies, waits for them, and re-layouts  60 us (2%)
    ppermute x20, waiting for transfers between devices, shifted(): lax.ppermute(value, axis, [(source, source + steps) for source in range(l...  666 us
    psum x1, waiting for transfers between devices, body(): lax.psum((grad_shards[0], grad_shards[1], grad_shards[2], grad_shards[3],...  337 us
    dot_general x16, matrix products, pair_scores(): jnp.einsum('qhd,khd->hqk', query_part, key_part, preferred_element_type=j...  231 us
    reduce_scatter x1, waiting for transfers between devices, body(): lax.psum_scatter(grad_list[2], 'fsdp', scatter_dimension=0, tiled=True)  222 us
    reduce_scatter x1, waiting for transfers between devices, body(): lax.psum_scatter(grad_list[8], 'fsdp', scatter_dimension=0, tiled=True)  192 us
    reduce_scatter x1, waiting for transfers between devices, body(): lax.psum_scatter(grad_list[10], 'fsdp', scatter_dimension=0, tiled=True)  191 us
    convert_element_type x8, other arithmetic, pair_backward(): score_grad = (prob_rows * (prob_grad - row_dot)).astype(jnp.bfloat16)  122 us
    ppermute x20, starting transfers between devices, shifted(): lax.ppermute(value, axis, [(source, source + steps) for source in range(l...  119 us
  transfers between devices with their start and end apart: 29, of which 15 were waited for; matrix products, arithmetic and copies ran while one was open for 16% of the time, Pallas kernels for 0%

commit v1 on v0

v1 whole, which is shorter than its diff:
```python
import math
from functools import partial

import jax
import jax.numpy as jnp
from jax import lax
from jax.experimental import pallas as pl
from jax.experimental.pallas import tpu as pltpu
from jax.sharding import Mesh, PartitionSpec as P

HEADS = 16
LONG = 2304
NORM_EPS = 1e-06
HEAD_DIM = 64
BLOCK = 512
FAR = 1e30
QB = 512
KB = 512


def rows_dot(a, b):
    return lax.dot_general(a, b, (((1,), (0,)), ((), ())), preferred_element_type=jnp.float32)


def membership(ends_ref, count, first, width):
    place = first + lax.broadcasted_iota(jnp.int32, (16, width), 1)
    row = lax.broadcasted_iota(jnp.int32, (16, width), 0)
    low = jnp.zeros((16, width), jnp.int32)
    high = jnp.zeros((16, width), jnp.int32)
    for i in range(count):
        begin = ends_ref[i - 1] if i > 0 else 0
        low = jnp.where(row == i, begin, low)
        high = jnp.where(row == i, ends_ref[i], high)
    return jnp.where((place >= low) & (place < high), 1.0, 0.0)


def image_span(ends_ref, count, first, last):
    low = jnp.int32(0)
    high = ends_ref[count - 1]
    for i in range(count - 1):
        end = ends_ref[i]
        low = jnp.where(end <= first, end, low)
    for i in range(count - 2, -1, -1):
        end = ends_ref[i]
        high = jnp.where(end > last, end, high)
    return low, high


def split3(x):
    top = x.astype(jnp.bfloat16)
    rest = x - top.astype(jnp.float32)
    mid = rest.astype(jnp.bfloat16)
    low = (rest - mid.astype(jnp.float32)).astype(jnp.bfloat16)
    return [top.astype(jnp.float32), mid.astype(jnp.float32), low.astype(jnp.float32)]


def forward_kernel(count, shift, ends_ref, base_ref, q_ref, k_ref, v_ref, o_ref, log_ref, qa, kn, va):
    q_blocks = q_ref.shape[0]
    k_blocks = k_ref.shape[0]
    key_count = k_blocks * BLOCK
    base = base_ref[0]

    @pl.loop(0, k_blocks)
    def _(i):
        at = pl.ds(pl.multiple_of(i * BLOCK, BLOCK), BLOCK)
        away = (membership(ends_ref, count, base - shift + i * BLOCK, BLOCK) - 1.0) * FAR
        both = jnp.concatenate([k_ref[i].astype(jnp.float32), away], axis=0)
        kn[at, :] = both.T.astype(jnp.bfloat16)
        va[:, at] = jnp.concatenate(
            [v_ref[i].astype(jnp.float32), jnp.ones((16, BLOCK), jnp.float32)], axis=0
        ).astype(jnp.bfloat16)

    @pl.loop(0, q_blocks)
    def _(i):
        at = pl.ds(pl.multiple_of(i * BLOCK, BLOCK), BLOCK)
        inside = membership(ends_ref, count, base + i * BLOCK, BLOCK)
        qa[:, at] = jnp.concatenate(
            [q_ref[i].astype(jnp.float32) * (HEAD_DIM ** -0.5), inside], axis=0
        ).astype(jnp.bfloat16)

    per = BLOCK // QB

    @pl.loop(0, q_blocks * per)
    def _(i):
        q_part = qa[:, pl.ds(pl.multiple_of(i * QB, QB), QB)]
        first = base + i * QB
        low, high = image_span(ends_ref, count, first, first + QB - 1)
        low = jnp.maximum(low - base + shift, 0) // KB
        high = jnp.minimum(high - base + shift + KB - 1, key_count) // KB

        def step(j, carry):
            top, acc = carry
            at = pl.ds(pl.multiple_of(j * KB, KB), KB)
            scores = rows_dot(kn[at, :], q_part)
            new_top = jnp.maximum(top, jnp.max(scores, axis=0, keepdims=True))
            weights = jnp.exp(scores - new_top)
            acc = acc * jnp.exp(top - new_top) + rows_dot(va[:, at], weights.astype(jnp.bfloat16))
            return new_top, acc

        top, acc = lax.fori_loop(
            low,
            high,
            step,
            (jnp.full((1, QB), -3e38, jnp.float32), jnp.zeros((HEAD_DIM + 16, QB), jnp.float32)),
        )
        total = acc[HEAD_DIM : HEAD_DIM + 1]
        o_ref[i // per, :, pl.ds(pl.multiple_of((i % per) * QB, QB), QB)] = (
            acc[:HEAD_DIM] / total
        ).astype(jnp.bfloat16)
        log_ref[:, pl.ds(pl.multiple_of(i * QB, QB), QB)] = top + jnp.log(total)


def backward_kernel(
    count, shift, ends_ref, base_ref, q_ref, k_ref, v_ref, o_ref, do_ref, log_ref,
    dq_ref, dk_ref, dv_ref, qa, da, kn, vn, qn, dn, ks, sums,
):
    q_blocks = q_ref.shape[0]
    k_blocks = k_ref.shape[0]
    key_count = k_blocks * BLOCK
    base = base_ref[0]
    scale = HEAD_DIM ** -0.5
    sums[...] = jnp.zeros_like(sums)

    @pl.loop(0, k_blocks)
    def _(i):
        at = pl.ds(pl.multiple_of(i * BLOCK, BLOCK), BLOCK)
        away = (membership(ends_ref, count, base - shift + i * BLOCK, BLOCK) - 1.0) * FAR
        ones = jnp.ones((16, BLOCK), jnp.float32)
        keys = k_ref[i].astype(jnp.float32)
        kn[at, :] = jnp.concatenate([keys, away, ones], axis=0).T.astype(jnp.bfloat16)
        vn[at, :] = jnp.concatenate([v_ref[i].astype(jnp.float32), ones], axis=0).T.astype(jnp.bfloat16)
        ks[:, at] = (keys * scale).astype(jnp.bfloat16)

    @pl.loop(0, q_blocks)
    def _(i):
        at = pl.ds(pl.multiple_of(i * BLOCK, BLOCK), BLOCK)
        inside = membership(ends_ref, count, base + i * BLOCK, BLOCK)
        pad = jnp.zeros((13, BLOCK), jnp.float32)
        scaled = q_ref[i].astype(jnp.float32) * scale
        qn[at, :] = scaled.T.astype(jnp.bfloat16)
        qa[:, at] = jnp.concatenate(
            [scaled, inside] + split3(-log_ref[:, at]) + [pad], axis=0
        ).astype(jnp.bfloat16)
        grads = do_ref[i].astype(jnp.float32)
        row_dot = jnp.sum(grads * o_ref[i].astype(jnp.float32), axis=0, keepdims=True)
        dn[at, :] = grads.T.astype(jnp.bfloat16)
        da[:, at] = jnp.concatenate([grads] + split3(-row_dot) + [pad], axis=0).astype(jnp.bfloat16)

    per = BLOCK // QB

    @pl.loop(0, q_blocks * per)
    def _(i):
        q_at = pl.ds(pl.multiple_of(i * QB, QB), QB)
        q_part = qa[:, q_at]
        d_part = da[:, q_at]
        q_rows = qn[q_at, :]
        d_rows = dn[q_at, :]
        first = base + i * QB
        low, high = image_span(ends_ref, count, first, first + QB - 1)
        low = jnp.maximum(low - base + shift, 0) // KB
        high = jnp.minimum(high - base + shift + KB - 1, key_count) // KB

        def step(j, dq):
            at = pl.ds(pl.multiple_of(j * KB, KB), KB)
            probs = jnp.exp(rows_dot(kn[at, :], q_part))
            score_grad = (probs * rows_dot(vn[at, :], d_part)).astype(jnp.bfloat16)
            sums[at, 0:HEAD_DIM] += rows_dot(score_grad, q_rows)
            sums[at, HEAD_DIM : 2 * HEAD_DIM] += rows_dot(probs.astype(jnp.bfloat16), d_rows)
            return dq + rows_dot(ks[:, at], score_grad)

        dq = lax.fori_loop(low, high, step, jnp.zeros((HEAD_DIM, QB), jnp.float32))
        dq_ref[i // per, :, pl.ds(pl.multiple_of((i % per) * QB, QB), QB)] = dq.astype(jnp.bfloat16)

    @pl.loop(0, k_blocks)
    def _(i):
        at = pl.ds(pl.multiple_of(i * BLOCK, BLOCK), BLOCK)
        both = sums[at, :].T
        dk_ref[i] = both[:HEAD_DIM].astype(dk_ref.dtype)
        dv_ref[i] = both[HEAD_DIM:].astype(dv_ref.dtype)


def vmem_spec():
    return pl.BlockSpec(memory_space=pltpu.VMEM)


def smem_spec():
    return pl.BlockSpec(memory_space=pltpu.SMEM)


def attention_forward(ends, base, q, k, v, shift):
    blocks, k_blocks = q.shape[0], k.shape[0]
    tokens, keys = blocks * BLOCK, k_blocks * BLOCK
    pairs = tokens * 2048
    return pl.pallas_call(
        partial(forward_kernel, ends.shape[0], shift),
        out_shape=(
            jax.ShapeDtypeStruct((blocks, HEAD_DIM, BLOCK), jnp.bfloat16),
            jax.ShapeDtypeStruct((1, tokens), jnp.float32),
        ),
        in_specs=[smem_spec(), smem_spec(), vmem_spec(), vmem_spec(), vmem_spec()],
        out_specs=(vmem_spec(), vmem_spec()),
        scratch_shapes=[
            pltpu.VMEM((HEAD_DIM + 16, tokens), jnp.bfloat16),
            pltpu.VMEM((keys, HEAD_DIM + 16), jnp.bfloat16),
            pltpu.VMEM((HEAD_DIM + 16, keys), jnp.bfloat16),
        ],
        compiler_params=pltpu.CompilerParams(vmem_limit_bytes=56 * 1024 * 1024),
        cost_estimate=pl.CostEstimate(flops=pairs * 4 * 64, bytes_accessed=tokens * 512, transcendentals=pairs),
    )(ends, base, q, k, v)


def attention_backward(ends, base, q, k, v, o, do, log, shift, kv_dtype):
    blocks, k_blocks = q.shape[0], k.shape[0]
    tokens, keys = blocks * BLOCK, k_blocks * BLOCK
    pairs = tokens * 2048
    return pl.pallas_call(
        partial(backward_kernel, ends.shape[0], shift),
        out_shape=(
            jax.ShapeDtypeStruct((blocks, HEAD_DIM, BLOCK), jnp.bfloat16),
            jax.ShapeDtypeStruct((k_blocks, HEAD_DIM, BLOCK), kv_dtype),
            jax.ShapeDtypeStruct((k_blocks, HEAD_DIM, BLOCK), kv_dtype),
        ),
        in_specs=[smem_spec(), smem_spec()] + [vmem_spec()] * 6,
        out_specs=(vmem_spec(), vmem_spec(), vmem_spec()),
        scratch_shapes=[
            pltpu.VMEM((HEAD_DIM + 32, tokens), jnp.bfloat16),
            pltpu.VMEM((HEAD_DIM + 16, tokens), jnp.bfloat16),
            pltpu.VMEM((keys, HEAD_DIM + 32), jnp.bfloat16),
            pltpu.VMEM((keys, HEAD_DIM + 16), jnp.bfloat16),
            pltpu.VMEM((tokens, HEAD_DIM), jnp.bfloat16),
            pltpu.VMEM((tokens, HEAD_DIM), jnp.bfloat16),
            pltpu.VMEM((HEAD_DIM, keys), jnp.bfloat16),
            pltpu.VMEM((keys, 2 * HEAD_DIM), jnp.float32),
        ],
        compiler_params=pltpu.CompilerParams(vmem_limit_bytes=56 * 1024 * 1024),
        cost_estimate=pl.CostEstimate(flops=pairs * 10 * 64, bytes_accessed=tokens * 1024, transcendentals=pairs),
    )(ends, base, q, k, v, o, do, log)


SEQ = ("z", "y", "c")
SWAP = ((0, 1), (1, 0))


def norm_forward(hidden, gain_vec, offset_vec):
    centre = hidden - jnp.mean(hidden, axis=-1, keepdims=True)
    spread = jnp.mean(centre * centre, axis=-1, keepdims=True)
    inv_std = lax.rsqrt(spread + NORM_EPS)
    scaled = centre * inv_std
    return (scaled * gain_vec + offset_vec, scaled, inv_std)


def norm_backward(grad_out, scaled, inv_std, gain_vec):
    gain_grad = jnp.sum(grad_out * scaled, axis=0)
    offset_grad = jnp.sum(grad_out, axis=0)
    grad_scaled = grad_out * gain_vec
    grad_in = inv_std * (
        grad_scaled
        - jnp.mean(grad_scaled, axis=-1, keepdims=True)
        - scaled * jnp.mean(grad_scaled * scaled, axis=-1, keepdims=True)
    )
    return (gain_grad, offset_grad, grad_in)


def dot(a, b, a_dim, b_dim):
    return lax.dot_general(
        a, b, (((a_dim,), (b_dim,)), ((), ())), preferred_element_type=jnp.float32
    )


def pick(x, i, axis=0):
    return lax.dynamic_index_in_dim(x, i, axis, keepdims=False)


def swap(x, axis):
    return lax.ppermute(x, axis, SWAP)


def in_order(own, other, position):
    return jnp.where(position == 0, jnp.stack([own, other]), jnp.stack([other, own]))


def join_fsdp(shard):
    if lax.axis_size("f") != 2:
        return lax.all_gather(shard, "f", axis=0, tiled=True)
    rows = shard.shape[0] // 2
    core = lax.axis_index("c")
    part = swap(lax.dynamic_slice_in_dim(shard, core * rows, rows, 0), "f")
    other = in_order(part, swap(part, "c"), core).reshape(shard.shape)
    return in_order(shard, other, lax.axis_index("f")).reshape((-1,) + shard.shape[1:])


def join_small(shard):
    if lax.axis_size("f") != 2:
        return lax.all_gather(shard, "f", axis=0, tiled=False)
    return in_order(shard, swap(shard, "f"), lax.axis_index("f"))


def halve(x, axis):
    here = lax.axis_index(axis)
    got = swap(pick(x, 1 - here), axis)
    return pick(x, here).astype(jnp.float32) + got.astype(jnp.float32)


def scatter_sum(x, axis):
    count, here = lax.axis_size(axis), lax.axis_index(axis)
    total = pick(x, here).astype(jnp.float32)
    for step in range(1, count):
        piece = pick(x, lax.rem(here + step, count))
        got = lax.ppermute(piece, axis, [(i, (i + step) % count) for i in range(count)])
        total = total + got.astype(jnp.float32)
    return total


def spread_parts(x, axis):
    count, here = lax.axis_size(axis), lax.axis_index(axis)
    out = jnp.zeros((count,) + x.shape, x.dtype)
    out = lax.dynamic_update_index_in_dim(out, x, here, 0)
    for step in range(1, count):
        got = lax.ppermute(x, axis, [(i, (i + step) % count) for i in range(count)])
        out = lax.dynamic_update_index_in_dim(out, got, lax.rem(here - step + count, count), 0)
    return out


def reduce_weight(grad, scale):
    parts, planes = lax.axis_size("f"), lax.axis_size("z")
    rows, cols = grad.shape
    low = jnp.bfloat16
    x = grad.reshape(parts, 2, -1, cols).transpose(1, 0, 2, 3).astype(low)
    x = halve(x, "c").astype(low)
    if parts == 2:
        x = halve(x, "f").astype(low)
    else:
        x = lax.psum_scatter(x, "f", scatter_dimension=0, tiled=False)
    x = x.reshape(2, -1, cols)
    x = halve(x, "y").astype(low)
    x = x.reshape(planes, -1, cols)
    x = scatter_sum(x, "z")
    if lax.axis_size("g") > 1:
        x = lax.psum(x, "g")
    x = (x * scale).astype(low)
    x = spread_parts(x, "z").reshape(-1, cols)
    x = in_order(x, swap(x, "y"), lax.axis_index("y")).reshape(-1, cols)
    x = in_order(x, swap(x, "c"), lax.axis_index("c")).reshape(-1, cols)
    return x.astype(jnp.float32)


def body(
    patches, pos_embed, lengths, out_grad,
    ln1_gain, ln1_bias, w_qkv, b_qv, w_out, b_out,
    ln2_gain, ln2_bias, w_fc1, b_fc1, w_fc2, b_fc2,
):
    f32, low = jnp.float32, jnp.bfloat16
    rows, width = patches.shape[1:]
    groups, parts = lax.axis_size("g"), lax.axis_size("f")
    head = lax.axis_index(SEQ)
    group = lax.axis_index("g")
    shard_index = lax.axis_index("f")
    scale = 1.0 / (parts * math.sqrt(rows * HEADS * groups))

    small = (ln1_gain, ln1_bias, b_qv, b_out, ln2_gain, ln2_bias, b_fc1, b_fc2)
    packed = join_small(jnp.concatenate(small))
    vectors, at = [], 0
    for vec in small:
        size = vec.shape[0]
        vectors.append(packed[:, at : at + size].reshape(-1).astype(f32))
        at += size
    gain_one, bias_one, qv_bias, out_bias, gain_two, bias_two, fc1_bias, fc2_bias = vectors

    shard_rows = w_qkv.shape[0]
    head_cols = lax.dynamic_slice_in_dim(
        w_qkv.reshape(shard_rows, 3, HEADS, HEAD_DIM), head, 1, 2
    ).reshape(shard_rows, 3 * HEAD_DIM)
    head_full = join_small(head_cols).reshape(width, 3 * HEAD_DIM)
    head_bias = jnp.concatenate(
        [
            lax.dynamic_slice_in_dim(qv_bias, head * HEAD_DIM, HEAD_DIM),
            jnp.zeros((HEAD_DIM,), f32),
            lax.dynamic_slice_in_dim(qv_bias, width + head * HEAD_DIM, HEAD_DIM),
        ]
    )

    hidden = patches[0].astype(f32) + pos_embed[0].astype(f32)
    normed_pre, scaled_one, inv_one = norm_forward(hidden, gain_one, bias_one)
    normed = normed_pre.astype(low)
    normed_all = lax.all_gather(normed, SEQ, axis=0, tiled=True)

    qkv_full = join_fsdp(w_qkv)
    out_full = join_fsdp(w_out)
    fc1_full = join_fsdp(w_fc1)
    fc2_full = join_fsdp(w_fc2)

    qkv = lax.dot_general(
        head_full, normed_all.reshape(HEADS, rows, width), (((0,), (2,)), ((), ())),
        preferred_element_type=f32,
    )
    qkv = (qkv + head_bias[:, None, None]).astype(low).transpose(1, 0, 2)
    q, k, v = (qkv[:, i * HEAD_DIM : (i + 1) * HEAD_DIM] for i in range(3))
    ends = jnp.cumsum(lengths[0]).astype(jnp.int32)
    base = (group * (rows * HEADS)).astype(jnp.int32).reshape(1)
    shift, margin = 0, 0
    up = [(i, i + 1) for i in range(groups - 1)]
    down = [(i + 1, i) for i in range(groups - 1)]
    if groups > 1:
        margin = -(-LONG // rows)
        shift = margin * rows
        both = jnp.stack([k, v])
        before = lax.ppermute(both[:, HEADS - margin :], "g", up)
        after = lax.ppermute(both[:, :margin], "g", down)
        k, v = jnp.concatenate([before, both, after], axis=1)
    attended, log_total = attention_forward(ends, base, q, k, v, shift)
    mixed = lax.all_to_all(attended, SEQ, 0, 0, tiled=True).reshape(width, rows)

    branch = dot(mixed, out_full, 0, 0) + out_bias
    middle = hidden + branch
    normed_two_pre, scaled_two, inv_two = norm_forward(middle, gain_two, bias_two)
    normed_two = normed_two_pre.astype(low)
    inner_sum = dot(normed_two, fc1_full, 1, 0) + fc1_bias
    active, gelu_pull = jax.vjp(partial(jax.nn.gelu, approximate=True), inner_sum)
    active_low = active.astype(low)
    block_out = middle + (dot(active_low, fc2_full, 1, 0) + fc2_bias)

    out_cot = out_grad[0]
    cot_full = out_cot.astype(f32)
    active_grad = dot(out_cot, fc2_full, 1, 1)
    inner_grad = gelu_pull(active_grad)[0].astype(low)
    norm_two_grad = dot(inner_grad, fc1_full, 1, 1)
    gain_two_grad, bias_two_grad, middle_from_norm = norm_backward(
        norm_two_grad, scaled_two, inv_two, gain_two
    )
    middle_grad = cot_full + middle_from_norm
    branch_grad = middle_grad.astype(low)
    mixed_grad = dot(out_full, branch_grad, 1, 1).astype(low)
    attended_grad = lax.all_to_all(
        mixed_grad.reshape(HEADS, HEAD_DIM, rows), SEQ, 0, 0, tiled=True
    )

    fc2_grad = reduce_weight(dot(active_low, out_cot, 0, 0), scale)
    fc1_grad = reduce_weight(dot(normed_two, inner_grad, 0, 0), scale)
    out_weight_grad = reduce_weight(dot(mixed, branch_grad, 1, 0), scale)

    dq, dk, dv = attention_backward(
        ends, base, q, k, v, attended, attended_grad, log_total, shift, f32 if groups > 1 else low
    )
    if groups > 1:
        both = jnp.stack([dk, dv])
        inner = both[:, margin : margin + HEADS]
        before = lax.ppermute(both[:, :margin], "g", down)
        after = lax.ppermute(both[:, margin + HEADS :], "g", up)
        inner = inner.at[:, HEADS - margin :].add(before).at[:, :margin].add(after)
        dk, dv = inner.astype(low)
    head_grad = jnp.concatenate([dq, dk, dv], axis=1)
    token_grad = lax.all_to_all(head_grad, SEQ, 0, 0, tiled=True)

    weight_part = lax.dot_general(
        normed_all.reshape(HEADS, rows, width), head_grad, (((0, 1), (0, 2)), ((), ())),
        preferred_element_type=f32,
    ).reshape(parts, shard_rows, 3 * HEAD_DIM)
    if parts == 2:
        weight_part = halve(weight_part, "f")
    else:
        weight_part = lax.psum_scatter(weight_part, "f", scatter_dimension=0, tiled=False)
    if groups > 1:
        weight_part = lax.psum(weight_part, "g")
    weight_all = lax.all_gather((weight_part * scale).astype(low), SEQ, axis=0, tiled=False)
    qkv_weight_grad = (
        weight_all.reshape(HEADS, shard_rows, 3, HEAD_DIM)
        .transpose(1, 2, 0, 3)
        .reshape(shard_rows, 3 * width)
        .astype(f32)
    )

    token_grad = (
        token_grad.reshape(HEADS, 3, HEAD_DIM, rows).transpose(1, 0, 2, 3).reshape(3 * width, rows)
    )
    token_sums = jnp.sum(token_grad.astype(f32), axis=1)
    norm_one_grad = dot(token_grad, qkv_full, 0, 1)
    gain_one_grad, bias_one_grad, hidden_from_norm = norm_backward(
        norm_one_grad, scaled_one, inv_one, gain_one
    )
    patch_grad = middle_grad + hidden_from_norm

    vectors = (
        gain_one_grad,
        bias_one_grad,
        jnp.concatenate([token_sums[:width], token_sums[2 * width :]]),
        jnp.sum(branch_grad.astype(f32), axis=0),
        gain_two_grad,
        bias_two_grad,
        jnp.sum(inner_grad.astype(f32), axis=0),
        jnp.sum(cot_full, axis=0),
    )
    total = lax.psum(
        jnp.concatenate([vec.reshape(parts, -1) for vec in vectors], axis=1) * scale,
        ("g",) + SEQ + ("f",),
    )
    total = pick(total, shard_index)
    sums, at = [], 0
    for vec in vectors:
        size = vec.shape[0] // parts
        sums.append(total[at : at + size])
        at += size
    return (
        block_out.astype(low)[None],
        patch_grad[None],
        sums[0],
        sums[1],
        qkv_weight_grad,
        sums[2],
        out_weight_grad,
        sums[3],
        sums[4],
        sums[5],
        fc1_grad,
        sums[6],
        fc2_grad,
        sums[7],
    )


def solution(mesh):
    seq, parts = mesh.shape["seq"], mesh.shape["fsdp"]
    fine = Mesh(mesh.devices.reshape(seq // HEADS, HEADS // 4, 2, 2, parts), ("g", "z", "y", "c", "f"))
    rows = P("f", ("g",) + SEQ, None)
    vec, mat = P("f"), P("f", None)
    in_specs = (rows, rows, mat, rows, vec, vec, mat, vec, mat, vec, vec, vec, mat, vec, mat, vec)
    out_specs = (rows, rows, vec, vec, mat, vec, mat, vec, vec, vec, mat, vec, mat, vec)
    return jax.shard_map(body, mesh=fine, in_specs=in_specs, out_specs=out_specs, check_vma=False)
```

time: 3000 us -> 876 us (0.29)
  waiting for transfers between devices: 1680 us -> 282 us
  matrix products: 684 us -> 89.5 us
  other arithmetic: 323 us -> 98.4 us
  Pallas kernels: 0 us -> 130 us
  blocking collectives: 106 us -> 60.6 us
    reduce_scatter x4 -> x0, waiting for transfers between devices: 605 us -> none  [the longest x1 222 us: body(): lax.psum_scatter(grad_list[2], 'fsdp', scatter_dimension=0, tiled=True)]
    dot_general x68 -> x12, matrix products: 684 us -> 89.5 us  [the longest x10 69.1 us: dot(): lax.dot_general(a, b, (((a_dim,), (b_dim,)), ((), ())), preferred_element...]
    ppermute x20 -> x44, waiting for transfers between devices: 666 us -> 274 us  [the longest x26 222 us: swap(): return lax.ppermute(x, axis, SWAP)]
    psum x1 -> x0, waiting for transfers between devices: 337 us -> none  [body(): lax.psum((grad_shards[0], grad_shards[1], grad_shards[2], grad_shards[3],...]
    pallas_call x0 -> x2, Pallas kernels: none -> 130 us  [the longest x1 78 us: attention_backward(): pl.pallas_call(partial(backward_kernel, ends.shape[0], shift), out_shape=...]
    convert_element_type x18 -> x15, other arithmetic: 142 us -> 34.5 us  [the longest x3 11.1 us: reduce_weight(): return x.astype(jnp.float32)]
    reduce_sum x12 -> x2, other arithmetic: 95 us -> 1.99 us  [the longest x1 1.51 us: body(): jnp.sum(branch_grad.astype(f32), axis=0)]
    all_gather x4 -> x2, waiting for transfers between devices: 67.5 us -> 0.01 us  [the longest x1 0.01 us: body(): normed_all = lax.all_gather(normed, SEQ, axis=0, tiled=True)]
  transfers between devices with their start and end apart: 29 -> 49, of which waited for: 15 -> 15; matrix products, arithmetic and copies ran while one was open for 16% -> 24% of each run, Pallas kernels for 0% -> 15%
where the time goes in v1:
time: 876 us; the launch traced here: 863 us
  waiting for transfers between devices  282 us (32%)
  Pallas kernels  130 us (15%)
  starting transfers between devices  103 us (12%)
  other arithmetic  98.4 us (11%)
  matrix products  89.5 us (10%)
  local copies, waits for them, and re-layouts  83.7 us (10%)
  blocking collectives  60.6 us (7%)
  between operations  15.4 us (2%)
    ppermute x26, waiting for transfers between devices, swap(): return lax.ppermute(x, axis, SWAP)  222 us
    pallas_call x1, Pallas kernels, attention_backward(): pl.pallas_call(partial(backward_kernel, ends.shape[0], shift), out_shape=...  78 us
    dot_general x10, matrix products, dot(): lax.dot_general(a, b, (((a_dim,), (b_dim,)), ((), ())), preferred_element...  69.1 us
    psum x1, blocking collectives, body(): lax.psum(jnp.concatenate([vec.reshape(parts, -1) for vec in vectors], axi...  60.6 us
    ppermute x9, starting transfers between devices, scatter_sum(): lax.ppermute(piece, axis, [(i, (i + step) % count) for i in range(count)])  55.4 us
    pallas_call x1, Pallas kernels, attention_forward(): pl.pallas_call(partial(forward_kernel, ends.shape[0], shift), out_shape=(...  52.4 us
    select_n x16, other arithmetic, in_order(): jnp.where(position == 0, jnp.stack([own, other]), jnp.stack([other, own]))  48.7 us
    ppermute x9, waiting for transfers between devices, scatter_sum(): lax.ppermute(piece, axis, [(i, (i + step) % count) for i in range(count)])  33.3 us
  transfers between devices with their start and end apart: 49, of which 15 were waited for; matrix products, arithmetic and copies ran while one was open for 24% of the time, Pallas kernels for 15%

profile of v1, /device:TPU:0, one launch (start us, length us, event | category | flops | bytes accessed | tf_op | source)
XLA Modules:
  0.0 863.3 jit_solution(9069227581501768313)
XLA Ops:
  34.0 75.9 %collective-permute-done.8 = bf16[256,3072]{1,0:T(8,128)(2,1)} collective-permute-done((bf16[256,3072]{1,0:T(8,128)(2,1)}, bf16[256,3072]{1,0:T(8,128)(2,1)}, u32[]{:S(2)}, u32[]{:S(2)}) %collective-permute-start.8) | collective-permute-done | bytes 1572896 | tf_op jit(solution)/shard_map/ppermute | solution.py:275
  119.1 46.9 %collective-permute-done.2 = bf16[256,1024]{1,0:T(8,128)(2,1)} collective-permute-done((bf16[256,1024]{1,0:T(8,128)(2,1)}, bf16[256,1024]{1,0:T(8,128)(2,1)}, u32[]{:S(2)}, u32[]{:S(2)}) %collective-permute-start.2) | collective-permute-done | bytes 524320 | tf_op jit(solution)/shard_map/ppermute | solution.py:275
  188.8 11.4 %fusion.26 = bf16[16,192,512]{2,1,0:T(8,128)(2,1)S(1)} fusion(f32[192]{0:T(256)S(1)} %copy-done.51, bf16[1024,192,1]{0,1,2:T(8,128)(2,1)S(1)} %copy-done.31, bf16[16,512,1024]{2,1,0:T(8,128)(2,1)} %bitcast.388), kind=kOutput, calls=%fused_computation.52 | convolution fusion | flops 3224371200 | bytes 20316928 | tf_op jit(solution)/shard_map/dot_general | solution.py:392
  202.0 52.4 %shard_map.263 = (bf16[16,64,512]{2,1,0:T(8,128)(2,1)}, f32[1,8192]{1,0:T(1,128)}) custom-call(s32[8]{0:T(128)} %bitcast.391, s32[1]{0:T(128)} %constant.205.clone.1.base_ref, bf16[16,64,512]{2,1,0:T(8,128)(2,1)} %get-tuple-element.70.q_ref, bf16[16,64,512]{2,1,0:T(8,128)(2,1)} %get-tuple-element.69.k_ref, bf16[16,64,512]{2,1,0:T(8,128)(2,1)} %get-tuple-element.68.v_ref), custom_call_target="tpu_custom_call" | custom-call | flops 4294967296 | bytes 4194304 | tf_op jit(solution)/shard_map/pallas_call | solution.py:194
  275.6 7.9 all-to-all-done
  287.9 9.8 %fusion.17 = (bf16[4096,512]{0,1:T(8,128)(2,1)}, f32[512,4096]{1,0:T(8,128)}) fusion(f32[4096]{0:T(1024)S(1)} %bitcast.372, bf16[1024,4096]{1,0:T(8,128)(2,1)S(1)} %bitcast.326, f32[512,1024]{1,0:T(8,128)S(1)} %get-tuple-element.98, f32[1024]{0:T(1024)S(1)} %bitcast.378, f32[1024]{0:T(1024)S(1)} %bitcast.367, f32[512]{0:T(512)S(1)} %add_rsqrt_fusion, ...), kind=kOutput, calls=%fused_computation.20 | convolution fusion | flops 4318560256 | bytes 23097344 | tf_op jit(solution)/shard_map/dot_general | solution.py:265
  297.7 13.3 %convert_reduce_fusion = (f32[4096]{0:T(1024)}, bf16[512,4096]{1,0:T(8,128)(2,1)S(1)}) fusion(f32[512,4096]{1,0:T(8,128)} %get-tuple-element.104, f32[4096]{0:T(1024)S(1)} %bitcast.373, bf16[4096,1024]{1,0:T(8,128)(2,1)S(1)} %bitcast.322, bf16[1,512,1024]{2,1,0:T(8,128)(2,1)S(1)} %copy-done.25), kind=kOutput, calls=%fused_computation.32 | convolution fusion | flops 4343197696 | bytes 22052864 | tf_op jit(solution)/shard_map/dot_general | solution.py:265
  319.6 7.2 convolution_convert_fusion
  331.7 9.6 %collective-permute-done.12 = bf16[256,1024]{1,0:T(8,128)(2,1)S(1)} collective-permute-done((bf16[256,1024]{1,0:T(8,128)(2,1)S(1)}, bf16[256,1024]{1,0:T(8,128)(2,1)S(1)}, u32[]{:S(2)}, u32[]{:S(2)}) %collective-permute-start.12) | collective-permute-done | bytes 524320 | tf_op jit(solution)/shard_map/ppermute | solution.py:275
  351.7 6.6 copy.48
  363.3 7.1 convolution_convert_fusion.1
  371.3 12.5 %collective-permute-done.15 = bf16[32,1024]{1,0:T(8,128)(2,1)S(1)} collective-permute-done((bf16[32,1024]{1,0:T(8,128)(2,1)S(1)}, bf16[32,1024]{1,0:T(8,128)(2,1)S(1)}, u32[]{:S(2)}, u32[]{:S(2)}) %collective-permute-start.15) | collective-permute-done | bytes 65568 | tf_op jit(solution)/shard_map/ppermute | solution.py:309
  395.9 78.0 %shard_map.264 = (bf16[16,64,512]{2,1,0:T(8,128)(2,1)}, bf16[16,64,512]{2,1,0:T(8,128)(2,1)}, bf16[16,64,512]{2,1,0:T(8,128)(2,1)}) custom-call(s32[8]{0:T(128)} %bitcast.392, s32[1]{0:T(128)} %constant.205.clone.1.base_ref, bf16[16,64,512]{2,1,0:T(8,128)(2,1)} %get-tuple-element.70.q_ref, bf16[16,64,512]{2,1,0:T(8,128)(2,1)} %get-tuple-element.69.k_ref, ...), custom_call_target="tpu_custom_call" | custom-call | flops 10737418240 | bytes 8388608 | tf_op jit(solution)/shard_map/pallas_call | solution.py:216
  483.2 9.0 %fusion.34 = f32[2,512,192]{1,2,0:T(8,128)S(1)} fusion(bf16[16,64,2,8,512]{4,3,2,1,0:T(8,128)(2,1)} %bitcast.389, bf16[16,192,512]{2,1,0:T(8,128)(2,1)S(1)} %constant_dynamic-update-slice_fusion), kind=kOutput, calls=%fused_computation.90 | convolution fusion | flops 3221225472 | bytes 20709376 | tf_op jit(solution)/shard_map/dot_general | solution.py:454
  502.0 29.9 %collective-permute-done.23 = bf16[256,4096]{1,0:T(8,128)(2,1)} collective-permute-done((bf16[256,4096]{1,0:T(8,128)(2,1)}, bf16[256,4096]{1,0:T(8,128)(2,1)}, u32[]{:S(2)}, u32[]{:S(2)}) %collective-permute-start.23) | collective-permute-done | bytes 2097184 | tf_op jit(solution)/shard_map/ppermute | solution.py:275
  536.1 10.0 %fusion.33 = bf16[1,512,1024]{2,1,0:T(8,128)(2,1)} fusion(f32[512,1024]{1,0:T(8,128)S(1)} %copy-done.15, bf16[4096,1024]{1,0:T(8,128)(2,1)S(1)} %bitcast.325, f32[512,4096]{1,0:T(8,128)} %get-tuple-element.104, f32[4096]{0:T(1024)S(1)} %bitcast.374, f32[1024]{0:T(1024)S(1)} %bitcast.377), kind=kOutput, calls=%fused_computation.89 | convolution fusion | flops 4317511680 | bytes 19943424 | tf_op jit(solution)/shard_map/dot_general | solution.py:265
  558.0 25.5 %collective-permute-done.34 = bf16[1024,1024]{1,0:T(8,128)(2,1)} collective-permute-done((bf16[1024,1024]{1,0:T(8,128)(2,1)}, bf16[1024,1024]{1,0:T(8,128)(2,1)}, u32[]{:S(2)}, u32[]{:S(2)}) %collective-permute-start.34) | collective-permute-done | bytes 2097184 | tf_op jit(solution)/shard_map/ppermute | solution.py:275
  593.5 34.2 %collective-permute-done.35 = bf16[512,1024]{1,0:T(8,128)(2,1)S(1)} collective-permute-done((bf16[512,1024]{1,0:T(8,128)(2,1)S(1)}, bf16[512,1024]{1,0:T(8,128)(2,1)S(1)}, u32[]{:S(2)}, u32[]{:S(2)}) %collective-permute-start.35) | collective-permute-done | bytes 1048608 | tf_op jit(solution)/shard_map/ppermute | solution.py:275
  634.4 39.8 %collective-permute-start.36 = (bf16[128,1024]{1,0:T(8,128)(2,1)S(1)}, bf16[128,1024]{1,0:T(8,128)(2,1)S(1)}, u32[]{:S(2)}, u32[]{:S(2)}) collective-permute-start(bf16[128,1024]{1,0:T(8,128)(2,1)S(1)} %get-tuple-element.71), channel_id=1, source_target_pairs={{0,8},{8,16},{16,24},{24,0},{1,9},{9,17},{17,25},{25,1},{2,10},{10... | collective-permute-start | bytes 786440 | tf_op jit(solution)/shard_map/ppermute | solution.py:309
  687.0 14.8 %collective-permute-done.37 = bf16[128,1024]{1,0:T(8,128)(2,1)S(1)} collective-permute-done((bf16[128,1024]{1,0:T(8,128)(2,1)S(1)}, bf16[128,1024]{1,0:T(8,128)(2,1)S(1)}, u32[]{:S(2)}, u32[]{:S(2)}) %collective-permute-start.37) | collective-permute-done | bytes 262176 | tf_op jit(solution)/shard_map/ppermute | solution.py:309
  707.4 10.2 %collective-permute-done.29 = bf16[32,4096]{1,0:T(8,128)(2,1)S(1)} collective-permute-done((bf16[32,4096]{1,0:T(8,128)(2,1)S(1)}, bf16[32,4096]{1,0:T(8,128)(2,1)S(1)}, u32[]{:S(2)}, u32[]{:S(2)}) %collective-permute-start.29) | collective-permute-done | bytes 262176 | tf_op jit(solution)/shard_map/ppermute | solution.py:319
  732.5 9.7 %multiply_reduce_fusion.1 = (f32[1024]{0:T(1024)S(1)}, f32[512]{0:T(512)S(1)}, f32[512]{0:T(512)S(1)}, f32[1024]{0:T(1024)S(1)}, f32[512,1024]{1,0:T(8,128)}) fusion(f32[512]{0:T(512)S(1)} %copy-done.38, f32[512]{0:T(512)S(1)} %copy-done.36, bf16[1,512,1024]{2,1,0:T(8,128)(2,1)} %param.17, bf16[1,512,1024]{2,1,0:T(8,128)(2,1)} %param.16, ...), kind=kOutput, calls=%fused_computation.72 | convolution fusion | flops 3227513856 | bytes 13651968 | tf_op jit(solution)/shard_map/dot_general | solution.py:265
  747.1 60.6 %psum.7 = f32[2,6144]{1,0:T(2,128)S(1)} all-reduce(f32[2,6144]{1,0:T(2,128)S(1)} %broadcast_multiply_fusion), channel_id=1, replica_groups=mesh['g'=1,'z'=4,'y'=2,'c'=2,'f'=2] {'g','z','y','c','f'}, use_global_device_ids=true, to_apply=%region_17.18 | all-reduce | flops 12288 | bytes 98304 | tf_op jit(solution)/shard_map/psum | solution.py:492
  831.3 6.6 copy.44
  (351 shorter events, 259.2 us)
Async XLA Ops:
  7.2 181.5 %all-gather.4.cloned.1.call-start = ((), (), s32[]{:S(2)}) async-start(), calls=%async_computation.3 | async-start | bytes 17825792 | tf_op jit(solution)/shard_map/all_gather | solution.py:385
  27.3 91.2 %collective-permute-start.4 = (bf16[256,4096]{1,0:T(8,128)(2,1)}, bf16[256,4096]{1,0:T(8,128)(2,1)}, u32[]{:S(2)}, u32[]{:S(2)}) collective-permute-start(bf16[256,4096]{1,0:T(8,128)(2,1)} %constant_dynamic-slice_fusion.3), channel_id=1, source_target_pairs={{0,1},{1,0},{2,3},{3,2},{4,5},{5,4},{6,7},{7,6},{8,9},{9,8},{10,11... | collective-permute-start | bytes 6291464 | tf_op jit(solution)/shard_map/ppermute | solution.py:275
  28.5 81.3 %collective-permute-start.8 = (bf16[256,3072]{1,0:T(8,128)(2,1)}, bf16[256,3072]{1,0:T(8,128)(2,1)}, u32[]{:S(2)}, u32[]{:S(2)}) collective-permute-start(bf16[256,3072]{1,0:T(8,128)(2,1)} %constant_dynamic-slice_fusion.1), channel_id=1, source_target_pairs={{0,1},{1,0},{2,3},{3,2},{4,5},{5,4},{6,7},{7,6},{8,9},{9,8},{10,11... | collective-permute-start | bytes 4718600 | tf_op jit(solution)/shard_map/ppermute | solution.py:275
  34.0 141.2 %collective-permute-start.6 = (bf16[1024,1024]{1,0:T(8,128)(2,1)}, bf16[1024,1024]{1,0:T(8,128)(2,1)}, u32[]{:S(2)}, u32[]{:S(2)}) collective-permute-start(bf16[1024,1024]{1,0:T(8,128)(2,1)} %constant_dynamic-slice_fusion.2), channel_id=1, source_target_pairs={{0,1},{1,0},{2,3},{3,2},{4,5},{5,4},{6,7},{7,6},{8,9},{9,8},{10,11... | collective-permute-start | bytes 6291464 | tf_op jit(solution)/shard_map/ppermute | solution.py:275
  109.9 65.8 %collective-permute-start.9 = (bf16[256,3072]{1,0:T(8,128)(2,1)}, bf16[256,3072]{1,0:T(8,128)(2,1)}, u32[]{:S(2)}, u32[]{:S(2)}) collective-permute-start(bf16[256,3072]{1,0:T(8,128)(2,1)} %collective-permute-done.8), channel_id=1, source_target_pairs={{0,2},{2,0},{1,3},{3,1},{4,6},{6,4},{5,7},{7,5},{8,10},{10,8},{9,1... | collective-permute-start | bytes 4718600 | tf_op jit(solution)/shard_map/ppermute | solution.py:275
  110.7 55.3 %collective-permute-start.2 = (bf16[256,1024]{1,0:T(8,128)(2,1)}, bf16[256,1024]{1,0:T(8,128)(2,1)}, u32[]{:S(2)}, u32[]{:S(2)}) collective-permute-start(bf16[256,1024]{1,0:T(8,128)(2,1)} %constant_dynamic-slice_fusion.4), channel_id=1, source_target_pairs={{0,1},{1,0},{2,3},{3,2},{4,5},{5,4},{6,7},{7,6},{8,9},{9,8},{10,11... | collective-permute-start | bytes 1572872 | tf_op jit(solution)/shard_map/ppermute | solution.py:275
  114.4 54.3 %collective-permute-start = (bf16[512,192]{0,1:T(8,128)(2,1)S(1)}, bf16[512,192]{0,1:T(8,128)(2,1)S(1)}, u32[]{:S(2)}, u32[]{:S(2)}) collective-permute-start(bf16[512,192]{0,1:T(8,128)(2,1)S(1)} %bitcast.360), channel_id=1, source_target_pairs={{0,1},{1,0},{2,3},{3,2},{4,5},{5,4},{6,7},{7,6},{8,9},{9,8},{10,11... | collective-permute-start | bytes 589832 | tf_op jit(solution)/shard_map/ppermute | solution.py:275
  118.4 64.1 %collective-permute-start.5 = (bf16[256,4096]{1,0:T(8,128)(2,1)}, bf16[256,4096]{1,0:T(8,128)(2,1)}, u32[]{:S(2)}, u32[]{:S(2)}) collective-permute-start(bf16[256,4096]{1,0:T(8,128)(2,1)} %collective-permute-done.4), channel_id=1, source_target_pairs={{0,2},{2,0},{1,3},{3,1},{4,6},{6,4},{5,7},{7,5},{8,10},{10,8},{9,1... | collective-permute-start | bytes 6291464 | tf_op jit(solution)/shard_map/ppermute | solution.py:275
  175.2 85.4 %collective-permute-start.7 = (bf16[1024,1024]{1,0:T(8,128)(2,1)}, bf16[1024,1024]{1,0:T(8,128)(2,1)}, u32[]{:S(2)}, u32[]{:S(2)}) collective-permute-start(bf16[1024,1024]{1,0:T(8,128)(2,1)} %collective-permute-done.6), channel_id=1, source_target_pairs={{0,2},{2,0},{1,3},{3,1},{4,6},{6,4},{5,7},{7,5},{8,10},{10,8},{9,1... | collective-permute-start | bytes 6291464 | tf_op jit(solution)/shard_map/ppermute | solution.py:275
  331.7 144.8 %collective-permute-start.22 = (bf16[2,256,4096]{2,1,0:T(8,128)(2,1)}, bf16[2,256,4096]{2,1,0:T(8,128)(2,1)}, u32[]{:S(2)}, u32[]{:S(2)}) collective-permute-start(bf16[2,256,4096]{2,1,0:T(8,128)(2,1)} %dynamic-slice_bitcast_fusion.1), channel_id=1, source_target_pairs={{0,2},{2,0},{1,3},{3,1},{4,6},{6,4},{5,7},{7,5},{8,10},{10,8},{9,1... | collective-permute-start | bytes 12582920 | tf_op jit(solution)/shard_map/ppermute | solution.py:275
  386.4 109.4 %collective-permute-start.33 = (bf16[2,1024,1024]{2,1,0:T(8,128)(2,1)}, bf16[2,1024,1024]{2,1,0:T(8,128)(2,1)}, u32[]{:S(2)}, u32[]{:S(2)}) collective-permute-start(bf16[2,1024,1024]{2,1,0:T(8,128)(2,1)} %dynamic-slice_bitcast_fusion), channel_id=1, source_target_pairs={{0,2},{2,0},{1,3},{3,1},{4,6},{6,4},{5,7},{7,5},{8,10},{10,8},{9,1... | collective-permute-start | bytes 12582920 | tf_op jit(solution)/shard_map/ppermute | solution.py:275
  393.4 101.5 %collective-permute-start.20 = (bf16[128,1024]{1,0:T(8,128)(2,1)S(1)}, bf16[128,1024]{1,0:T(8,128)(2,1)S(1)}, u32[]{:S(2)}, u32[]{:S(2)}) collective-permute-start(bf16[128,1024]{1,0:T(8,128)(2,1)S(1)} %bitcast.358), channel_id=1, source_target_pairs={{0,4},{4,0},{1,5},{5,1},{2,6},{6,2},{3,7},{7,3},{8,12},{12,8},{9,1... | collective-permute-start | bytes 786440 | tf_op jit(solution)/shard_map/ppermute | solution.py:275
  493.0 61.5 %collective-permute-start.10 = (f32[512,192]{0,1:T(8,128)}, f32[512,192]{0,1:T(8,128)S(1)}, u32[]{:S(2)}, u32[]{:S(2)}) collective-permute-start(f32[512,192]{0,1:T(8,128)} %dynamic-slice_bitcast_fusion.8), channel_id=1, source_target_pairs={{0,1},{1,0},{2,3},{3,2},{4,5},{5,4},{6,7},{7,6},{8,9},{9,8},{10,11... | collective-permute-start | bytes 1179656 | tf_op jit(solution)/shard_map/ppermute | solution.py:275
  495.8 60.5 %collective-permute-start.21 = (bf16[256,1024]{1,0:T(8,128)(2,1)}, bf16[256,1024]{1,0:T(8,128)(2,1)}, u32[]{:S(2)}, u32[]{:S(2)}) collective-permute-start(bf16[256,1024]{1,0:T(8,128)(2,1)} %bitcast.72), channel_id=1, source_target_pairs={{0,2},{2,0},{1,3},{3,1},{4,6},{6,4},{5,7},{7,5},{8,10},{10,8},{9,1... | collective-permute-start | bytes 1572872 | tf_op jit(solution)/shard_map/ppermute | solution.py:275
  501.9 81.7 %collective-permute-start.34 = (bf16[1024,1024]{1,0:T(8,128)(2,1)}, bf16[1024,1024]{1,0:T(8,128)(2,1)}, u32[]{:S(2)}, u32[]{:S(2)}) collective-permute-start(bf16[1024,1024]{1,0:T(8,128)(2,1)} %dynamic-slice_bitcast_fusion.2), channel_id=1, source_target_pairs={{0,1},{1,0},{2,3},{3,2},{4,5},{5,4},{6,7},{7,6},{8,9},{9,8},{10,11... | collective-permute-start | bytes 6291464 | tf_op jit(solution)/shard_map/ppermute | solution.py:275
  548.5 170.5 %all-to-all-start.2 = ((bf16[16,192,512]{2,1,0:T(8,128)(2,1)}), bf16[16,192,512]{2,1,0:T(8,128)(2,1)S(1)}, u32[]{:S(2)}, u32[]{:S(2)}) async-start(bf16[16,192,512]{2,1,0:T(8,128)(2,1)} %copy-done.20), calls=%async_computation.2 | async-start | bytes 6291456 | tf_op jit(solution)/shard_map/all_to_all | solution.py:452
  554.5 262.4 %all-gather.6.cloned.1.call-start = ((), (), s32[]{:S(2)}) async-start(), calls=%async_computation.4 | async-start | bytes 3342336 | tf_op jit(solution)/shard_map/all_gather | solution.py:464
  592.8 86.4 %collective-permute-start.26 = (bf16[32,4096]{1,0:T(8,128)(2,1)S(1)}, bf16[32,4096]{1,0:T(8,128)(2,1)S(1)}, u32[]{:S(2)}, u32[]{:S(2)}) collective-permute-start(bf16[32,4096]{1,0:T(8,128)(2,1)S(1)} %get-tuple-element.76), channel_id=1, source_target_pairs={{0,16},{8,24},{16,0},{24,8},{1,17},{9,25},{17,1},{25,9},{2,18},{10... | collective-permute-start | bytes 786440 | tf_op jit(solution)/shard_map/ppermute | solution.py:309
  592.8 86.4 %collective-permute-start.25 = (bf16[32,4096]{1,0:T(8,128)(2,1)S(1)}, bf16[32,4096]{1,0:T(8,128)(2,1)S(1)}, u32[]{:S(2)}, u32[]{:S(2)}) collective-permute-start(bf16[32,4096]{1,0:T(8,128)(2,1)S(1)} %get-tuple-element.74), channel_id=1, source_target_pairs={{0,8},{8,16},{16,24},{24,0},{1,9},{9,17},{17,25},{25,1},{2,10},{10... | collective-permute-start | bytes 786440 | tf_op jit(solution)/shard_map/ppermute | solution.py:309
  628.2 55.5 %collective-permute-start.38 = (bf16[128,1024]{1,0:T(8,128)(2,1)S(1)}, bf16[128,1024]{1,0:T(8,128)(2,1)S(1)}, u32[]{:S(2)}, u32[]{:S(2)}) collective-permute-start(bf16[128,1024]{1,0:T(8,128)(2,1)S(1)} %get-tuple-element.72), channel_id=1, source_target_pairs={{0,24},{8,0},{16,8},{24,16},{1,25},{9,1},{17,9},{25,17},{2,26},{10... | collective-permute-start | bytes 786440 | tf_op jit(solution)/shard_map/ppermute | solution.py:309
  630.2 71.6 %collective-permute-start.37 = (bf16[128,1024]{1,0:T(8,128)(2,1)S(1)}, bf16[128,1024]{1,0:T(8,128)(2,1)S(1)}, u32[]{:S(2)}, u32[]{:S(2)}) collective-permute-start(bf16[128,1024]{1,0:T(8,128)(2,1)S(1)} %get-tuple-element.73), channel_id=1, source_target_pairs={{0,16},{8,24},{16,0},{24,8},{1,17},{9,25},{17,1},{25,9},{2,18},{10... | collective-permute-start | bytes 786440 | tf_op jit(solution)/shard_map/ppermute | solution.py:309
  634.4 67.4 %collective-permute-start.36 = (bf16[128,1024]{1,0:T(8,128)(2,1)S(1)}, bf16[128,1024]{1,0:T(8,128)(2,1)S(1)}, u32[]{:S(2)}, u32[]{:S(2)}) collective-permute-start(bf16[128,1024]{1,0:T(8,128)(2,1)S(1)} %get-tuple-element.71), channel_id=1, source_target_pairs={{0,8},{8,16},{16,24},{24,0},{1,9},{9,17},{17,25},{25,1},{2,10},{10... | collective-permute-start | bytes 786440 | tf_op jit(solution)/shard_map/ppermute | solution.py:309
  742.2 67.6 %collective-permute-start.42 = (bf16[512,1024]{1,0:T(8,128)(2,1)S(1)}, bf16[512,1024]{1,0:T(8,128)(2,1)}, u32[]{:S(2)}, u32[]{:S(2)}) collective-permute-start(bf16[512,1024]{1,0:T(8,128)(2,1)S(1)} %bitcast.338), channel_id=1, source_target_pairs={{0,4},{4,0},{1,5},{5,1},{2,6},{6,2},{3,7},{7,3},{8,12},{12,8},{9,1... | collective-permute-start | bytes 3145736 | tf_op jit(solution)/shard_map/ppermute | solution.py:275
  747.1 90.7 %collective-permute-start.32 = (bf16[256,4096]{1,0:T(8,128)(2,1)}, bf16[256,4096]{1,0:T(8,128)(2,1)}, u32[]{:S(2)}, u32[]{:S(2)}) collective-permute-start(bf16[256,4096]{1,0:T(8,128)(2,1)} %bitcast.99), channel_id=1, source_target_pairs={{0,2},{2,0},{1,3},{3,1},{4,6},{6,4},{5,7},{7,5},{8,10},{10,8},{9,1... | collective-permute-start | bytes 6291464 | tf_op jit(solution)/shard_map/ppermute | solution.py:275
  (84 other events, 1626.8 us)
Sparse Core Ops, SparseCore 0:
  24.1 127.2 all-gather.3
  557.5 94.7 all-gather.5

commit v2 on v1

v2 whole, which is shorter than its diff:
```python
import math
from functools import partial

import jax
import jax.numpy as jnp
from jax import lax
from jax.experimental import pallas as pl
from jax.experimental.pallas import tpu as pltpu
from jax.sharding import Mesh, PartitionSpec as P

HEADS = 16
LONG = 2304
NORM_EPS = 1e-06
CHUNKS = 4
HEAD_DIM = 64
BLOCK = 512
FAR = 1e30
QB = 512
KB = 512
CALM_SCORE = 60.0
FORWARD_COST = 50_000_000_000
BACKWARD_COST = 75_000_000_000


def rows_dot(a, b):
    return lax.dot_general(a, b, (((1,), (0,)), ((), ())), preferred_element_type=jnp.float32)


def membership(ends_ref, count, first, width):
    place = first + lax.broadcasted_iota(jnp.int32, (16, width), 1)
    row = lax.broadcasted_iota(jnp.int32, (16, width), 0)
    low = jnp.zeros((16, width), jnp.int32)
    high = jnp.zeros((16, width), jnp.int32)
    for i in range(count):
        begin = ends_ref[i - 1] if i > 0 else 0
        low = jnp.where(row == i, begin, low)
        high = jnp.where(row == i, ends_ref[i], high)
    return jnp.where((place >= low) & (place < high), 1.0, 0.0)


def image_span(ends_ref, count, first, last):
    low = jnp.int32(0)
    high = ends_ref[count - 1]
    for i in range(count - 1):
        end = ends_ref[i]
        low = jnp.where(end <= first, end, low)
    for i in range(count - 2, -1, -1):
        end = ends_ref[i]
        high = jnp.where(end > last, end, high)
    return low, high


def split3(x):
    top = x.astype(jnp.bfloat16)
    rest = x - top.astype(jnp.float32)
    mid = rest.astype(jnp.bfloat16)
    low = (rest - mid.astype(jnp.float32)).astype(jnp.bfloat16)
    return [top.astype(jnp.float32), mid.astype(jnp.float32), low.astype(jnp.float32)]


def parts_of(ref):
    return [ref.at[:, i * HEAD_DIM : (i + 1) * HEAD_DIM, :] for i in range(ref.shape[1] // HEAD_DIM)]


def forward_kernel(count, shift, ends_ref, base_ref, own_ref, *refs):
    q_ref, k_ref, v_ref = parts_of(own_ref)
    if shift:
        k_ref, v_ref = parts_of(refs[0])
        refs = refs[1:]
    o_ref, log_ref, qa, kn, va, peak = refs
    peak[...] = jnp.zeros_like(peak)
    q_blocks = q_ref.shape[0]
    k_blocks = k_ref.shape[0]
    key_count = k_blocks * BLOCK
    base = base_ref[0]

    @pl.loop(0, k_blocks)
    def _(i):
        at = pl.ds(pl.multiple_of(i * BLOCK, BLOCK), BLOCK)
        away = (membership(ends_ref, count, base - shift + i * BLOCK, BLOCK) - 1.0) * FAR
        keys = k_ref[i].astype(jnp.float32)
        peak[1:2] = jnp.maximum(peak[1:2], jnp.sum(keys * keys, axis=0, keepdims=True))
        both = jnp.concatenate([keys, away], axis=0)
        kn[at, :] = both.T.astype(jnp.bfloat16)
        va[:, at] = jnp.concatenate(
            [v_ref[i].astype(jnp.float32), jnp.ones((16, BLOCK), jnp.float32)], axis=0
        ).astype(jnp.bfloat16)

    @pl.loop(0, q_blocks)
    def _(i):
        at = pl.ds(pl.multiple_of(i * BLOCK, BLOCK), BLOCK)
        inside = membership(ends_ref, count, base + i * BLOCK, BLOCK)
        asked = q_ref[i].astype(jnp.float32)
        peak[0:1] = jnp.maximum(peak[0:1], jnp.sum(asked * asked, axis=0, keepdims=True))
        qa[:, at] = jnp.concatenate(
            [asked * (HEAD_DIM ** -0.5), inside], axis=0
        ).astype(jnp.bfloat16)

    per = BLOCK // QB
    calm = CALM_SCORE * HEAD_DIM ** 0.5
    peaks = [jnp.max(peak[i : i + 1]) for i in range(2)]

    def span(i):
        first = base + i * QB
        low, high = image_span(ends_ref, count, first, first + QB - 1)
        low = jnp.maximum(low - base + shift, 0) // KB
        return low, jnp.minimum(high - base + shift + KB - 1, key_count) // KB

    def finish(i, top, acc):
        total = acc[HEAD_DIM : HEAD_DIM + 1]
        o_ref[i // per, :, pl.ds(pl.multiple_of((i % per) * QB, QB), QB)] = (
            acc[:HEAD_DIM] / total
        ).astype(jnp.bfloat16)
        log_ref[:, pl.ds(pl.multiple_of(i * QB, QB), QB)] = top + jnp.log(total)

    small = peaks[0] * peaks[1] <= calm * calm

    @pl.when(small)
    def _():
        @pl.loop(0, q_blocks * per)
        def _(i):
            q_part = qa[:, pl.ds(pl.multiple_of(i * QB, QB), QB)]

            def step(j, acc):
                at = pl.ds(pl.multiple_of(j * KB, KB), KB)
                weights = jnp.exp(rows_dot(kn[at, :], q_part)).astype(jnp.bfloat16)
                return acc + rows_dot(va[:, at], weights)

            acc = lax.fori_loop(*span(i), step, jnp.zeros((HEAD_DIM + 16, QB), jnp.float32))
            finish(i, 0.0, acc)

    @pl.when(jnp.logical_not(small))
    def _():
        @pl.loop(0, q_blocks * per)
        def _(i):
            q_part = qa[:, pl.ds(pl.multiple_of(i * QB, QB), QB)]

            def step(j, carry):
                top, acc = carry
                at = pl.ds(pl.multiple_of(j * KB, KB), KB)
                scores = rows_dot(kn[at, :], q_part)
                new_top = jnp.maximum(top, jnp.max(scores, axis=0, keepdims=True))
                weights = jnp.exp(scores - new_top).astype(jnp.bfloat16)
                acc = acc * jnp.exp(top - new_top) + rows_dot(va[:, at], weights)
                return new_top, acc

            start = (
                jnp.full((1, QB), -3e38, jnp.float32),
                jnp.zeros((HEAD_DIM + 16, QB), jnp.float32),
            )
            finish(i, *lax.fori_loop(*span(i), step, start))


def backward_kernel(count, shift, first_block, chunk, last, ends_ref, base_ref, own_ref, *refs):
    q_ref, k_ref, v_ref = parts_of(own_ref)
    if shift:
        k_ref, v_ref = parts_of(refs[0])
        refs = refs[1:]
    o_ref, do_ref, log_ref, *refs = refs
    if first_block > 0:
        sums_in, _, *refs = refs
    grad_ref, *refs = refs
    sums_out = None
    if shift:
        window_ref, *refs = refs
    if not last:
        sums_out, *refs = refs
    qa, da, kn, vn, qn, dn, ks, sums, dq_part, sums_sem, dq_sem, *refs = refs
    k_blocks = k_ref.shape[0]
    key_count = k_blocks * BLOCK
    base = base_ref[0]
    scale = HEAD_DIM ** -0.5
    start = base + first_block * BLOCK
    low, high = image_span(ends_ref, count, start, start + chunk * BLOCK - 1)
    low = jnp.maximum(low - base + shift, 0) // BLOCK
    high = jnp.minimum(high - base + shift + BLOCK - 1, key_count) // BLOCK
    held_low, held_high = (0, k_blocks) if last or first_block == 0 else (low, high)

    def block_at(i):
        return pl.ds(pl.multiple_of(i * BLOCK, BLOCK), BLOCK)

    if first_block > 0:

        @pl.loop(held_low, held_high)
        def _(i):
            pltpu.make_async_copy(sums_in.at[block_at(i)], sums.at[block_at(i)], sums_sem.at[i]).start()

    else:
        sums[...] = jnp.zeros_like(sums)

    @pl.loop(low, high)
    def _(i):
        at = block_at(i)
        away = (membership(ends_ref, count, base - shift + i * BLOCK, BLOCK) - 1.0) * FAR
        ones = jnp.ones((16, BLOCK), jnp.float32)
        keys = k_ref[i].astype(jnp.float32)
        kn[at, :] = jnp.concatenate([keys, away, ones], axis=0).T.astype(jnp.bfloat16)
        vn[at, :] = jnp.concatenate([v_ref[i].astype(jnp.float32), ones], axis=0).T.astype(jnp.bfloat16)
        ks[:, at] = (keys * scale).astype(jnp.bfloat16)

    @pl.loop(0, chunk)
    def _(i):
        at = block_at(i)
        block = first_block + i
        inside = membership(ends_ref, count, base + block * BLOCK, BLOCK)
        pad = jnp.zeros((13, BLOCK), jnp.float32)
        scaled = q_ref[block].astype(jnp.float32) * scale
        qn[at, :] = scaled.T.astype(jnp.bfloat16)
        qa[:, at] = jnp.concatenate(
            [scaled, inside] + split3(-log_ref[:, block_at(block)]) + [pad], axis=0
        ).astype(jnp.bfloat16)
        grads = do_ref[block].astype(jnp.float32)
        row_dot = jnp.sum(grads * o_ref[block].astype(jnp.float32), axis=0, keepdims=True)
        dn[at, :] = grads.T.astype(jnp.bfloat16)
        da[:, at] = jnp.concatenate([grads] + split3(-row_dot) + [pad], axis=0).astype(jnp.bfloat16)

    if first_block > 0:

        @pl.loop(held_low, held_high)
        def _(i):
            pltpu.make_async_copy(sums_in.at[block_at(i)], sums.at[block_at(i)], sums_sem.at[i]).wait()

    @pl.loop(0, chunk)
    def _(i):
        q_at = block_at(i)
        q_part = qa[:, q_at]
        d_part = da[:, q_at]
        q_rows = qn[q_at, :]
        d_rows = dn[q_at, :]
        first = start + i * BLOCK
        key_low, key_high = image_span(ends_ref, count, first, first + BLOCK - 1)
        key_low = jnp.maximum(key_low - base + shift, 0) // BLOCK
        key_high = jnp.minimum(key_high - base + shift + BLOCK - 1, key_count) // BLOCK

        def step(j, dq):
            at = block_at(j)
            probs = jnp.exp(rows_dot(kn[at, :], q_part))
            score_grad = (probs * rows_dot(vn[at, :], d_part)).astype(jnp.bfloat16)
            sums[at, 0:HEAD_DIM] += rows_dot(score_grad, q_rows)
            sums[at, HEAD_DIM : 2 * HEAD_DIM] += rows_dot(probs.astype(jnp.bfloat16), d_rows)
            return dq + rows_dot(ks[:, at], score_grad)

        dq = lax.fori_loop(key_low, key_high, step, jnp.zeros((HEAD_DIM, BLOCK), jnp.float32))
        dq_part[i] = dq.astype(jnp.bfloat16)

    def query_copy(i):
        return pltpu.make_async_copy(
            dq_part.at[i], grad_ref.at[first_block + i, 0:HEAD_DIM], dq_sem.at[i]
        )

    for i in range(chunk):
        query_copy(i).start()
    if not last:

        @pl.loop(held_low, held_high)
        def _(i):
            pltpu.make_async_copy(sums.at[block_at(i)], sums_out.at[block_at(i)], sums_sem.at[i]).start()

        @pl.loop(held_low, held_high)
        def _(i):
            pltpu.make_async_copy(sums.at[block_at(i)], sums_out.at[block_at(i)], sums_sem.at[i]).wait()

    elif shift:

        @pl.loop(0, k_blocks)
        def _(i):
            window_ref[i] = sums[block_at(i), :].T

    else:
        kv_part, kv_sem = refs

        def key_copy(i):
            return pltpu.make_async_copy(
                kv_part.at[i], grad_ref.at[i, HEAD_DIM : 3 * HEAD_DIM], kv_sem.at[i]
            )

        @pl.loop(0, k_blocks)
        def _(i):
            kv_part[i] = sums[block_at(i), :].T.astype(jnp.bfloat16)
            key_copy(i).start()

        @pl.loop(0, k_blocks)
        def _(i):
            key_copy(i).wait()

    for i in range(chunk):
        query_copy(i).wait()


def vmem_spec():
    return pl.BlockSpec(memory_space=pltpu.VMEM)


def smem_spec():
    return pl.BlockSpec(memory_space=pltpu.SMEM)


def attention_forward(ends, base, own, window, shift):
    blocks = own.shape[0]
    tokens, keys = blocks * BLOCK, blocks * BLOCK + 2 * shift
    arrays = [own] + ([window] if shift else [])
    return pl.pallas_call(
        partial(forward_kernel, ends.shape[0], shift),
        out_shape=(
            jax.ShapeDtypeStruct((blocks, HEAD_DIM, BLOCK), jnp.bfloat16),
            jax.ShapeDtypeStruct((1, tokens), jnp.float32),
        ),
        in_specs=[smem_spec(), smem_spec()] + [vmem_spec()] * len(arrays),
        out_specs=(vmem_spec(), vmem_spec()),
        scratch_shapes=[
            pltpu.VMEM((HEAD_DIM + 16, tokens), jnp.bfloat16),
            pltpu.VMEM((keys, HEAD_DIM + 16), jnp.bfloat16),
            pltpu.VMEM((HEAD_DIM + 16, keys), jnp.bfloat16),
            pltpu.VMEM((8, BLOCK), jnp.float32),
        ],
        compiler_params=pltpu.CompilerParams(vmem_limit_bytes=48 * 1024 * 1024),
        cost_estimate=pl.CostEstimate(
            flops=FORWARD_COST, bytes_accessed=tokens * 512, transcendentals=0
        ),
    )(ends, base, *arrays)


def attention_backward(ends, base, own, window, o, do, log, shift, first_block, chunk, carried):
    blocks = own.shape[0]
    tokens, keys = chunk * BLOCK, blocks * BLOCK + 2 * shift
    last = first_block + chunk == blocks
    low, f32 = jnp.bfloat16, jnp.float32
    arrays = [own] + ([window] if shift else []) + [o, do, log]
    in_specs = [smem_spec(), smem_spec()] + [vmem_spec()] * len(arrays)
    out_shape = [jax.ShapeDtypeStruct((blocks, HEAD_DIM if shift else 3 * HEAD_DIM, BLOCK), low)]
    out_specs = [any_spec()]
    aliases = {}
    if carried is not None:
        place_at = 2 + len(arrays)
        arrays += list(carried)
        in_specs += [any_spec(), any_spec()]
        aliases = {place_at + 1: 0}
        if not last:
            aliases[place_at] = 1
    if shift:
        out_shape.append(jax.ShapeDtypeStruct((keys // BLOCK, 2 * HEAD_DIM, BLOCK), f32))
        out_specs.append(vmem_spec())
    if not last:
        out_shape.append(jax.ShapeDtypeStruct((keys, 2 * HEAD_DIM), f32))
        out_specs.append(any_spec())
    scratch = [
        pltpu.VMEM((HEAD_DIM + 32, tokens), low),
        pltpu.VMEM((HEAD_DIM + 16, tokens), low),
        pltpu.VMEM((keys, HEAD_DIM + 32), low),
        pltpu.VMEM((keys, HEAD_DIM + 16), low),
        pltpu.VMEM((tokens, HEAD_DIM), low),
        pltpu.VMEM((tokens, HEAD_DIM), low),
        pltpu.VMEM((HEAD_DIM, keys), low),
        pltpu.VMEM((keys, 2 * HEAD_DIM), f32),
        pltpu.VMEM((chunk, HEAD_DIM, BLOCK), low),
        pltpu.SemaphoreType.DMA((keys // BLOCK,)),
        pltpu.SemaphoreType.DMA((chunk,)),
    ]
    if last and not shift:
        scratch += [
            pltpu.VMEM((blocks, 2 * HEAD_DIM, BLOCK), low),
            pltpu.SemaphoreType.DMA((blocks,)),
        ]
    return pl.pallas_call(
        partial(backward_kernel, ends.shape[0], shift, first_block, chunk, last),
        out_shape=out_shape,
        in_specs=in_specs,
        out_specs=out_specs,
        scratch_shapes=scratch,
        input_output_aliases=aliases,
        compiler_params=pltpu.CompilerParams(vmem_limit_bytes=50 * 1024 * 1024),
        cost_estimate=pl.CostEstimate(
            flops=BACKWARD_COST * chunk // blocks, bytes_accessed=tokens * 1024, transcendentals=0
        ),
    )(ends, base, *arrays)


def any_spec():
    return pl.BlockSpec(memory_space=pl.ANY)


def block_rows(rows, cols):
    while rows * cols > 512 * 1024 and rows % 16 == 0:
        rows //= 2
    return rows


def take_kernel(at_ref, in_ref, out_ref):
    out_ref[...] = in_ref[...]


def take(x, index, count):
    rows, cols = x.shape[0] // count, x.shape[1]
    size = block_rows(rows, cols)
    steps = rows // size
    return pl.pallas_call(
        take_kernel,
        out_shape=jax.ShapeDtypeStruct((rows, cols), x.dtype),
        grid_spec=pltpu.PrefetchScalarGridSpec(
            num_scalar_prefetch=1,
            grid=(steps,),
            in_specs=[pl.BlockSpec((size, cols), lambda j, at_ref: (at_ref[0] * steps + j, 0))],
            out_specs=pl.BlockSpec((size, cols), lambda j, at_ref: (j, 0)),
        ),
        cost_estimate=pl.CostEstimate(
            flops=0, bytes_accessed=2 * rows * cols * x.dtype.itemsize, transcendentals=0
        ),
    )(index.astype(jnp.int32).reshape(1), x)


def place_kernel(owner, row_ref, col_ref, *refs):
    out_ref = refs[-1]
    for i, piece in enumerate(owner):

        @pl.when(pl.program_id(0) == i)
        def _(piece=piece):
            out_ref[...] = refs[piece][...].astype(out_ref.dtype)


def place(pieces, row_at, col_at, dtype, rows, shape):
    cols = pieces[0].shape[1]
    owner = [n for n, piece in enumerate(pieces) for _ in range(piece.shape[0] // rows)]
    count = len(owner)
    size = block_rows(rows, cols)
    steps = rows // size

    def piece_map(piece):
        turns = [i for i in range(count) if owner[i] == piece]
        first, last = turns[0], turns[-1]

        def index(s, j, row_ref, col_ref):
            inside = j + (s - first) * steps
            end = (last - first + 1) * steps - 1
            return (jnp.where(s < first, 0, jnp.where(s > last, end, inside)), 0)

        return index

    return pl.pallas_call(
        partial(place_kernel, owner),
        out_shape=jax.ShapeDtypeStruct(shape, dtype),
        grid_spec=pltpu.PrefetchScalarGridSpec(
            num_scalar_prefetch=2,
            grid=(count, steps),
            in_specs=[pl.BlockSpec((size, cols), piece_map(i)) for i in range(len(pieces))],
            out_specs=pl.BlockSpec(
                (size, cols), lambda s, j, row_ref, col_ref: (row_ref[s] * steps + j, col_ref[s])
            ),
        ),
        cost_estimate=pl.CostEstimate(
            flops=0,
            bytes_accessed=count * rows * cols * (2 + jnp.dtype(dtype).itemsize),
            transcendentals=0,
        ),
    )(row_at, col_at, *pieces)


def project_kernel(count, place_ref, w_ref, bias_ref, *refs):
    blocks, out_ref, made, sem = refs[:count], refs[-3], refs[-2], refs[-1]

    def copy(i):
        return pltpu.make_async_copy(made.at[i], out_ref.at[place_ref[i]], sem.at[i])

    for i in range(count):
        part = lax.dot_general(
            w_ref[...], blocks[i][...], (((1,), (1,)), ((), ())), preferred_element_type=jnp.float32
        )
        made[i] = (part + bias_ref[...]).astype(jnp.bfloat16)
        copy(i).start()
    for i in range(count):
        copy(i).wait()


def project(so_far, places, w, bias, blocks):
    count = len(blocks)
    rows, width = blocks[0].shape
    cols = w.shape[0]
    arrays = [w, bias, *blocks] + ([] if so_far is None else [so_far])
    specs = [vmem_spec()] * (2 + count) + ([] if so_far is None else [any_spec()])
    return pl.pallas_call(
        partial(project_kernel, count),
        out_shape=jax.ShapeDtypeStruct((HEADS, cols, rows), jnp.bfloat16),
        in_specs=[smem_spec()] + specs,
        out_specs=any_spec(),
        scratch_shapes=[
            pltpu.VMEM((count, cols, rows), jnp.bfloat16),
            pltpu.SemaphoreType.DMA((count,)),
        ],
        input_output_aliases={} if so_far is None else {3 + count: 0},
        compiler_params=pltpu.CompilerParams(vmem_limit_bytes=24 * 1024 * 1024),
        cost_estimate=pl.CostEstimate(
            flops=4 * count * rows * width * cols, bytes_accessed=count * rows * width * 2, transcendentals=0
        ),
    )(jnp.stack(places).astype(jnp.int32), *arrays)


SLOTS = 4


def head_weight_kernel(count, place_ref, grad_ref, *refs):
    blocks, (out_ref, held, sem) = refs[:count], refs[count:]

    def copy(b):
        return pltpu.make_async_copy(blocks[b], held.at[b % SLOTS], sem.at[b % SLOTS])

    for b in range(SLOTS - 1):
        copy(b).start()
    out_ref[...] = jnp.zeros_like(out_ref)

    @pl.loop(0, count)
    def _(i):
        slot = lax.rem(i, SLOTS)
        pltpu.make_async_copy(blocks[0], held.at[slot], sem.at[slot]).wait()
        for b in range(SLOTS - 1, count):

            @pl.when(i + SLOTS - 1 == b)
            def _(b=b):
                copy(b).start()

        out_ref[...] += rows_dot(grad_ref[place_ref[i]], held[slot])


def head_weight(places, grad, blocks):
    count = len(blocks)
    rows, width = blocks[0].shape
    cols = grad.shape[1]
    return pl.pallas_call(
        partial(head_weight_kernel, count),
        out_shape=jax.ShapeDtypeStruct((cols, width), jnp.float32),
        in_specs=[smem_spec(), vmem_spec()] + [any_spec()] * count,
        out_specs=vmem_spec(),
        scratch_shapes=[
            pltpu.VMEM((SLOTS, rows, width), jnp.bfloat16),
            pltpu.SemaphoreType.DMA((SLOTS,)),
        ],
        compiler_params=pltpu.CompilerParams(vmem_limit_bytes=24 * 1024 * 1024),
        cost_estimate=pl.CostEstimate(
            flops=4 * count * rows * width * cols, bytes_accessed=count * rows * width * 2, transcendentals=0
        ),
    )(jnp.stack(places).astype(jnp.int32), grad, *blocks)


def place_of_head(head):
    return (head % 2) * (HEADS // 2) + (head // 2 % 2) * (HEADS // 4) + head // 4


def weave_kernel(heads_ref, out_ref):
    heads = heads_ref.shape[0]
    for part in range(3):
        for pair in range(heads // 2):
            rows = slice(part * HEAD_DIM, (part + 1) * HEAD_DIM)
            both = [heads_ref[place_of_head(2 * pair + i), rows] for i in range(2)]
            both = jnp.concatenate(both, axis=0)
            at = (part * heads + 2 * pair) * HEAD_DIM
            out_ref[:, at : at + 2 * HEAD_DIM] = both.astype(jnp.float32).T


def weave(heads):
    count, cols, rows = heads.shape
    size = 128
    return pl.pallas_call(
        weave_kernel,
        out_shape=jax.ShapeDtypeStruct((rows, count * cols), jnp.float32),
        grid=(rows // size,),
        in_specs=[pl.BlockSpec((count, cols, size), lambda i: (0, 0, i))],
        out_specs=pl.BlockSpec((size, count * cols), lambda i: (i, 0)),
        cost_estimate=pl.CostEstimate(
            flops=0, bytes_accessed=6 * count * cols * rows, transcendentals=0
        ),
    )(heads)


SEQ = ("z", "y", "c")
SWAP = ((0, 1), (1, 0))


def norm_forward(hidden, gain_vec, offset_vec):
    centre = hidden - jnp.mean(hidden, axis=-1, keepdims=True)
    spread = jnp.mean(centre * centre, axis=-1, keepdims=True)
    inv_std = lax.rsqrt(spread + NORM_EPS)
    scaled = centre * inv_std
    return (scaled * gain_vec + offset_vec, scaled, inv_std)


def norm_backward(grad_out, scaled, inv_std, gain_vec):
    gain_grad = jnp.sum(grad_out * scaled, axis=0)
    offset_grad = jnp.sum(grad_out, axis=0)
    grad_scaled = grad_out * gain_vec
    grad_in = inv_std * (
        grad_scaled
        - jnp.mean(grad_scaled, axis=-1, keepdims=True)
        - scaled * jnp.mean(grad_scaled * scaled, axis=-1, keepdims=True)
    )
    return (gain_grad, offset_grad, grad_in)


def dot(a, b, a_dim, b_dim):
    return lax.dot_general(
        a, b, (((a_dim,), (b_dim,)), ((), ())), preferred_element_type=jnp.float32
    )


def tie(x, *others):
    others = [other for other in others if other is not None]
    return lax.optimization_barrier((x, *others))[0] if others else x


def linear(start, first, a, second, b):
    start, first, second = (jnp.array(x, jnp.int32) for x in (start, first, second))
    return start + first * a + second * b


def pick(x, i, axis=0):
    return lax.dynamic_index_in_dim(x, i, axis, keepdims=False)


def swap(x, axis):
    return lax.ppermute(x, axis, SWAP)


def in_order(own, other, position):
    return jnp.where(position == 0, jnp.stack([own, other]), jnp.stack([other, own]))


def fetch_fsdp(shard, pieces, *others):
    if lax.axis_size("f") != 2:
        return [lax.all_gather(shard, "f", axis=0, tiled=True)]
    rows = shard.shape[0] // (2 * pieces)
    first = lax.axis_index("c") * pieces
    shard = tie(shard, *others)
    return [swap(take(shard, first + i, 2 * pieces), "f") for i in range(pieces)]


def share_cores(fetched, *others):
    if lax.axis_size("f") != 2:
        return fetched
    return fetched + [swap(tie(piece, *others), "c") for piece in fetched]


def join_fsdp(shard, pieces, *others):
    if lax.axis_size("f") != 2:
        return pieces[0]
    core, here = lax.axis_index("c"), lax.axis_index("f")
    count = len(pieces) // 2
    step = range(count)
    at = linear(
        (*range(2 * count), *(2 * count + i for i in step), *(3 * count + i for i in step)),
        (2 * count,) * (2 * count) + (-2 * count,) * (2 * count),
        here,
        (0,) * (2 * count) + (count,) * count + (-count,) * count,
        core,
    )
    rows, cols = shard.shape
    return place(
        [tie(shard, *others), *pieces], at, jnp.zeros_like(at), shard.dtype, rows // (2 * count), (2 * rows, cols)
    )


def join_small(shard):
    if lax.axis_size("f") != 2:
        return lax.all_gather(shard, "f", axis=0, tiled=False)
    return in_order(shard, swap(shard, "f"), lax.axis_index("f"))


def halve(x, axis, pairs=SWAP, here=None):
    here = lax.axis_index(axis) if here is None else here
    got = lax.ppermute(pick(x, 1 - here), axis, pairs)
    return pick(x, here).astype(jnp.float32) + got.astype(jnp.float32)


def plane_pairs(bit):
    return [(i, i ^ bit) for i in range(4)]


class WeightSum:
    def __init__(self, left, right, scale, left_dim=0):
        self.left, self.right, self.scale, self.left_dim = left, right, scale, left_dim
        self.size = left.shape[1 - left_dim] // lax.axis_size("f")
        self.cols = right.shape[1] // 2

    def term(self, c, f):
        left = lax.dynamic_slice_in_dim(self.left, f * self.size, self.size, 1 - self.left_dim)
        right = lax.dynamic_slice_in_dim(self.right, c * self.cols, self.cols, 1)
        return dot(left, right, self.left_dim, 0)

    def other_core(self, *others):
        low = jnp.bfloat16
        self.right = tie(self.right, *others)
        core = lax.axis_index("c")
        parts, here = lax.axis_size("f"), lax.axis_index("f")
        order = [1 - here, here] if parts == 2 else range(parts)
        sent = [self.term(1 - core, f).astype(low) for f in order]
        self.got = [swap(part, "c") for part in sent]
        return sent[-1]

    def other_f(self, *others):
        low, f32 = jnp.bfloat16, jnp.float32
        self.right = tie(self.right, *others)
        core, parts, here = lax.axis_index("c"), lax.axis_size("f"), lax.axis_index("f")
        if parts == 2:
            sent = (self.term(core, 1 - here) + self.got[0].astype(f32)).astype(low)
            self.far = swap(sent, "f")
            return sent
        total = [(self.term(core, f) + self.got[f].astype(f32)).astype(low) for f in range(parts)]
        self.total = lax.psum_scatter(jnp.stack(total), "f", scatter_dimension=0, tiled=False)
        return self.total

    def half(self, x, axis, pairs, here):
        x = x.reshape(2, -1, self.cols)
        sent = pick(x, 1 - here)
        self.kept, self.coming = pick(x, here), lax.ppermute(sent, axis, pairs)
        return sent

    def near_y(self, *others):
        low, f32 = jnp.bfloat16, jnp.float32
        core, parts, here = lax.axis_index("c"), lax.axis_size("f"), lax.axis_index("f")
        if parts == 2:
            self.right = tie(self.right, *others)
            x = self.term(core, here) + self.got[1].astype(f32) + self.far.astype(f32)
        else:
            x = self.total
        return self.half(x.astype(low), "y", SWAP, lax.axis_index("y"))

    def added(self, *others):
        coming = tie(self.coming, *others)
        return self.kept.astype(jnp.float32) + coming.astype(jnp.float32)

    def near_z(self, *others):
        x = self.added(*others).astype(jnp.bfloat16)
        return self.half(x, "z", plane_pairs(1), lax.rem(lax.axis_index("z"), 2))

    def far_z(self, *others):
        x = self.added(*others).astype(jnp.bfloat16)
        return self.half(x, "z", plane_pairs(2), lax.axis_index("z") // 2)

    def back_far_z(self, *others):
        x = self.added(*others)
        if lax.axis_size("g") > 1:
            x = lax.psum(x, "g")
        self.x = (x * self.scale).astype(jnp.bfloat16)
        self.coming = lax.ppermute(self.x, "z", plane_pairs(2))
        return self.x

    def back_near_z(self, *others):
        coming = tie(self.coming, *others)
        self.x = in_order(self.x, coming, lax.axis_index("z") // 2).reshape(-1, self.cols)
        self.coming = lax.ppermute(self.x, "z", plane_pairs(1))
        return self.x

    def back_y(self, *others):
        coming = tie(self.coming, *others)
        x = in_order(self.x, coming, lax.rem(lax.axis_index("z"), 2)).reshape(-1, self.cols)
        near = swap(x, "y")
        self.pieces = [x, near, swap(x, "c"), swap(near, "c")]
        return x

    def result(self, *others):
        y, c = lax.axis_index("y"), lax.axis_index("c")
        pieces = [tie(self.pieces[0], *others)] + self.pieces[1:]
        row_at = linear((0, 1, 0, 1), (1, -1, 1, -1), y, (0, 0, 0, 0), c)
        col_at = linear((0, 0, 1, 1), (0, 0, 0, 0), y, (1, 1, -1, -1), c)
        rows, cols = pieces[0].shape
        return place(pieces, row_at, col_at, jnp.float32, rows, (2 * rows, 2 * cols))


class VectorSum:
    def __init__(self, vectors, scale):
        self.sizes = [vec.shape[0] // lax.axis_size("f") for vec in vectors]
        self.x = jnp.concatenate([vec.reshape(lax.axis_size("f"), -1) for vec in vectors], axis=1) * scale

    def core(self, *others):
        self.x = tie(self.x, *others)
        self.coming = swap(self.x, "c")
        return self.x

    def other_f(self, *others):
        x = self.x + tie(self.coming, *others)
        if lax.axis_size("f") == 2:
            here = lax.axis_index("f")
            self.x, sent = pick(x, here), pick(x, 1 - here)
            self.coming = swap(sent, "f")
            return sent
        self.x = lax.psum_scatter(x, "f", scatter_dimension=0, tiled=False)
        self.coming = jnp.zeros_like(self.x)
        return self.x

    def hop(self, axis, pairs, others):
        self.x = self.x + tie(self.coming, *others)
        self.coming = lax.ppermute(self.x, axis, pairs)
        return self.x

    def near_y(self, *others):
        return self.hop("y", SWAP, others)

    def near_z(self, *others):
        return self.hop("z", plane_pairs(1), others)

    def far_z(self, *others):
        return self.hop("z", plane_pairs(2), others)

    def result(self, *others):
        self.total = self.x + tie(self.coming, *others)
        if lax.axis_size("g") > 1:
            self.total = lax.psum(self.total, "g")
        return self.total

    def vectors(self):
        at = 0
        for size in self.sizes:
            yield self.total[at : at + size]
            at += size


def arrivals(count):
    table = []
    for z in range(count):
        hops = []
        for t in range(1, count):
            if z - t >= 0:
                hops.append(("up", t))
            if z + t < count:
                hops.append(("down", t))
        table.append(hops)
    return table


def gather_group(x, use, beside):
    z, y, c = (lax.axis_index(axis) for axis in SEQ)
    count = lax.axis_size("z")
    table = arrivals(count)
    up, down = x, x
    hops = {}
    block, plane = x, z
    state, crossing = None, []
    for t in range(1, count + 1):
        first = plane * 4
        if t < count:
            up = lax.ppermute(up, "z", [(i, i + 1) for i in range(t - 1, count - 1)])
            down = lax.ppermute(down, "z", [(i, i - 1) for i in range(1, count - t + 1)])
        near = swap(block, "y")
        across = swap(block, "c")
        up, down, near, across, crossing, state, _ = lax.optimization_barrier(
            (up, down, near, across, crossing, state, beside[t - 1] if t <= len(beside) else [])
        )
        items = [(block, first + 2 * y + c), (across, first + 2 * y + 1 - c)]
        items += [(near, first + 2 * (1 - y) + c), *crossing]
        state = use(state, [item[0] for item in items], [item[1] for item in items])
        crossing = [(swap(near, "c"), first + 2 * (1 - y) + 1 - c)]
        if t < count:
            hops["up", t], hops["down", t] = up, down
            names = sorted({table[i][t - 1] for i in range(count)})
            block, plane = None, z
            for name in names:
                here = [i for i in range(count) if table[i][t - 1] == name]
                chosen = (z >= here[0]) & (z <= here[-1])
                block = hops[name] if block is None else jnp.where(chosen, hops[name], block)
                plane = jnp.where(chosen, z + (-name[1] if name[0] == "up" else name[1]), plane)
    return use(state, [item[0] for item in crossing], [item[1] for item in crossing])


def body(
    patches, pos_embed, lengths, out_grad,
    ln1_gain, ln1_bias, w_qkv, b_qv, w_out, b_out,
    ln2_gain, ln2_bias, w_fc1, b_fc1, w_fc2, b_fc2,
):
    f32, low = jnp.float32, jnp.bfloat16
    rows, width = patches.shape[1:]
    groups, parts = lax.axis_size("g"), lax.axis_size("f")
    head = lax.axis_index(SEQ)
    group = lax.axis_index("g")
    shard_index = lax.axis_index("f")
    scale = 1.0 / (parts * math.sqrt(rows * HEADS * groups))

    gain_one, bias_one, qv_bias = (
        join_small(vec).reshape(-1).astype(f32) for vec in (ln1_gain, ln1_bias, b_qv)
    )
    hidden = patches[0].astype(f32) + pos_embed[0].astype(f32)
    normed_pre, scaled_one, inv_one = norm_forward(hidden, gain_one, bias_one)
    normed = normed_pre.astype(low)

    shard_rows = w_qkv.shape[0]
    head_cols = lax.dynamic_slice_in_dim(
        w_qkv.reshape(shard_rows, 3, HEADS, HEAD_DIM), head, 1, 2
    ).reshape(shard_rows, 3 * HEAD_DIM)
    head_full = join_small(head_cols).reshape(width, 3 * HEAD_DIM).T
    head_bias = jnp.concatenate(
        [
            lax.dynamic_slice_in_dim(qv_bias, head * HEAD_DIM, HEAD_DIM),
            jnp.zeros((HEAD_DIM,), f32),
            lax.dynamic_slice_in_dim(qv_bias, width + head * HEAD_DIM, HEAD_DIM),
        ]
    )[:, None]

    kept_blocks, kept_places = [], []

    def add_blocks(qkv, blocks, places):
        kept_blocks.extend(blocks)
        kept_places.extend(places)
        return project(qkv, places, head_full, head_bias, blocks)

    out_part = fetch_fsdp(w_out, 1, normed)
    fc1_part = fetch_fsdp(w_fc1, 2, normed)
    fc2_part = fetch_fsdp(w_fc2, 2, normed)
    beside = [out_part, fc1_part[:1], fc1_part[1:], fc2_part[:1]]
    qkv = gather_group(normed, add_blocks, beside)
    out_part, fc1_part = share_cores(out_part), share_cores(fc1_part)
    ends = jnp.cumsum(lengths[0]).astype(jnp.int32)
    base = (group * (rows * HEADS)).astype(jnp.int32).reshape(1)
    shift, window = 0, None
    up = [(i, i + 1) for i in range(groups - 1)]
    down = [(i + 1, i) for i in range(groups - 1)]
    if groups > 1:
        margin = -(-LONG // rows)
        shift = margin * rows
        both = qkv[:, HEAD_DIM:]
        before = lax.ppermute(both[HEADS - margin :], "g", up)
        after = lax.ppermute(both[:margin], "g", down)
        window = jnp.concatenate([before, both, after], axis=0)
    attended, log_total = attention_forward(
        ends, base, qkv, window, shift
    )
    qkv_part = fetch_fsdp(w_qkv, 1, attended)
    fc2_part = share_cores(fc2_part, attended)
    out_full = join_fsdp(w_out, out_part, attended)
    fc1_full = join_fsdp(w_fc1, fc1_part, attended)
    fc2_full = join_fsdp(w_fc2, fc2_part, attended)
    small = (b_out, ln2_gain, ln2_bias, b_fc1, b_fc2)
    packed = join_small(tie(jnp.concatenate(small), normed))
    vectors, at = [], 0
    for vec in small:
        size = vec.shape[0]
        vectors.append(packed[:, at : at + size].reshape(-1).astype(f32))
        at += size
    out_bias, gain_two, bias_two, fc1_bias, fc2_bias = vectors
    mixed = lax.all_to_all(attended, SEQ, 0, 0, tiled=True).reshape(width, rows)

    branch = dot(mixed, out_full, 0, 0) + out_bias
    middle = hidden + tie(branch, fc2_full)
    normed_two_pre, scaled_two, inv_two = norm_forward(middle, gain_two, bias_two)
    normed_two = normed_two_pre.astype(low)
    inner_sum = dot(normed_two, fc1_full, 1, 0) + fc1_bias
    active, gelu_pull = jax.vjp(partial(jax.nn.gelu, approximate=True), inner_sum)
    active_low = active.astype(low)

    out_cot = out_grad[0]
    cot_full = out_cot.astype(f32)
    qkv_part = share_cores(qkv_part, active_low)
    fc2_sum = WeightSum(active_low, out_cot, scale)
    token = fc2_sum.other_core()
    block_out = middle + (dot(tie(active_low, token), fc2_full, 1, 0) + fc2_bias)
    token = fc2_sum.other_f(block_out)
    active_grad = dot(tie(out_cot, token), fc2_full, 1, 1)
    inner_grad = gelu_pull(active_grad)[0].astype(low)
    fc1_sum = WeightSum(normed_two, inner_grad, scale)
    norm_two_grad = dot(inner_grad, fc1_full, 1, 1)
    gain_two_grad, bias_two_grad, middle_from_norm = norm_backward(
        norm_two_grad, scaled_two, inv_two, gain_two
    )
    middle_grad = cot_full + middle_from_norm
    branch_grad = middle_grad.astype(low)
    out_sum = WeightSum(mixed, branch_grad, scale, 1)
    mixed_grad = dot(out_full, branch_grad, 1, 1).astype(low)
    attended_grad = lax.all_to_all(
        mixed_grad.reshape(HEADS, HEAD_DIM, rows), SEQ, 0, 0, tiled=True
    )
    early = VectorSum(
        (
            jnp.sum(branch_grad.astype(f32), axis=0),
            gain_two_grad,
            bias_two_grad,
            jnp.sum(inner_grad.astype(f32), axis=0),
            jnp.sum(cot_full, axis=0),
        ),
        scale,
    )
    token = fc1_sum.other_core(mixed_grad)
    early.core(mixed_grad)
    token = early.other_f(token)
    token = fc1_sum.other_f(token)
    token = out_sum.other_core(token)
    token = fc2_sum.near_y(token)
    tokens = [out_sum.other_f(token)]

    chunk = HEADS if groups > 1 else HEADS // CHUNKS
    plan = {
        0: [fc2_sum.near_z, early.near_y],
        1: [fc2_sum.far_z, fc1_sum.near_y, early.near_z],
        2: [fc2_sum.back_far_z, fc1_sum.near_z, out_sum.near_y, early.far_z],
        3: [fc2_sum.back_near_z, fc1_sum.far_z, out_sum.near_z, early.result],
    }
    carried = None
    for step in range(HEADS // chunk):
        results = attention_backward(
            ends, tie(base, *tokens), qkv, window, attended, attended_grad, log_total, shift,
            step * chunk, chunk, carried,
        )
        carried = results[::-1]
        tokens = [move(results[0]) for move in plan.pop(step)]
    for left in plan.values():
        for move in left:
            move(results[0])
    head_grad, *window_grad = results
    if groups > 1:
        both = window_grad[0]
        inner = both[margin : margin + HEADS]
        before = lax.ppermute(both[:margin], "g", down)
        after = lax.ppermute(both[margin + HEADS :], "g", up)
        inner = inner.at[HEADS - margin :].add(before).at[:margin].add(after)
        head_grad = jnp.concatenate([head_grad, inner.astype(low)], axis=1)
    token_grad = lax.all_to_all(head_grad, SEQ, 0, 0, tiled=True)

    weight_part = head_weight(kept_places, head_grad, kept_blocks)
    qkv_full = join_fsdp(w_qkv, qkv_part, weight_part)
    weight_part = weight_part.reshape(3 * HEAD_DIM, parts, shard_rows).transpose(1, 0, 2)
    if parts == 2:
        weight_part = halve(weight_part, "f")
    else:
        weight_part = lax.psum_scatter(weight_part, "f", scatter_dimension=0, tiled=False)
    if groups > 1:
        weight_part = lax.psum(weight_part, "g")

    weight_part = (weight_part * scale).astype(low)
    fc2_sum.back_y(weight_part)
    fc1_sum.back_far_z(weight_part)
    out_sum.far_z(weight_part)
    fc1_sum.back_near_z()
    out_sum.back_far_z()
    fc2_grad = fc2_sum.result()

    token_grad = (
        tie(token_grad, fc2_grad).reshape(HEADS, 3, HEAD_DIM, rows).transpose(1, 0, 2, 3).reshape(3 * width, rows)
    )
    norm_one_grad = dot(token_grad, qkv_full, 0, 1)
    gain_one_grad, bias_one_grad, hidden_from_norm = norm_backward(
        norm_one_grad, scaled_one, inv_one, gain_one
    )
    patch_grad = middle_grad + hidden_from_norm

    head_sums = jnp.sum(head_grad.astype(f32), axis=(0, 2))
    qv_grad = jnp.zeros((2 * width,), f32)
    qv_grad = lax.dynamic_update_slice(qv_grad, head_sums[:HEAD_DIM], (head * HEAD_DIM,))
    qv_grad = lax.dynamic_update_slice(
        qv_grad, head_sums[2 * HEAD_DIM :], (width + head * HEAD_DIM,)
    )
    late = VectorSum((gain_one_grad, bias_one_grad, qv_grad), scale)
    token = late.core()
    hops = [
        lax.ppermute(tie(weight_part, token), "z", [(i, (i + k) % 4) for i in range(4)]) for k in range(1, 4)
    ]
    token = late.other_f(token)
    fc1_sum.back_y(token)
    out_sum.back_near_z(token)
    plane = lax.axis_index("z")
    planes = jnp.zeros((4,) + weight_part.shape, low)
    for k, piece in enumerate([weight_part] + hops):
        planes = lax.dynamic_update_index_in_dim(planes, piece, lax.rem(plane + 4 - k, 4), 0)
    planes = in_order(planes, swap(planes, "y"), lax.axis_index("y"))
    late.near_y(planes)
    out_sum.back_y(planes)
    planes = in_order(planes, swap(planes, "c"), lax.axis_index("c"))
    late.near_z(planes)
    qkv_weight_grad = weave(planes.reshape((HEADS,) + weight_part.shape))
    late.far_z(qkv_weight_grad)
    fc1_grad, out_weight_grad = fc1_sum.result(), out_sum.result()
    late.result(fc1_grad)
    ln1_gain_sum, ln1_bias_sum, qv_sum = late.vectors()
    out_bias_sum, ln2_gain_sum, ln2_bias_sum, fc1_bias_sum, fc2_bias_sum = early.vectors()
    return (
        block_out.astype(low)[None],
        patch_grad[None],
        ln1_gain_sum,
        ln1_bias_sum,
        qkv_weight_grad,
        qv_sum,
        out_weight_grad,
        out_bias_sum,
        ln2_gain_sum,
        ln2_bias_sum,
        fc1_grad,
        fc1_bias_sum,
        fc2_grad,
        fc2_bias_sum,
    )


def solution(mesh):
    seq, parts = mesh.shape["seq"], mesh.shape["fsdp"]
    fine = Mesh(mesh.devices.reshape(seq // HEADS, HEADS // 4, 2, 2, parts), ("g", "z", "y", "c", "f"))
    rows = P("f", ("g",) + SEQ, None)
    vec, mat = P("f"), P("f", None)
    in_specs = (rows, rows, mat, rows, vec, vec, mat, vec, mat, vec, vec, vec, mat, vec, mat, vec)
    out_specs = (rows, rows, vec, vec, mat, vec, mat, vec, vec, vec, mat, vec, mat, vec)
    return jax.shard_map(body, mesh=fine, in_specs=in_specs, out_specs=out_specs, check_vma=False)
```

time: 876 us -> 741 us (0.85)
  Pallas kernels: 130 us -> 216 us
  blocking collectives: 60.6 us -> 0 us
  other arithmetic: 98.4 us -> 51.4 us
  waiting for transfers between devices: 282 us -> 235 us
  local copies, waits for them, and re-layouts: 83.7 us -> 44.3 us
  between operations: 15.4 us -> 2.69 us
    ppermute x26 -> x53, waiting for transfers between devices: 222 us -> 71.7 us  [swap(): return lax.ppermute(x, axis, SWAP)]
    ppermute x18 -> x31, waiting for transfers between devices: 51.9 us -> 158 us  [the longest x3 62.9 us: back_far_z(): self.coming = lax.ppermute(self.x, 'z', plane_pairs(2))]
    pallas_call x1 -> x24, Pallas kernels: 78 us -> 181 us  [the longest x4 84.8 us: attention_backward(): pl.pallas_call(partial(backward_kernel, ends.shape[0], shift, first_block...]
    psum x1 -> x0, blocking collectives: 60.6 us -> none  [body(): lax.psum(jnp.concatenate([vec.reshape(parts, -1) for vec in vectors], axi...]
    select_n x16 -> x10, other arithmetic: 48.7 us -> 14.3 us  [in_order(): jnp.where(position == 0, jnp.stack([own, other]), jnp.stack([other, own]))]
    convert_element_type x14 -> x13, other arithmetic: 33 us -> 12.5 us  [the longest x3 7.94 us: near_y(): return self.half(x.astype(low), 'y', SWAP, lax.axis_index('y'))]
    dot_general x2 -> x0, matrix products: 20.4 us -> none  [the longest x1 11.4 us: body(): lax.dot_general(head_full, normed_all.reshape(HEADS, rows, width), (((0,)...]
    ppermute x18 -> x31, starting transfers between devices: 67.4 us -> 50.1 us  [the longest x9 15.7 us: half(): self.kept, self.coming = (pick(x, here), lax.ppermute(sent, axis, pairs))]
  transfers between devices with their start and end apart: 49 -> 87, of which waited for: 15 -> 26; matrix products, arithmetic and copies ran while one was open for 24% -> 17% of each run, Pallas kernels for 15% -> 26%
where the time goes in v2:
time: 741 us; the launch traced here: 730 us
  waiting for transfers between devices  235 us (32%)
  Pallas kernels  216 us (29%)
  starting transfers between devices  98.6 us (13%)
  matrix products  81.6 us (11%)
  other arithmetic  51.4 us (7%)
  local copies, waits for them, and re-layouts  44.3 us (6%)
    pallas_call x4, Pallas kernels, attention_backward(): pl.pallas_call(partial(backward_kernel, ends.shape[0], shift, first_block...  84.8 us
    dot_general x19, matrix products, dot(): lax.dot_general(a, b, (((a_dim,), (b_dim,)), ((), ())), preferred_element...  81.6 us
    ppermute x53, waiting for transfers between devices, swap(): return lax.ppermute(x, axis, SWAP)  71.7 us
    ppermute x3, waiting for transfers between devices, back_far_z(): self.coming = lax.ppermute(self.x, 'z', plane_pairs(2))  62.9 us
    pallas_call x7, Pallas kernels, place(): pl.pallas_call(partial(place_kernel, owner), out_shape=jax.ShapeDtypeStru...  47.9 us
    pallas_call x1, Pallas kernels, attention_forward(): pl.pallas_call(partial(forward_kernel, ends.shape[0], shift), out_shape=(...  35.3 us
    ppermute x53, starting transfers between devices, swap(): return lax.ppermute(x, axis, SWAP)  32.3 us
    ppermute x3, waiting for transfers between devices, gather_group(): lax.ppermute(down, 'z', [(i, i - 1) for i in range(1, count - t + 1)])  27 us
  transfers between devices with their start and end apart: 87, of which 26 were waited for; matrix products, arithmetic and copies ran while one was open for 17% of the time, Pallas kernels for 26%

profile of v2, /device:TPU:0, one launch (start us, length us, event | category | flops | bytes accessed | tf_op | source)
XLA Modules:
  0.0 729.5 jit_solution(10499886418265811208)
XLA Ops:
  20.4 11.6 %collective-permute-done.8.refs_1_ = bf16[256,1024]{1,0:T(8,128)(2,1)} collective-permute-done((bf16[256,1024]{1,0:T(8,128)(2,1)}, bf16[256,1024]{1,0:T(8,128)(2,1)}, u32[]{:S(2)}, u32[]{:S(2)}) %collective-permute-start.8) | collective-permute-done | bytes 524320 | tf_op jit(solution)/shard_map/ppermute | solution.py:617
  50.0 11.3 %collective-permute-done.1 = bf16[1024]{0:T(1024)(128)(2,1)S(1)} collective-permute-done((bf16[1024]{0:T(1024)(128)(2,1)S(1)}, bf16[1024]{0:T(1024)(128)(2,1)S(1)}, u32[]{:S(2)}, u32[]{:S(2)}) %collective-permute-start.1) | collective-permute-done | bytes 2080 | tf_op jit(solution)/shard_map/ppermute | solution.py:617
  75.4 13.0 %collective-permute-done.10 = bf16[512,1024]{1,0:T(8,128)(2,1)} collective-permute-done((bf16[512,1024]{1,0:T(8,128)(2,1)}, bf16[512,1024]{1,0:T(8,128)(2,1)}, u32[]{:S(2)}, u32[]{:S(2)}) %collective-permute-start.10) | collective-permute-done | bytes 1048608 | tf_op jit(solution)/shard_map/ppermute | solution.py:838
  103.3 11.2 %collective-permute-done.17.refs_2_.refs_9_ = bf16[512,1024]{1,0:T(8,128)(2,1)} collective-permute-done((bf16[512,1024]{1,0:T(8,128)(2,1)}, bf16[512,1024]{1,0:T(8,128)(2,1)}, u32[]{:S(2)}, u32[]{:S(2)}) %collective-permute-start.17) | collective-permute-done | bytes 1048608 | tf_op jit(solution)/shard_map/ppermute | solution.py:617
  115.3 8.8 %collective-permute-done.16 = bf16[512,1024]{1,0:T(8,128)(2,1)} collective-permute-done((bf16[512,1024]{1,0:T(8,128)(2,1)}, bf16[512,1024]{1,0:T(8,128)(2,1)}, u32[]{:S(2)}, u32[]{:S(2)}) %collective-permute-start.16) | collective-permute-done | bytes 1048608 | tf_op jit(solution)/shard_map/ppermute | solution.py:838
  137.2 14.6 %collective-permute-done.21.refs_2_.refs_13_ = bf16[512,1024]{1,0:T(8,128)(2,1)} collective-permute-done((bf16[512,1024]{1,0:T(8,128)(2,1)}, bf16[512,1024]{1,0:T(8,128)(2,1)}, u32[]{:S(2)}, u32[]{:S(2)}) %collective-permute-start.21) | collective-permute-done | bytes 1048608 | tf_op jit(solution)/shard_map/ppermute | solution.py:617
  163.3 35.3 %shard_map.542 = (bf16[16,64,512]{2,1,0:T(8,128)(2,1)S(1)}, f32[1,8192]{1,0:T(1,128)S(1)}) custom-call(s32[8]{0:T(128)S(1)} %bitcast.212, s32[1]{0:T(128)} %constant.206.clone.1.base_ref, bf16[16,192,512]{2,1,0:T(8,128)(2,1)S(1)} %shard_map.541.own_ref), custom_call_target="tpu_custom_call" | custom-call | flops 49999998976 | bytes 4194304 | tf_op jit(solution)/shard_map/pallas_call | solution.py:302
  222.7 8.9 %shard_map.546 = bf16[1024,4096]{1,0:T(8,128)(2,1)} custom-call(s32[8]{0:T(128)} %multiply_add_fusion.2.row_ref, s32[8]{0:T(128)} %broadcast_13_col_ref.2.col_ref, bf16[512,4096]{1,0:T(8,128)(2,1)} %refs_0_.2, bf16[128,4096]{1,0:T(8,128)(2,1)} %copy-done.44, bf16[128,4096]{1,0:T(8,128)(2,1)} %collective-permute-done.20.refs_2_, ...), custom_call_target="tpu_custom_call" | custom-call | bytes 16777216 | tf_op jit(solution)/shard_map/pallas_call | solution.py:438
  231.6 9.0 %shard_map.545 = bf16[4096,1024]{1,0:T(8,128)(2,1)} custom-call(s32[8]{0:T(128)} %multiply_add_fusion.2.row_ref, s32[8]{0:T(128)} %broadcast_13_col_ref.2.col_ref, bf16[2048,1024]{1,0:T(8,128)(2,1)} %refs_0_.1, bf16[512,1024]{1,0:T(8,128)(2,1)} %collective-permute-done.24.refs_1_, bf16[512,1024]{1,0:T(8,128)(2,1)} %collective-permute-done.28.refs_2_, ...), custom_call_target="tpu_custom_call" | custom-call | bytes 16777216 | tf_op jit(solution)/shard_map/pallas_call | solution.py:438
  248.5 8.7 %multiply_convert_fusion = (bf16[512,4096]{1,0:T(8,128)(2,1)S(1)}, f32[512,4096]{1,0:T(8,128)}) fusion(f32[4096]{0:T(1024)S(1)} %bitcast.281, bf16[512,1024]{1,0:T(8,128)(2,1)S(1)} %add_convert_fusion.4, bf16[1024,4096]{1,0:T(8,128)(2,1)S(1)} %copy-done.34), kind=kOutput, calls=%fused_computation.10 | convolution fusion | flops 4315938816 | bytes 22036480 | tf_op jit(solution)/shard_map/dot_general | solution.py:597
  264.9 9.0 %add_add_fusion = bf16[512,1024]{1,0:T(8,128)(2,1)} fusion(f32[512,1024]{1,0:T(8,128)S(1)} %get-tuple-element.196, bf16[512,4096]{1,0:T(8,128)(2,1)S(1)} %copy-done.51, bf16[4096,1024]{1,0:T(8,128)(2,1)} %shard_map.545, f32[1024]{0:T(1024)S(1)} %bitcast.286), kind=kOutput, calls=%fused_computation.39 | convolution fusion | flops 4296540160 | bytes 15732736 | tf_op jit(solution)/shard_map/dot_general | solution.py:597
  278.4 13.6 %convert_reduce_fusion = (f32[4096]{0:T(1024)S(1)}, bf16[512,4096]{1,0:T(8,128)(2,1)S(1)}) fusion(f32[512,4096]{1,0:T(8,128)} %get-tuple-element.217, f32[4096]{0:T(1024)S(1)} %bitcast.282, bf16[512,1024]{1,0:T(8,128)(2,1)S(1)} %bitcast.241, bf16[4096,1024]{1,0:T(8,128)(2,1)} %shard_map.545), kind=kOutput, calls=%fused_computation.9 | convolution fusion | flops 4343197696 | bytes 22052864 | tf_op jit(solution)/shard_map/dot_general | solution.py:597
  340.2 18.1 %shard_map.547 = (bf16[16,192,512]{2,1,0:T(8,128)(2,1)}, f32[8192,128]{1,0:T(8,128)}) custom-call(s32[8]{0:T(128)S(1)} %bitcast.213, s32[1]{0:T(128)} %constant.206.clone.1.base_ref, bf16[16,192,512]{2,1,0:T(8,128)(2,1)} %copy-done, bf16[16,64,512]{2,1,0:T(8,128)(2,1)S(1)} %copy-done.10, bf16[16,64,512]{2,1,0:T(8,128)(2,1)S(1)} %all-to-all-done.1.refs_1_, ...), custom_call_target="tpu_custom_call" | custom-call | flops 18749999104 | bytes 2097152 | tf_op jit(solution)/shard_map/pallas_call | solution.py:364
  366.0 23.9 %shard_map.548 = (bf16[16,192,512]{2,1,0:T(8,128)(2,1)}, f32[8192,128]{1,0:T(8,128)}) custom-call(s32[8]{0:T(128)S(1)} %bitcast.214, s32[1]{0:T(128)} %constant.206.clone.1.base_ref, bf16[16,192,512]{2,1,0:T(8,128)(2,1)} %copy-done, bf16[16,64,512]{2,1,0:T(8,128)(2,1)S(1)} %copy-done.10, ...), custom_call_target="tpu_custom_call", output_to_operand_aliasing={{0}: (7, {}), {1}: (6, {})} | custom-call | flops 18749999104 | bytes 2097152 | tf_op jit(solution)/shard_map/pallas_call | solution.py:364
  402.8 19.3 %shard_map.549 = (bf16[16,192,512]{2,1,0:T(8,128)(2,1)}, f32[8192,128]{1,0:T(8,128)}) custom-call(s32[8]{0:T(128)S(1)} %bitcast.215, s32[1]{0:T(128)} %constant.206.clone.1.base_ref, bf16[16,192,512]{2,1,0:T(8,128)(2,1)} %copy-done, bf16[16,64,512]{2,1,0:T(8,128)(2,1)S(1)} %copy-done.10, ...), custom_call_target="tpu_custom_call", output_to_operand_aliasing={{0}: (7, {}), {1}: (6, {})} | custom-call | flops 18749999104 | bytes 2097152 | tf_op jit(solution)/shard_map/pallas_call | solution.py:364
  427.9 23.5 %shard_map.550.grad_ref = bf16[16,192,512]{2,1,0:T(8,128)(2,1)} custom-call(s32[8]{0:T(128)S(1)} %bitcast.216, s32[1]{0:T(128)} %constant.206.clone.1.base_ref, bf16[16,192,512]{2,1,0:T(8,128)(2,1)} %copy-done, bf16[16,64,512]{2,1,0:T(8,128)(2,1)S(1)} %copy-done.10, bf16[16,64,512]{2,1,0:T(8,128)(2,1)S(1)} %all-to-all-done.1.refs_1_, ...), custom_call_target="tpu_custom_call", output_to_operand_aliasing={{}: (7, {})} | custom-call | flops 18749999104 | bytes 2097152 | tf_op jit(solution)/shard_map/pallas_call | solution.py:364
  463.7 8.2 %shard_map.551 = f32[192,1024]{1,0:T(8,128)S(1)} custom-call(s32[16]{0:T(128)S(1)} %stack.294.place_ref, bf16[16,192,512]{2,1,0:T(8,128)(2,1)S(1)} %copy-done.1, bf16[512,1024]{1,0:T(8,128)(2,1)S(1)} %copy-done.4, bf16[512,1024]{1,0:T(8,128)(2,1)S(1)} %copy-done.13, bf16[512,1024]{1,0:T(8,128)(2,1)} %collective-permute-done.6.refs_2_, ...), custom_call_target="tpu_custom_call" | custom-call | flops 6442450944 | bytes 16777216 | tf_op jit(solution)/shard_map/pallas_call | solution.py:526
  480.5 58.2 %collective-permute-done.50 = bf16[256,512]{1,0:T(8,128)(2,1)} collective-permute-done((bf16[256,512]{1,0:T(8,128)(2,1)}, bf16[256,512]{1,0:T(8,128)(2,1)}, u32[]{:S(2)}, u32[]{:S(2)}) %collective-permute-start.50) | collective-permute-done | bytes 262176 | tf_op jit(solution)/shard_map/ppermute | solution.py:740
  545.7 8.8 %collective-permute-done.51 = bf16[512,512]{1,0:T(8,128)(2,1)} collective-permute-done((bf16[512,512]{1,0:T(8,128)(2,1)}, bf16[512,512]{1,0:T(8,128)(2,1)}, u32[]{:S(2)}, u32[]{:S(2)}) %collective-permute-start.51) | collective-permute-done | bytes 524320 | tf_op jit(solution)/shard_map/ppermute | solution.py:746
  562.3 11.8 %collective-permute-done.68 = bf16[128,2048]{1,0:T(8,128)(2,1)S(1)} collective-permute-done((bf16[128,2048]{1,0:T(8,128)(2,1)S(1)}, bf16[128,2048]{1,0:T(8,128)(2,1)S(1)}, u32[]{:S(2)}, u32[]{:S(2)}) %collective-permute-start.68) | collective-permute-done | bytes 524320 | tf_op jit(solution)/shard_map/ppermute | solution.py:710
  582.5 9.2 %shard_map.554 = bf16[1024,3072]{1,0:T(8,128)(2,1)} custom-call(s32[4]{0:T(128)} %multiply_add_fusion.3.row_ref, s32[4]{0:T(128)} %broadcast_14_col_ref.2.col_ref, bf16[512,3072]{1,0:T(8,128)(2,1)} %refs_0_.3, bf16[256,3072]{1,0:T(8,128)(2,1)} %collective-permute-done.56.refs_1_, bf16[256,3072]{1,0:T(8,128)(2,1)} %collective-permute-done.57.refs_2_), custom_call_target="tpu_custom_call" | custom-call | bytes 12582912 | tf_op jit(solution)/shard_map/pallas_call | solution.py:438
  608.0 9.0 %multiply_reduce_fusion = (f32[1024]{0:T(1024)S(1)}, f32[512]{0:T(512)S(1)}, f32[512]{0:T(512)}, f32[1024]{0:T(1024)S(1)}, f32[512,1024]{1,0:T(8,128)}) fusion(f32[512]{0:T(512)S(1)} %copy-done.63, f32[512]{0:T(512)S(1)} %copy-done.61, bf16[1,512,1024]{2,1,0:T(8,128)(2,1)S(1)} %copy-done.17, bf16[1,512,1024]{2,1,0:T(8,128)(2,1)S(1)} %copy-done.20, ...), kind=kOutput, calls=%fused_computation.29 | convolution fusion | flops 3227513856 | bytes 13651968 | tf_op jit(solution)/shard_map/dot_general | solution.py:597
  627.4 18.0 %collective-permute-done.61 = bf16[192,512]{1,0:T(8,128)(2,1)S(1)} collective-permute-done((bf16[192,512]{1,0:T(8,128)(2,1)S(1)}, bf16[192,512]{1,0:T(8,128)(2,1)S(1)}, u32[]{:S(2)}, u32[]{:S(2)}) %collective-permute-start.61) | collective-permute-done | bytes 196640 | tf_op jit(solution)/shard_map/ppermute | solution.py:1047
  652.3 10.5 %collective-permute-done.71 = bf16[128,2048]{1,0:T(8,128)(2,1)S(1)} collective-permute-done((bf16[128,2048]{1,0:T(8,128)(2,1)S(1)}, bf16[128,2048]{1,0:T(8,128)(2,1)S(1)}, u32[]{:S(2)}, u32[]{:S(2)}) %collective-permute-start.71) | collective-permute-done | bytes 524320 | tf_op jit(solution)/shard_map/ppermute | solution.py:746
  (503 shorter events, 353.2 us)
Async XLA Ops:
  32.0 30.6 %collective-permute-start.14 = (bf16[128,4096]{1,0:T(8,128)(2,1)}, bf16[128,4096]{1,0:T(8,128)(2,1)S(1)}, u32[]{:S(2)}, u32[]{:S(2)}) collective-permute-start(bf16[128,4096]{1,0:T(8,128)(2,1)} %shard_map.535), channel_id=1, source_target_pairs={{0,1},{1,0},{2,3},{3,2},{4,5},{5,4},{6,7},{7,6},{8,9},{9,8},{10,11... | collective-permute-start | bytes 3145736 | tf_op jit(solution)/shard_map/ppermute | solution.py:617
  92.9 31.1 %collective-permute-start.16 = (bf16[512,1024]{1,0:T(8,128)(2,1)}, bf16[512,1024]{1,0:T(8,128)(2,1)}, u32[]{:S(2)}, u32[]{:S(2)}) collective-permute-start(bf16[512,1024]{1,0:T(8,128)(2,1)} %collective-permute-done.10), channel_id=1, source_target_pairs={{8,0},{9,1},{10,2},{11,3},{12,4},{13,5},{14,6},{15,7}} | collective-permute-start | bytes 3145736 | tf_op jit(solution)/shard_map/ppermute | solution.py:838
  94.2 29.8 %collective-permute-start.19 = (bf16[512,1024]{1,0:T(8,128)(2,1)}, bf16[512,1024]{1,0:T(8,128)(2,1)}, u32[]{:S(2)}, u32[]{:S(2)}) collective-permute-start(bf16[512,1024]{1,0:T(8,128)(2,1)} %collective-permute-done.11.refs_2_.refs_5_), channel_id=1, source_target_pairs={{0,2},{2,0},{1,3},{3,1},{4,6},{6,4},{5,7},{7,5},{8,10},{10,8},{9,1... | collective-permute-start | bytes 3145736 | tf_op jit(solution)/shard_map/ppermute | solution.py:617
  154.3 55.2 %collective-permute-start.28 = (bf16[512,1024]{1,0:T(8,128)(2,1)}, bf16[512,1024]{1,0:T(8,128)(2,1)}, u32[]{:S(2)}, u32[]{:S(2)}) collective-permute-start(bf16[512,1024]{1,0:T(8,128)(2,1)} %shard_map.544), channel_id=1, source_target_pairs={{0,1},{1,0},{2,3},{3,2},{4,5},{5,4},{6,7},{7,6},{8,9},{9,8},{10,11... | collective-permute-start | bytes 3145736 | tf_op jit(solution)/shard_map/ppermute | solution.py:617
  199.7 41.0 %all-to-all-start = ((bf16[16,64,512]{2,1,0:T(8,128)(2,1)}), bf16[16,64,512]{2,1,0:T(8,128)(2,1)S(1)}, u32[]{:S(2)}, u32[]{:S(2)}) async-start(bf16[16,64,512]{2,1,0:T(8,128)(2,1)} %copy-done.9), calls=%async_computation | async-start | bytes 2097152 | tf_op jit(solution)/shard_map/all_to_all | solution.py:934
  264.6 63.5 %collective-permute-start.36 = (bf16[2048,512]{1,0:T(8,128)(2,1)}, bf16[2048,512]{1,0:T(8,128)(2,1)}, u32[]{:S(2)}, u32[]{:S(2)}) collective-permute-start(bf16[2048,512]{1,0:T(8,128)(2,1)} %convolution_convert_fusion.3), channel_id=1, source_target_pairs={{0,2},{2,0},{1,3},{3,1},{4,6},{6,4},{5,7},{7,5},{8,10},{10,8},{9,1... | collective-permute-start | bytes 6291464 | tf_op jit(solution)/shard_map/ppermute | solution.py:617
  278.3 49.9 %collective-permute-start.37 = (bf16[2048,512]{1,0:T(8,128)(2,1)}, bf16[2048,512]{1,0:T(8,128)(2,1)}, u32[]{:S(2)}, u32[]{:S(2)}) collective-permute-start(bf16[2048,512]{1,0:T(8,128)(2,1)} %add_convert_fusion.3), channel_id=1, source_target_pairs={{0,1},{1,0},{2,3},{3,2},{4,5},{5,4},{6,7},{7,6},{8,9},{9,8},{10,11... | collective-permute-start | bytes 6291464 | tf_op jit(solution)/shard_map/ppermute | solution.py:617
  317.2 78.0 %collective-permute-start.43 = (bf16[512,2048]{1,0:T(8,128)(2,1)}, bf16[512,2048]{1,0:T(8,128)(2,1)}, u32[]{:S(2)}, u32[]{:S(2)}) collective-permute-start(bf16[512,2048]{1,0:T(8,128)(2,1)} %convolution_convert_fusion.1), channel_id=1, source_target_pairs={{0,2},{2,0},{1,3},{3,1},{4,6},{6,4},{5,7},{7,5},{8,10},{10,8},{9,1... | collective-permute-start | bytes 6291464 | tf_op jit(solution)/shard_map/ppermute | solution.py:617
  317.9 40.4 %collective-permute-start.41 = (f32[4096]{0:T(1024)S(1)}, f32[4096]{0:T(1024)S(1)}, u32[]{:S(2)}, u32[]{:S(2)}) collective-permute-start(f32[4096]{0:T(1024)S(1)} %bitcast.283), channel_id=1, source_target_pairs={{0,1},{1,0},{2,3},{3,2},{4,5},{5,4},{6,7},{7,6},{8,9},{9,8},{10,11... | collective-permute-start | bytes 49160 | tf_op jit(solution)/shard_map/ppermute | solution.py:617
  334.0 63.2 %collective-permute-start.44 = (bf16[512,2048]{1,0:T(8,128)(2,1)}, bf16[512,2048]{1,0:T(8,128)(2,1)}, u32[]{:S(2)}, u32[]{:S(2)}) collective-permute-start(bf16[512,2048]{1,0:T(8,128)(2,1)} %add_convert_fusion.2), channel_id=1, source_target_pairs={{0,1},{1,0},{2,3},{3,2},{4,5},{5,4},{6,7},{7,6},{8,9},{9,8},{10,11... | collective-permute-start | bytes 6291464 | tf_op jit(solution)/shard_map/ppermute | solution.py:617
  334.4 88.8 %collective-permute-start.47 = (bf16[512,512]{1,0:T(8,128)(2,1)}, bf16[512,512]{1,0:T(8,128)(2,1)}, u32[]{:S(2)}, u32[]{:S(2)}) collective-permute-start(bf16[512,512]{1,0:T(8,128)(2,1)} %convolution_convert_fusion.6), channel_id=1, source_target_pairs={{0,2},{2,0},{1,3},{3,1},{4,6},{6,4},{5,7},{7,5},{8,10},{10,8},{9,1... | collective-permute-start | bytes 1572872 | tf_op jit(solution)/shard_map/ppermute | solution.py:617
  358.3 31.5 %collective-permute-start.45 = (f32[4096]{0:T(1024)S(1)}, f32[4096]{0:T(1024)S(1)}, u32[]{:S(2)}, u32[]{:S(2)}) collective-permute-start(f32[4096]{0:T(1024)S(1)} %add.563), channel_id=1, source_target_pairs={{0,4},{4,0},{1,5},{5,1},{2,6},{6,2},{3,7},{7,3},{8,12},{12,8},{9,1... | collective-permute-start | bytes 49160 | tf_op jit(solution)/shard_map/ppermute | solution.py:788
  363.3 31.6 %collective-permute-start.40 = (bf16[512,512]{1,0:T(8,128)(2,1)}, bf16[512,512]{1,0:T(8,128)(2,1)S(1)}, u32[]{:S(2)}, u32[]{:S(2)}) collective-permute-start(bf16[512,512]{1,0:T(8,128)(2,1)} %dynamic-slice_bitcast_fusion.3), channel_id=1, source_target_pairs={{0,8},{8,0},{16,24},{24,16},{1,9},{9,1},{17,25},{25,17},{2,10},{10... | collective-permute-start | bytes 1572872 | tf_op jit(solution)/shard_map/ppermute | solution.py:710
  389.9 33.5 %collective-permute-start.48 = (bf16[512,512]{1,0:T(8,128)(2,1)}, bf16[512,512]{1,0:T(8,128)(2,1)}, u32[]{:S(2)}, u32[]{:S(2)}) collective-permute-start(bf16[512,512]{1,0:T(8,128)(2,1)} %add_convert_fusion.7), channel_id=1, source_target_pairs={{0,1},{1,0},{2,3},{3,2},{4,5},{5,4},{6,7},{7,6},{8,9},{9,8},{10,11... | collective-permute-start | bytes 1572872 | tf_op jit(solution)/shard_map/ppermute | solution.py:617
  451.4 154.0 %all-to-all-start.2 = ((bf16[16,192,512]{2,1,0:T(8,128)(2,1)}), bf16[16,192,512]{2,1,0:T(8,128)(2,1)}, u32[]{:S(2)}, u32[]{:S(2)}) async-start(bf16[16,192,512]{2,1,0:T(8,128)(2,1)} %shard_map.550.grad_ref), calls=%async_computation.2 | async-start | bytes 6291456 | tf_op jit(solution)/shard_map/all_to_all | solution.py:1009
  458.5 100.8 %collective-permute-start.56 = (bf16[256,3072]{1,0:T(8,128)(2,1)}, bf16[256,3072]{1,0:T(8,128)(2,1)}, u32[]{:S(2)}, u32[]{:S(2)}) collective-permute-start(bf16[256,3072]{1,0:T(8,128)(2,1)} %shard_map.553), channel_id=1, source_target_pairs={{0,1},{1,0},{2,3},{3,2},{4,5},{5,4},{6,7},{7,6},{8,9},{9,8},{10,11... | collective-permute-start | bytes 4718600 | tf_op jit(solution)/shard_map/ppermute | solution.py:617
  458.5 80.2 %collective-permute-start.50 = (bf16[256,512]{1,0:T(8,128)(2,1)}, bf16[256,512]{1,0:T(8,128)(2,1)}, u32[]{:S(2)}, u32[]{:S(2)}) collective-permute-start(bf16[256,512]{1,0:T(8,128)(2,1)} %fusion.33), channel_id=1, source_target_pairs={{0,16},{8,24},{16,0},{24,8},{1,17},{9,25},{17,1},{25,9},{2,18},{10... | collective-permute-start | bytes 786440 | tf_op jit(solution)/shard_map/ppermute | solution.py:740
  478.5 64.4 %collective-permute-start.52 = (f32[192,512]{1,0:T(8,128)}, f32[192,512]{1,0:T(8,128)}, u32[]{:S(2)}, u32[]{:S(2)}) collective-permute-start(f32[192,512]{1,0:T(8,128)} %bitcast.205), channel_id=1, source_target_pairs={{0,1},{1,0},{2,3},{3,2},{4,5},{5,4},{6,7},{7,6},{8,9},{9,8},{10,11... | collective-permute-start | bytes 1179656 | tf_op jit(solution)/shard_map/ppermute | solution.py:666
  559.8 32.0 %collective-permute-start.76 = (bf16[128,512]{1,0:T(8,128)(2,1)S(1)}, bf16[128,512]{1,0:T(8,128)(2,1)}, u32[]{:S(2)}, u32[]{:S(2)}) collective-permute-start(bf16[128,512]{1,0:T(8,128)(2,1)S(1)} %dynamic-slice_bitcast_fusion.7), channel_id=1, source_target_pairs={{0,8},{8,0},{16,24},{24,16},{1,9},{9,1},{17,25},{25,17},{2,10},{10... | collective-permute-start | bytes 393224 | tf_op jit(solution)/shard_map/ppermute | solution.py:710
  562.3 34.6 %collective-permute-start.54 = (bf16[1024,512]{1,0:T(8,128)(2,1)}, bf16[1024,512]{1,0:T(8,128)(2,1)S(1)}, u32[]{:S(2)}, u32[]{:S(2)}) collective-permute-start(bf16[1024,512]{1,0:T(8,128)(2,1)} %bitcast.56.refs_0_), channel_id=1, source_target_pairs={{0,2},{2,0},{1,3},{3,1},{4,6},{6,4},{5,7},{7,5},{8,10},{10,8},{9,1... | collective-permute-start | bytes 3145736 | tf_op jit(solution)/shard_map/ppermute | solution.py:617
  617.1 31.1 %collective-permute-start.70 = (bf16[64,2048]{1,0:T(8,128)(2,1)S(1)}, bf16[64,2048]{1,0:T(8,128)(2,1)S(1)}, u32[]{:S(2)}, u32[]{:S(2)}) collective-permute-start(bf16[64,2048]{1,0:T(8,128)(2,1)S(1)} %fusion.31), channel_id=1, source_target_pairs={{0,16},{8,24},{16,0},{24,8},{1,17},{9,25},{17,1},{25,9},{2,18},{10... | collective-permute-start | bytes 786440 | tf_op jit(solution)/shard_map/ppermute | solution.py:740
  619.1 32.5 %collective-permute-start.58 = (f32[2,2048]{1,0:T(2,128)S(1)}, f32[2,2048]{1,0:T(2,128)S(1)}, u32[]{:S(2)}, u32[]{:S(2)}) collective-permute-start(f32[2,2048]{1,0:T(2,128)S(1)} %maximum_multiply_fusion), channel_id=1, source_target_pairs={{0,2},{2,0},{1,3},{3,1},{4,6},{6,4},{5,7},{7,5},{8,10},{10,8},{9,1... | collective-permute-start | bytes 49160 | tf_op jit(solution)/shard_map/ppermute | solution.py:617
  668.0 35.8 %collective-permute-start.66 = (bf16[2,4,192,512]{3,2,1,0:T(8,128)(2,1)}, bf16[2,4,192,512]{3,2,1,0:T(8,128)(2,1)}, u32[]{:S(2)}, u32[]{:S(2)}) collective-permute-start(bf16[2,4,192,512]{3,2,1,0:T(8,128)(2,1)} %maximum_select_fusion.1), channel_id=1, source_target_pairs={{0,2},{2,0},{1,3},{3,1},{4,6},{6,4},{5,7},{7,5},{8,10},{10,8},{9,1... | collective-permute-start | bytes 4718600 | tf_op jit(solution)/shard_map/ppermute | solution.py:617
  685.0 36.3 %collective-permute-start.73 = (bf16[256,2048]{1,0:T(8,128)(2,1)S(1)}, bf16[256,2048]{1,0:T(8,128)(2,1)}, u32[]{:S(2)}, u32[]{:S(2)}) collective-permute-start(bf16[256,2048]{1,0:T(8,128)(2,1)S(1)} %bitcast.230), channel_id=1, source_target_pairs={{0,2},{2,0},{1,3},{3,1},{4,6},{6,4},{5,7},{7,5},{8,10},{10,8},{9,1... | collective-permute-start | bytes 3145736 | tf_op jit(solution)/shard_map/ppermute | solution.py:617
  (147 other events, 1973.0 us)

commit v3 on v2

--- a/solution.py
+++ b/solution.py
@@ -11,7 +11,7 @@
 HEADS = 16
 LONG = 2304
 NORM_EPS = 1e-06
-CHUNKS = 4
+CHUNKS = (2, 3, 3, 3, 3, 2)
 HEAD_DIM = 64
 BLOCK = 512
 FAR = 1e30
@@ -314,9 +314,7 @@
             pltpu.VMEM((8, BLOCK), jnp.float32),
         ],
         compiler_params=pltpu.CompilerParams(vmem_limit_bytes=48 * 1024 * 1024),
-        cost_estimate=pl.CostEstimate(
-            flops=FORWARD_COST, bytes_accessed=tokens * 512, transcendentals=0
-        ),
+        cost_estimate=pl.CostEstimate(flops=FORWARD_COST, bytes_accessed=tokens * 512, transcendentals=0),
     )(ends, base, *arrays)
 
 
@@ -369,9 +367,7 @@
         scratch_shapes=scratch,
         input_output_aliases=aliases,
         compiler_params=pltpu.CompilerParams(vmem_limit_bytes=50 * 1024 * 1024),
-        cost_estimate=pl.CostEstimate(
-            flops=BACKWARD_COST * chunk // blocks, bytes_accessed=tokens * 1024, transcendentals=0
-        ),
+        cost_estimate=pl.CostEstimate(flops=BACKWARD_COST * chunk // blocks, bytes_accessed=tokens * 1024, transcendentals=0),
     )(ends, base, *arrays)
 
 
@@ -402,9 +398,7 @@
             in_specs=[pl.BlockSpec((size, cols), lambda j, at_ref: (at_ref[0] * steps + j, 0))],
             out_specs=pl.BlockSpec((size, cols), lambda j, at_ref: (j, 0)),
         ),
-        cost_estimate=pl.CostEstimate(
-            flops=0, bytes_accessed=2 * rows * cols * x.dtype.itemsize, transcendentals=0
-        ),
+        cost_estimate=pl.CostEstimate(flops=0, bytes_accessed=2 * rows * cols * x.dtype.itemsize, transcendentals=0),
     )(index.astype(jnp.int32).reshape(1), x)
 
 
@@ -417,8 +411,8 @@
             out_ref[...] = refs[piece][...].astype(out_ref.dtype)
 
 
-def place(pieces, row_at, col_at, dtype, rows, shape):
-    cols = pieces[0].shape[1]
+def place(pieces, row_at, col_at, dtype, rows, shape, cols=None, block=0):
+    cols = cols or pieces[0].shape[1]
     owner = [n for n, piece in enumerate(pieces) for _ in range(piece.shape[0] // rows)]
     count = len(owner)
     size = block_rows(rows, cols)
@@ -431,7 +425,7 @@
         def index(s, j, row_ref, col_ref):
             inside = j + (s - first) * steps
             end = (last - first + 1) * steps - 1
-            return (jnp.where(s < first, 0, jnp.where(s > last, end, inside)), 0)
+            return (jnp.where(s < first, 0, jnp.where(s > last, end, inside)), block)
 
         return index
 
@@ -454,17 +448,49 @@
     )(row_at, col_at, *pieces)
 
 
+def head_columns_kernel(head_ref, q_ref, k_ref, v_ref, out_ref):
+    odd = lax.rem(head_ref[0], 2) == 1
+    for part, ref in enumerate((q_ref, k_ref, v_ref)):
+        both = ref[...].astype(jnp.float32).T
+        mine = jnp.where(odd, both[HEAD_DIM:], both[:HEAD_DIM])
+        out_ref[part * HEAD_DIM : (part + 1) * HEAD_DIM] = mine.astype(out_ref.dtype)
+
+
+def head_columns(w, head):
+    rows, pairs = w.shape[0], HEADS // 2
+
+    def spec(part):
+        return pl.BlockSpec(
+            (rows, 2 * HEAD_DIM), lambda i, head_ref: (0, part * pairs + head_ref[0] // 2)
+        )
+
+    return pl.pallas_call(
+        head_columns_kernel,
+        out_shape=jax.ShapeDtypeStruct((3 * HEAD_DIM, rows), w.dtype),
+        grid_spec=pltpu.PrefetchScalarGridSpec(
+            num_scalar_prefetch=1,
+            grid=(1,),
+            in_specs=[spec(part) for part in range(3)],
+            out_specs=pl.BlockSpec((3 * HEAD_DIM, rows), lambda i, head_ref: (0, 0)),
+        ),
+    )(head.astype(jnp.int32).reshape(1), w, w, w)
+
+
 def project_kernel(count, place_ref, w_ref, bias_ref, *refs):
     blocks, out_ref, made, sem = refs[:count], refs[-3], refs[-2], refs[-1]
 
     def copy(i):
         return pltpu.make_async_copy(made.at[i], out_ref.at[place_ref[i]], sem.at[i])
 
+    size = w_ref.shape[2]
     for i in range(count):
-        part = lax.dot_general(
-            w_ref[...], blocks[i][...], (((1,), (1,)), ((), ())), preferred_element_type=jnp.float32
-        )
-        made[i] = (part + bias_ref[...]).astype(jnp.bfloat16)
+        total = bias_ref[...]
+        for f in range(w_ref.shape[0]):
+            total += lax.dot_general(
+                w_ref[f], blocks[i][:, f * size : (f + 1) * size], (((1,), (1,)), ((), ())),
+                preferred_element_type=jnp.float32,
+            )
+        made[i] = total.astype(jnp.bfloat16)
         copy(i).start()
     for i in range(count):
         copy(i).wait()
@@ -473,7 +499,7 @@
 def project(so_far, places, w, bias, blocks):
     count = len(blocks)
     rows, width = blocks[0].shape
-    cols = w.shape[0]
+    cols = w.shape[1]
     arrays = [w, bias, *blocks] + ([] if so_far is None else [so_far])
     specs = [vmem_spec()] * (2 + count) + ([] if so_far is None else [any_spec()])
     return pl.pallas_call(
@@ -487,9 +513,7 @@
         ],
         input_output_aliases={} if so_far is None else {3 + count: 0},
         compiler_params=pltpu.CompilerParams(vmem_limit_bytes=24 * 1024 * 1024),
-        cost_estimate=pl.CostEstimate(
-            flops=4 * count * rows * width * cols, bytes_accessed=count * rows * width * 2, transcendentals=0
-        ),
+        cost_estimate=pl.CostEstimate(flops=4 * count * rows * width * cols, bytes_accessed=count * rows * width * 2, transcendentals=0),
     )(jnp.stack(places).astype(jnp.int32), *arrays)
 
 
@@ -533,40 +557,40 @@
             pltpu.SemaphoreType.DMA((SLOTS,)),
         ],
         compiler_params=pltpu.CompilerParams(vmem_limit_bytes=24 * 1024 * 1024),
-        cost_estimate=pl.CostEstimate(
-            flops=4 * count * rows * width * cols, bytes_accessed=count * rows * width * 2, transcendentals=0
-        ),
+        cost_estimate=pl.CostEstimate(flops=4 * count * rows * width * cols, bytes_accessed=count * rows * width * 2, transcendentals=0),
     )(jnp.stack(places).astype(jnp.int32), grad, *blocks)
 
 
-def place_of_head(head):
-    return (head % 2) * (HEADS // 2) + (head // 2 % 2) * (HEADS // 4) + head // 4
-
-
-def weave_kernel(heads_ref, out_ref):
-    heads = heads_ref.shape[0]
+def weave_kernel(count, at_ref, *refs):
+    pieces, (out_ref, held) = refs[:count], refs[count:]
+    for i in range(count):
+        held[at_ref[i]] = pieces[i][...]
     for part in range(3):
-        for pair in range(heads // 2):
+        for pair in range(count // 2):
             rows = slice(part * HEAD_DIM, (part + 1) * HEAD_DIM)
-            both = [heads_ref[place_of_head(2 * pair + i), rows] for i in range(2)]
-            both = jnp.concatenate(both, axis=0)
-            at = (part * heads + 2 * pair) * HEAD_DIM
+            both = jnp.concatenate([held[2 * pair, rows], held[2 * pair + 1, rows]], axis=0)
+            at = (part * count + 2 * pair) * HEAD_DIM
             out_ref[:, at : at + 2 * HEAD_DIM] = both.astype(jnp.float32).T
 
 
-def weave(heads):
-    count, cols, rows = heads.shape
+def weave(pieces, places):
+    count = len(pieces)
+    cols, rows = pieces[0].shape
     size = 128
     return pl.pallas_call(
-        weave_kernel,
+        partial(weave_kernel, count),
         out_shape=jax.ShapeDtypeStruct((rows, count * cols), jnp.float32),
-        grid=(rows // size,),
-        in_specs=[pl.BlockSpec((count, cols, size), lambda i: (0, 0, i))],
-        out_specs=pl.BlockSpec((size, count * cols), lambda i: (i, 0)),
+        grid_spec=pltpu.PrefetchScalarGridSpec(
+            num_scalar_prefetch=1,
+            grid=(rows // size,),
+            in_specs=[pl.BlockSpec((cols, size), lambda i, at_ref: (0, i))] * count,
+            out_specs=pl.BlockSpec((size, count * cols), lambda i, at_ref: (i, 0)),
+            scratch_shapes=[pltpu.VMEM((count, cols, size), pieces[0].dtype)],
+        ),
         cost_estimate=pl.CostEstimate(
             flops=0, bytes_accessed=6 * count * cols * rows, transcendentals=0
         ),
-    )(heads)
+    )(places, *pieces)
 
 
 SEQ = ("z", "y", "c")
@@ -623,11 +647,11 @@
 
 def fetch_fsdp(shard, pieces, *others):
     if lax.axis_size("f") != 2:
-        return [lax.all_gather(shard, "f", axis=0, tiled=True)]
-    rows = shard.shape[0] // (2 * pieces)
+        return [], [lax.all_gather(shard, "f", axis=0, tiled=True)]
     first = lax.axis_index("c") * pieces
     shard = tie(shard, *others)
-    return [swap(take(shard, first + i, 2 * pieces), "f") for i in range(pieces)]
+    taken = [take(shard, first + i, 2 * pieces) for i in range(pieces)]
+    return taken, [swap(part, "f") for part in taken]
 
 
 def share_cores(fetched, *others):
@@ -672,94 +696,132 @@
 
 
 class WeightSum:
-    def __init__(self, left, right, scale, left_dim=0):
-        self.left, self.right, self.scale, self.left_dim = left, right, scale, left_dim
-        self.size = left.shape[1 - left_dim] // lax.axis_size("f")
-        self.cols = right.shape[1] // 2
-
-    def term(self, c, f):
-        left = lax.dynamic_slice_in_dim(self.left, f * self.size, self.size, 1 - self.left_dim)
-        right = lax.dynamic_slice_in_dim(self.right, c * self.cols, self.cols, 1)
-        return dot(left, right, self.left_dim, 0)
+    def __init__(self, terms, scale):
+        self.terms, self.scale = terms, scale
+        self.widths = [right.shape[1] // 2 for _, right, _ in terms]
+        self.cols = sum(self.widths)
+        self.rows = terms[0][0].shape[1 - terms[0][2]] // lax.axis_size("f")
+
+    def after(self, others):
+        self.terms = [(left, tie(right, *others), dim) for left, right, dim in self.terms]
+
+    def term(self, n, c, f, half=None):
+        left, right, dim = self.terms[n]
+        rows, start = self.rows, f * self.rows
+        if half is not None:
+            rows //= 2
+            start = start + half * rows
+        left = lax.dynamic_slice_in_dim(left, start, rows, 1 - dim)
+        right = lax.dynamic_slice_in_dim(right, c * self.widths[n], self.widths[n], 1)
+        return dot(left, right, dim, 0)
+
+    def joined(self, parts):
+        parts = [part.astype(jnp.bfloat16) for part in parts]
+        return parts[0] if len(parts) == 1 else jnp.concatenate(parts, axis=1)
+
+    def half_of(self, x, half):
+        rows = x.shape[0] // 2
+        return lax.dynamic_slice_in_dim(x, half * rows, rows, 0).astype(jnp.float32)
 
     def other_core(self, *others):
-        low = jnp.bfloat16
-        self.right = tie(self.right, *others)
-        core = lax.axis_index("c")
-        parts, here = lax.axis_size("f"), lax.axis_index("f")
+        self.after(others)
+        core, parts, here = lax.axis_index("c"), lax.axis_size("f"), lax.axis_index("f")
         order = [1 - here, here] if parts == 2 else range(parts)
-        sent = [self.term(1 - core, f).astype(low) for f in order]
-        self.got = [swap(part, "c") for part in sent]
+        self.got = []
+        for f in order:
+            sent = [self.term(n, 1 - core, f).astype(jnp.bfloat16) for n in range(len(self.terms))]
+            self.got.append([swap(part, "c") for part in sent])
         return sent[-1]
 
     def other_f(self, *others):
-        low, f32 = jnp.bfloat16, jnp.float32
-        self.right = tie(self.right, *others)
+        self.after(others)
         core, parts, here = lax.axis_index("c"), lax.axis_size("f"), lax.axis_index("f")
+        y, count = lax.axis_index("y"), range(len(self.terms))
         if parts == 2:
-            sent = (self.term(core, 1 - here) + self.got[0].astype(f32)).astype(low)
-            self.far = swap(sent, "f")
+            self.far = []
+            for half in (1 - y, y):
+                sent = self.joined(
+                    [self.term(n, core, 1 - here, half) + self.half_of(self.got[0][n], half) for n in count]
+                )
+                self.far.append(swap(sent, "f"))
+                self.after([sent])
             return sent
-        total = [(self.term(core, f) + self.got[f].astype(f32)).astype(low) for f in range(parts)]
+        total = [
+            self.joined([self.term(n, core, f) + self.got[f][n].astype(jnp.float32) for n in count])
+            for f in range(parts)
+        ]
         self.total = lax.psum_scatter(jnp.stack(total), "f", scatter_dimension=0, tiled=False)
         return self.total
 
-    def half(self, x, axis, pairs, here):
-        x = x.reshape(2, -1, self.cols)
-        sent = pick(x, 1 - here)
-        self.kept, self.coming = pick(x, here), lax.ppermute(sent, axis, pairs)
+    def here_half(self, k, half):
+        core, parts, here = lax.axis_index("c"), lax.axis_size("f"), lax.axis_index("f")
+        if parts != 2:
+            return [self.half_of(self.total, half)]
+        x, at = [], 0
+        for n, width in enumerate(self.widths):
+            total = self.term(n, core, here, half) + self.half_of(self.got[1][n], half)
+            x.append(total + self.far[k][:, at : at + width].astype(jnp.float32))
+            at += width
+        return x
+
+    def near_y(self, *others):
+        self.after(others)
+        sent = self.joined(self.here_half(0, 1 - lax.axis_index("y")))
+        self.coming = lax.ppermute(sent, "y", SWAP)
         return sent
 
-    def near_y(self, *others):
-        low, f32 = jnp.bfloat16, jnp.float32
-        core, parts, here = lax.axis_index("c"), lax.axis_size("f"), lax.axis_index("f")
-        if parts == 2:
-            self.right = tie(self.right, *others)
-            x = self.term(core, here) + self.got[1].astype(f32) + self.far.astype(f32)
-        else:
-            x = self.total
-        return self.half(x.astype(low), "y", SWAP, lax.axis_index("y"))
-
-    def added(self, *others):
-        coming = tie(self.coming, *others)
-        return self.kept.astype(jnp.float32) + coming.astype(jnp.float32)
-
     def near_z(self, *others):
-        x = self.added(*others).astype(jnp.bfloat16)
-        return self.half(x, "z", plane_pairs(1), lax.rem(lax.axis_index("z"), 2))
+        self.coming = tie(self.coming, *others)
+        self.after(others)
+        x, at = [], 0
+        for part in self.here_half(1, lax.axis_index("y")):
+            width = part.shape[1]
+            x.append(part + self.coming[:, at : at + width].astype(jnp.float32))
+            at += width
+        x = self.joined(x).reshape(2, -1, self.cols)
+        low_z = lax.rem(lax.axis_index("z"), 2)
+        sent = pick(x, 1 - low_z)
+        self.kept, self.coming = pick(x, low_z), lax.ppermute(sent, "z", plane_pairs(1))
+        return sent
+
+    def added(self, x, others):
+        return x.astype(jnp.float32) + tie(self.coming, *others).astype(jnp.float32)
 
     def far_z(self, *others):
-        x = self.added(*others).astype(jnp.bfloat16)
-        return self.half(x, "z", plane_pairs(2), lax.axis_index("z") // 2)
-
-    def back_far_z(self, *others):
-        x = self.added(*others)
+        self.x = self.added(self.kept, others).astype(jnp.bfloat16)
+        self.coming = lax.ppermute(self.x, "z", plane_pairs(2))
+        return self.x
+
+    def back_near_z(self, *others):
+        x = self.added(self.x, others)
         if lax.axis_size("g") > 1:
             x = lax.psum(x, "g")
         self.x = (x * self.scale).astype(jnp.bfloat16)
-        self.coming = lax.ppermute(self.x, "z", plane_pairs(2))
-        return self.x
-
-    def back_near_z(self, *others):
-        coming = tie(self.coming, *others)
-        self.x = in_order(self.x, coming, lax.axis_index("z") // 2).reshape(-1, self.cols)
         self.coming = lax.ppermute(self.x, "z", plane_pairs(1))
         return self.x
 
     def back_y(self, *others):
         coming = tie(self.coming, *others)
         x = in_order(self.x, coming, lax.rem(lax.axis_index("z"), 2)).reshape(-1, self.cols)
-        near = swap(x, "y")
-        self.pieces = [x, near, swap(x, "c"), swap(near, "c")]
+        self.near = lax.ppermute(x, "y", SWAP)
+        self.x, self.across = x, swap(x, "c")
         return x
 
-    def result(self, *others):
+    def results(self, *others):
         y, c = lax.axis_index("y"), lax.axis_index("c")
-        pieces = [tie(self.pieces[0], *others)] + self.pieces[1:]
+        near = tie(self.near, *others)
+        pieces = [self.x, near, self.across, swap(near, "c")]
         row_at = linear((0, 1, 0, 1), (1, -1, 1, -1), y, (0, 0, 0, 0), c)
         col_at = linear((0, 0, 1, 1), (0, 0, 0, 0), y, (1, 1, -1, -1), c)
-        rows, cols = pieces[0].shape
-        return place(pieces, row_at, col_at, jnp.float32, rows, (2 * rows, 2 * cols))
+        rows, at, results = pieces[0].shape[0], 0, []
+        for width in self.widths:
+            results.append(
+                place(
+                    pieces, row_at, col_at, jnp.float32, rows, (2 * rows, 2 * width), width, at // width
+                )
+            )
+            at += width
+        return results
 
 
 class VectorSum:
@@ -830,21 +892,21 @@
     up, down = x, x
     hops = {}
     block, plane = x, z
-    state, crossing = None, []
+    state, items = None, []
     for t in range(1, count + 1):
         first = plane * 4
         if t < count:
             up = lax.ppermute(up, "z", [(i, i + 1) for i in range(t - 1, count - 1)])
             down = lax.ppermute(down, "z", [(i, i - 1) for i in range(1, count - t + 1)])
         near = swap(block, "y")
-        across = swap(block, "c")
-        up, down, near, across, crossing, state, _ = lax.optimization_barrier(
-            (up, down, near, across, crossing, state, beside[t - 1] if t <= len(beside) else [])
+        items += [(block, first + 2 * y + c), (swap(block, "c"), first + 2 * y + 1 - c)]
+        across, places = zip(*items)
+        across = lax.optimization_barrier(across)
+        state = use(state, across, places)
+        up, down, near, state, _ = lax.optimization_barrier(
+            (up, down, near, state, beside[t - 1] if t <= len(beside) else [])
         )
-        items = [(block, first + 2 * y + c), (across, first + 2 * y + 1 - c)]
-        items += [(near, first + 2 * (1 - y) + c), *crossing]
-        state = use(state, [item[0] for item in items], [item[1] for item in items])
-        crossing = [(swap(near, "c"), first + 2 * (1 - y) + 1 - c)]
+        items = [(near, first + 2 * (1 - y) + c), (swap(near, "c"), first + 2 * (1 - y) + 1 - c)]
         if t < count:
             hops["up", t], hops["down", t] = up, down
             names = sorted({table[i][t - 1] for i in range(count)})
@@ -854,7 +916,7 @@
                 chosen = (z >= here[0]) & (z <= here[-1])
                 block = hops[name] if block is None else jnp.where(chosen, hops[name], block)
                 plane = jnp.where(chosen, z + (-name[1] if name[0] == "up" else name[1]), plane)
-    return use(state, [item[0] for item in crossing], [item[1] for item in crossing])
+    return use(state, *zip(*items))
 
 
 def body(
@@ -878,10 +940,7 @@
     normed = normed_pre.astype(low)
 
     shard_rows = w_qkv.shape[0]
-    head_cols = lax.dynamic_slice_in_dim(
-        w_qkv.reshape(shard_rows, 3, HEADS, HEAD_DIM), head, 1, 2
-    ).reshape(shard_rows, 3 * HEAD_DIM)
-    head_full = join_small(head_cols).reshape(width, 3 * HEAD_DIM).T
+    head_full = join_small(head_columns(w_qkv, head)).reshape(parts, 3 * HEAD_DIM, shard_rows)
     head_bias = jnp.concatenate(
         [
             lax.dynamic_slice_in_dim(qv_bias, head * HEAD_DIM, HEAD_DIM),
@@ -890,6 +949,7 @@
         ]
     )[:, None]
 
+    normed = tie(normed, head_bias, head_full)
     kept_blocks, kept_places = [], []
 
     def add_blocks(qkv, blocks, places):
@@ -897,12 +957,13 @@
         kept_places.extend(places)
         return project(qkv, places, head_full, head_bias, blocks)
 
-    out_part = fetch_fsdp(w_out, 1, normed)
-    fc1_part = fetch_fsdp(w_fc1, 2, normed)
-    fc2_part = fetch_fsdp(w_fc2, 2, normed)
-    beside = [out_part, fc1_part[:1], fc1_part[1:], fc2_part[:1]]
+    out_taken, out_part = fetch_fsdp(w_out, 1, normed)
+    fc1_taken, fc1_part = fetch_fsdp(w_fc1, 2, normed)
+    fc2_taken, fc2_part = fetch_fsdp(w_fc2, 2, normed)
+    qkv_taken, qkv_part = fetch_fsdp(w_qkv, 2, normed)
+    out_full = join_fsdp(w_out, share_cores(out_part))
+    beside = [out_part + out_taken + fc1_taken + fc2_taken + qkv_taken, [], fc1_part[:1], fc1_part[1:] + [out_full]]
     qkv = gather_group(normed, add_blocks, beside)
-    out_part, fc1_part = share_cores(out_part), share_cores(fc1_part)
     ends = jnp.cumsum(lengths[0]).astype(jnp.int32)
     base = (group * (rows * HEADS)).astype(jnp.int32).reshape(1)
     shift, window = 0, None
@@ -918,10 +979,8 @@
     attended, log_total = attention_forward(
         ends, base, qkv, window, shift
     )
-    qkv_part = fetch_fsdp(w_qkv, 1, attended)
     fc2_part = share_cores(fc2_part, attended)
-    out_full = join_fsdp(w_out, out_part, attended)
-    fc1_full = join_fsdp(w_fc1, fc1_part, attended)
+    fc1_full = join_fsdp(w_fc1, share_cores(fc1_part), attended)
     fc2_full = join_fsdp(w_fc2, fc2_part, attended)
     small = (b_out, ln2_gain, ln2_bias, b_fc1, b_fc2)
     packed = join_small(tie(jnp.concatenate(small), normed))
@@ -934,7 +993,7 @@
     mixed = lax.all_to_all(attended, SEQ, 0, 0, tiled=True).reshape(width, rows)
 
     branch = dot(mixed, out_full, 0, 0) + out_bias
-    middle = hidden + tie(branch, fc2_full)
+    middle = hidden + tie(branch, fc2_full, qkv_part[0])
     normed_two_pre, scaled_two, inv_two = norm_forward(middle, gain_two, bias_two)
     normed_two = normed_two_pre.astype(low)
     inner_sum = dot(normed_two, fc1_full, 1, 0) + fc1_bias
@@ -943,61 +1002,51 @@
 
     out_cot = out_grad[0]
     cot_full = out_cot.astype(f32)
-    qkv_part = share_cores(qkv_part, active_low)
-    fc2_sum = WeightSum(active_low, out_cot, scale)
+    active_low, *qkv_part = lax.optimization_barrier((active_low, *qkv_part))
+    qkv_part = share_cores(qkv_part)
+    fc2_sum = WeightSum([(active_low, out_cot, 0)], scale)
     token = fc2_sum.other_core()
-    block_out = middle + (dot(tie(active_low, token), fc2_full, 1, 0) + fc2_bias)
-    token = fc2_sum.other_f(block_out)
     active_grad = dot(tie(out_cot, token), fc2_full, 1, 1)
     inner_grad = gelu_pull(active_grad)[0].astype(low)
-    fc1_sum = WeightSum(normed_two, inner_grad, scale)
-    norm_two_grad = dot(inner_grad, fc1_full, 1, 1)
+    token = fc2_sum.other_f(inner_grad)
+    norm_two_grad = dot(tie(inner_grad, token), fc1_full, 1, 1)
     gain_two_grad, bias_two_grad, middle_from_norm = norm_backward(
         norm_two_grad, scaled_two, inv_two, gain_two
     )
     middle_grad = cot_full + middle_from_norm
     branch_grad = middle_grad.astype(low)
-    out_sum = WeightSum(mixed, branch_grad, scale, 1)
     mixed_grad = dot(out_full, branch_grad, 1, 1).astype(low)
     attended_grad = lax.all_to_all(
         mixed_grad.reshape(HEADS, HEAD_DIM, rows), SEQ, 0, 0, tiled=True
     )
-    early = VectorSum(
-        (
-            jnp.sum(branch_grad.astype(f32), axis=0),
-            gain_two_grad,
-            bias_two_grad,
-            jnp.sum(inner_grad.astype(f32), axis=0),
-            jnp.sum(cot_full, axis=0),
-        ),
-        scale,
-    )
-    token = fc1_sum.other_core(mixed_grad)
-    early.core(mixed_grad)
-    token = early.other_f(token)
-    token = fc1_sum.other_f(token)
-    token = out_sum.other_core(token)
+    rest_sum = WeightSum([(normed_two, inner_grad, 0), (mixed, branch_grad, 1)], scale)
+    token = rest_sum.other_core(mixed_grad)
     token = fc2_sum.near_y(token)
-    tokens = [out_sum.other_f(token)]
-
-    chunk = HEADS if groups > 1 else HEADS // CHUNKS
-    plan = {
-        0: [fc2_sum.near_z, early.near_y],
-        1: [fc2_sum.far_z, fc1_sum.near_y, early.near_z],
-        2: [fc2_sum.back_far_z, fc1_sum.near_z, out_sum.near_y, early.far_z],
-        3: [fc2_sum.back_near_z, fc1_sum.far_z, out_sum.near_z, early.result],
-    }
-    carried = None
-    for step in range(HEADS // chunk):
+    token = rest_sum.other_f(token)
+    block_out = middle + (dot(tie(active_low, token), fc2_full, 1, 0) + fc2_bias)
+    tokens = [block_out]
+
+    plan = [
+        [fc2_sum.near_z, rest_sum.near_y],
+        [fc2_sum.far_z, rest_sum.near_z],
+        [fc2_sum.back_near_z, rest_sum.far_z],
+        [fc2_sum.back_y],
+        [rest_sum.back_near_z, lambda *after: fc2_sum.near],
+        [rest_sum.back_y],
+    ]
+    carried, first = None, 0
+    for chunk in [HEADS] if groups > 1 else CHUNKS:
         results = attention_backward(
             ends, tie(base, *tokens), qkv, window, attended, attended_grad, log_total, shift,
-            step * chunk, chunk, carried,
+            first, chunk, carried,
         )
-        carried = results[::-1]
-        tokens = [move(results[0]) for move in plan.pop(step)]
-    for left in plan.values():
-        for move in left:
-            move(results[0])
+        carried, first = results[::-1], first + chunk
+        tokens = []
+        for move in plan.pop(0):
+            tokens.append(move(results[0], *tokens))
+    for moves in plan:
+        for move in moves:
+            tokens.append(move(results[0]))
     head_grad, *window_grad = results
     if groups > 1:
         both = window_grad[0]
@@ -1006,10 +1055,9 @@
         after = lax.ppermute(both[margin + HEADS :], "g", up)
         inner = inner.at[HEADS - margin :].add(before).at[:margin].add(after)
         head_grad = jnp.concatenate([head_grad, inner.astype(low)], axis=1)
-    token_grad = lax.all_to_all(head_grad, SEQ, 0, 0, tiled=True)
+    token_grad = lax.all_to_all(tie(head_grad, *tokens), SEQ, 0, 0, tiled=True)
 
     weight_part = head_weight(kept_places, head_grad, kept_blocks)
-    qkv_full = join_fsdp(w_qkv, qkv_part, weight_part)
     weight_part = weight_part.reshape(3 * HEAD_DIM, parts, shard_rows).transpose(1, 0, 2)
     if parts == 2:
         weight_part = halve(weight_part, "f")
@@ -1019,12 +1067,14 @@
         weight_part = lax.psum(weight_part, "g")
 
     weight_part = (weight_part * scale).astype(low)
-    fc2_sum.back_y(weight_part)
-    fc1_sum.back_far_z(weight_part)
-    out_sum.far_z(weight_part)
-    fc1_sum.back_near_z()
-    out_sum.back_far_z()
-    fc2_grad = fc2_sum.result()
+    qkv_full = join_fsdp(w_qkv, qkv_part, weight_part)
+    (fc2_grad,) = fc2_sum.results(qkv_full)
+    fc1_grad, out_weight_grad = rest_sum.results(fc2_grad)
+    token_grad = tie(token_grad, fc1_grad, out_weight_grad)
+    z, y, c = (lax.axis_index(axis) for axis in SEQ)
+    hops = [weight_part] + [
+        lax.ppermute(weight_part, "z", [(i, (i + k) % 4) for i in range(4)]) for k in range(1, 4)
+    ]
 
     token_grad = (
         tie(token_grad, fc2_grad).reshape(HEADS, 3, HEAD_DIM, rows).transpose(1, 0, 2, 3).reshape(3 * width, rows)
@@ -1041,29 +1091,36 @@
     qv_grad = lax.dynamic_update_slice(
         qv_grad, head_sums[2 * HEAD_DIM :], (width + head * HEAD_DIM,)
     )
-    late = VectorSum((gain_one_grad, bias_one_grad, qv_grad), scale)
+    late = VectorSum(
+        (
+            gain_one_grad,
+            bias_one_grad,
+            qv_grad,
+            jnp.sum(branch_grad.astype(f32), axis=0),
+            gain_two_grad,
+            bias_two_grad,
+            jnp.sum(inner_grad.astype(f32), axis=0),
+            jnp.sum(cot_full, axis=0),
+        ),
+        scale,
+    )
+    hops = [tie(piece, gain_one_grad) for piece in hops]
     token = late.core()
-    hops = [
-        lax.ppermute(tie(weight_part, token), "z", [(i, (i + k) % 4) for i in range(4)]) for k in range(1, 4)
-    ]
     token = late.other_f(token)
-    fc1_sum.back_y(token)
-    out_sum.back_near_z(token)
-    plane = lax.axis_index("z")
-    planes = jnp.zeros((4,) + weight_part.shape, low)
-    for k, piece in enumerate([weight_part] + hops):
-        planes = lax.dynamic_update_index_in_dim(planes, piece, lax.rem(plane + 4 - k, 4), 0)
-    planes = in_order(planes, swap(planes, "y"), lax.axis_index("y"))
-    late.near_y(planes)
-    out_sum.back_y(planes)
-    planes = in_order(planes, swap(planes, "c"), lax.axis_index("c"))
-    late.near_z(planes)
-    qkv_weight_grad = weave(planes.reshape((HEADS,) + weight_part.shape))
-    late.far_z(qkv_weight_grad)
-    fc1_grad, out_weight_grad = fc1_sum.result(), out_sum.result()
-    late.result(fc1_grad)
-    ln1_gain_sum, ln1_bias_sum, qv_sum = late.vectors()
-    out_bias_sum, ln2_gain_sum, ln2_bias_sum, fc1_bias_sum, fc2_bias_sum = early.vectors()
+    pieces = hops + [swap(piece, "y") for piece in hops]
+    pieces += [swap(tie(piece, token), "c") for piece in pieces]
+    token = late.near_y(token)
+    token = late.near_z(token)
+    late.far_z(token)
+    planes = lax.rem(z + 4 - jnp.arange(4, dtype=jnp.int32), 4) * 4
+    near_places = [planes + 2 * y + c, planes + 2 * (1 - y) + c]
+    places = jnp.concatenate(near_places + [place_at + 1 - 2 * c for place_at in near_places])
+    qkv_weight_grad = weave(pieces, places)
+    late.result()
+    (
+        ln1_gain_sum, ln1_bias_sum, qv_sum, out_bias_sum,
+        ln2_gain_sum, ln2_bias_sum, fc1_bias_sum, fc2_bias_sum,
+    ) = late.vectors()
     return (
         block_out.astype(low)[None],
         patch_grad[None],

time: 741 us -> 636 us (0.86)
  waiting for transfers between devices: 235 us -> 148 us
  other arithmetic: 51.4 us -> 33.9 us
  Pallas kernels: 216 us -> 231 us
  starting transfers between devices: 98.6 us -> 86.1 us
  local copies, waits for them, and re-layouts: 44.3 us -> 33.5 us
  matrix products: 81.6 us -> 90.2 us
    ppermute x15 -> x11, waiting for transfers between devices: 100 us -> 42.6 us  [the longest x2 26.8 us: back_y(): self.near = lax.ppermute(x, 'y', SWAP)]
    ppermute x3 -> x2, waiting for transfers between devices: 24.1 us -> 3.28 us  [back_near_z(): self.coming = lax.ppermute(self.x, 'z', plane_pairs(1))]
    ppermute x3, waiting for transfers between devices: 27 us -> 13.6 us  [gather_group(): lax.ppermute(down, 'z', [(i, i - 1) for i in range(1, count - t + 1)])]
    select_n x10 -> x4, other arithmetic: 14.3 us -> 2.52 us  [in_order(): jnp.where(position == 0, jnp.stack([own, other]), jnp.stack([other, own]))]
    pallas_call x4 -> x6, Pallas kernels: 84.8 us -> 94.3 us  [attention_backward(): pl.pallas_call(partial(backward_kernel, ends.shape[0], shift, first_block...]
    ppermute x1, waiting for transfers between devices: 0.01 us -> 8.75 us  [halve(): got = lax.ppermute(pick(x, 1 - here), axis, pairs)]
    dot_general x19 -> x25, matrix products: 81.6 us -> 90.2 us  [dot(): lax.dot_general(a, b, (((a_dim,), (b_dim,)), ((), ())), preferred_element...]
    ppermute x6 -> x3, starting transfers between devices: 7.75 us -> 0.08 us  [hop(): self.coming = lax.ppermute(self.x, axis, pairs)]
  transfers between devices with their start and end apart: 87 -> 85, of which waited for: 26 -> 30; matrix products, arithmetic and copies ran while one was open for 17% -> 19% of each run, Pallas kernels for 26% -> 36%
where the time goes in v3:
time: 636 us; the launch traced here: 626 us
  Pallas kernels  231 us (36%)
  waiting for transfers between devices  148 us (23%)
  matrix products  90.2 us (14%)
  starting transfers between devices  86.1 us (14%)
  other arithmetic  33.9 us (5%)
  local copies, waits for them, and re-layouts  33.5 us (5%)
    pallas_call x6, Pallas kernels, attention_backward(): pl.pallas_call(partial(backward_kernel, ends.shape[0], shift, first_block...  94.3 us
    dot_general x25, matrix products, dot(): lax.dot_general(a, b, (((a_dim,), (b_dim,)), ((), ())), preferred_element...  90.2 us
    ppermute x59, waiting for transfers between devices, swap(): return lax.ppermute(x, axis, SWAP)  71.7 us
    pallas_call x7, Pallas kernels, place(): pl.pallas_call(partial(place_kernel, owner), out_shape=jax.ShapeDtypeStru...  46.9 us
    pallas_call x1, Pallas kernels, attention_forward(): pl.pallas_call(partial(forward_kernel, ends.shape[0], shift), out_shape=(...  36.3 us
    ppermute x59, starting transfers between devices, swap(): return lax.ppermute(x, axis, SWAP)  32.9 us
    ppermute x2, waiting for transfers between devices, back_y(): self.near = lax.ppermute(x, 'y', SWAP)  26.8 us
    pallas_call x5, Pallas kernels, project(): pl.pallas_call(partial(project_kernel, count), out_shape=jax.ShapeDtypeSt...  21.2 us
  transfers between devices with their start and end apart: 85, of which 30 were waited for; matrix products, arithmetic and copies ran while one was open for 19% of the time, Pallas kernels for 36%

profile of v3, /device:TPU:0, one launch (start us, length us, event | category | flops | bytes accessed | tf_op | source)
XLA Modules:
  0.0 625.6 jit_solution(3085833126414993207)
XLA Ops:
  59.8 14.7 %collective-permute-done.11.refs_0_.refs_6_ = bf16[512,1024]{1,0:T(8,128)(2,1)} collective-permute-done((bf16[512,1024]{1,0:T(8,128)(2,1)}, bf16[512,1024]{1,0:T(8,128)(2,1)}, u32[]{:S(2)}, u32[]{:S(2)}) %collective-permute-start.11) | collective-permute-done | bytes 1048608 | tf_op jit(solution)/shard_map/ppermute | solution.py:641
  93.9 12.1 %collective-permute-done.19.refs_1_ = bf16[128,4096]{1,0:T(8,128)(2,1)} collective-permute-done((bf16[128,4096]{1,0:T(8,128)(2,1)}, bf16[128,4096]{1,0:T(8,128)(2,1)}, u32[]{:S(2)}, u32[]{:S(2)}) %collective-permute-start.19) | collective-permute-done | bytes 1048608 | tf_op jit(solution)/shard_map/ppermute | solution.py:641
  106.3 8.1 %collective-permute-done.15 = bf16[512,1024]{1,0:T(8,128)(2,1)} collective-permute-done((bf16[512,1024]{1,0:T(8,128)(2,1)}, bf16[512,1024]{1,0:T(8,128)(2,1)}, u32[]{:S(2)}, u32[]{:S(2)}) %collective-permute-start.15) | collective-permute-done | bytes 1048608 | tf_op jit(solution)/shard_map/ppermute | solution.py:900
  132.7 9.9 %collective-permute-done.23.refs_2_ = bf16[128,4096]{1,0:T(8,128)(2,1)} collective-permute-done((bf16[128,4096]{1,0:T(8,128)(2,1)}, bf16[128,4096]{1,0:T(8,128)(2,1)}, u32[]{:S(2)}, u32[]{:S(2)}) %collective-permute-start.23) | collective-permute-done | bytes 1048608 | tf_op jit(solution)/shard_map/ppermute | solution.py:641
  149.9 36.3 %shard_map.493 = (bf16[16,64,512]{2,1,0:T(8,128)(2,1)S(1)}, f32[1,8192]{1,0:T(1,128)S(1)}) custom-call(s32[8]{0:T(128)S(1)} %bitcast.132, s32[1]{0:T(128)} %constant.117.clone.1.base_ref, bf16[16,192,512]{2,1,0:T(8,128)(2,1)S(1)} %shard_map.492.own_ref), custom_call_target="tpu_custom_call" | custom-call | flops 49999998976 | bytes 4194304 | tf_op jit(solution)/shard_map/pallas_call | solution.py:302
  201.4 8.9 %shard_map.495 = bf16[1024,4096]{1,0:T(8,128)(2,1)} custom-call(s32[8]{0:T(128)} %multiply_add_fusion.2.row_ref, s32[8]{0:T(128)} %broadcast_17_col_ref.2.col_ref, bf16[512,4096]{1,0:T(8,128)(2,1)} %refs_0_.3, bf16[128,4096]{1,0:T(8,128)(2,1)} %collective-permute-done.19.refs_1_, bf16[128,4096]{1,0:T(8,128)(2,1)} %collective-permute-done.23.refs_2_, ...), custom_call_target="tpu_custom_call" | custom-call | bytes 16777216 | tf_op jit(solution)/shard_map/pallas_call | solution.py:432
  210.3 9.2 %shard_map.494 = bf16[4096,1024]{1,0:T(8,128)(2,1)} custom-call(s32[8]{0:T(128)} %multiply_add_fusion.2.row_ref, s32[8]{0:T(128)} %broadcast_17_col_ref.2.col_ref, bf16[2048,1024]{1,0:T(8,128)(2,1)} %refs_0_.2, bf16[512,1024]{1,0:T(8,128)(2,1)} %collective-permute-done.27.refs_1_, bf16[512,1024]{1,0:T(8,128)(2,1)} %collective-permute-done.28.refs_2_, ...), custom_call_target="tpu_custom_call" | custom-call | bytes 16777216 | tf_op jit(solution)/shard_map/pallas_call | solution.py:432
  225.5 8.6 %multiply_convert_fusion = (bf16[512,4096]{1,0:T(8,128)(2,1)S(1)}, f32[512,4096]{1,0:T(8,128)}) fusion(f32[4096]{0:T(1024)S(1)} %bitcast.177, bf16[512,1024]{1,0:T(8,128)(2,1)S(1)} %add_convert_fusion.8, bf16[1024,4096]{1,0:T(8,128)(2,1)S(1)} %copy-done.36), kind=kOutput, calls=%fused_computation.10 | convolution fusion | flops 4315938816 | bytes 22036480 | tf_op jit(solution)/shard_map/dot_general | solution.py:621
  240.5 12.7 %convert_reduce_fusion = (f32[4096]{0:T(1024)S(1)}, bf16[512,4096]{1,0:T(8,128)(2,1)S(1)}) fusion(f32[512,4096]{1,0:T(8,128)} %get-tuple-element.271, f32[4096]{0:T(1024)S(1)} %bitcast.178, bf16[512,1024]{1,0:T(8,128)(2,1)S(1)} %bitcast.153, bf16[4096,1024]{1,0:T(8,128)(2,1)S(1)} %bitcast.147), kind=kOutput, calls=%fused_computation.9 | convolution fusion | flops 4343197696 | bytes 22052864 | tf_op jit(solution)/shard_map/dot_general | solution.py:621
  293.0 8.4 %collective-permute-done.37 = bf16[1024,512]{1,0:T(8,128)(2,1)} collective-permute-done((bf16[1024,512]{1,0:T(8,128)(2,1)}, bf16[1024,512]{1,0:T(8,128)(2,1)}, u32[]{:S(2)}, u32[]{:S(2)}) %collective-permute-start.37) | collective-permute-done | bytes 1048608 | tf_op jit(solution)/shard_map/ppermute | solution.py:641
  316.0 9.0 %add_add_fusion = bf16[512,1024]{1,0:T(8,128)(2,1)} fusion(f32[512,1024]{1,0:T(8,128)S(1)} %copy-done.22, bf16[512,4096]{1,0:T(8,128)(2,1)S(1)} %copy-done.45, bf16[4096,1024]{1,0:T(8,128)(2,1)} %shard_map.494, f32[1024]{0:T(1024)S(1)} %bitcast.181), kind=kOutput, calls=%fused_computation.32 | convolution fusion | flops 4296540160 | bytes 15732736 | tf_op jit(solution)/shard_map/dot_general | solution.py:621
  325.1 10.3 %shard_map.496 = (bf16[16,192,512]{2,1,0:T(8,128)(2,1)}, f32[8192,128]{1,0:T(8,128)}) custom-call(s32[8]{0:T(128)S(1)} %bitcast.133, s32[1]{0:T(128)} %constant.117.clone.1.base_ref, bf16[16,192,512]{2,1,0:T(8,128)(2,1)} %copy-done, bf16[16,64,512]{2,1,0:T(8,128)(2,1)S(1)} %copy-done.8, bf16[16,64,512]{2,1,0:T(8,128)(2,1)S(1)} %all-to-all-done.1.refs_1_, ...), custom_call_target="tpu_custom_call" | custom-call | flops 9374999552 | bytes 1048576 | tf_op jit(solution)/shard_map/pallas_call | solution.py:362
  344.0 8.0 %collective-permute-done.43 = bf16[256,2560]{1,0:T(8,128)(2,1)} collective-permute-done((bf16[256,2560]{1,0:T(8,128)(2,1)}, bf16[256,2560]{1,0:T(8,128)(2,1)}, u32[]{:S(2)}, u32[]{:S(2)}) %collective-permute-start.43) | collective-permute-done | bytes 1310752 | tf_op jit(solution)/shard_map/ppermute | solution.py:641
  358.8 22.1 %shard_map.497 = (bf16[16,192,512]{2,1,0:T(8,128)(2,1)}, f32[8192,128]{1,0:T(8,128)}) custom-call(s32[8]{0:T(128)S(1)} %bitcast.134, s32[1]{0:T(128)} %constant.117.clone.1.base_ref, bf16[16,192,512]{2,1,0:T(8,128)(2,1)} %copy-done, bf16[16,64,512]{2,1,0:T(8,128)(2,1)S(1)} %copy-done.8, ...), custom_call_target="tpu_custom_call", output_to_operand_aliasing={{0}: (7, {}), {1}: (6, {})} | custom-call | flops 14062499840 | bytes 1572864 | tf_op jit(solution)/shard_map/pallas_call | solution.py:362
  393.4 21.9 %shard_map.498 = (bf16[16,192,512]{2,1,0:T(8,128)(2,1)}, f32[8192,128]{1,0:T(8,128)}) custom-call(s32[8]{0:T(128)S(1)} %bitcast.135, s32[1]{0:T(128)} %constant.117.clone.1.base_ref, bf16[16,192,512]{2,1,0:T(8,128)(2,1)} %copy-done, bf16[16,64,512]{2,1,0:T(8,128)(2,1)S(1)} %copy-done.8, ...), custom_call_target="tpu_custom_call", output_to_operand_aliasing={{0}: (7, {}), {1}: (6, {})} | custom-call | flops 14062499840 | bytes 1572864 | tf_op jit(solution)/shard_map/pallas_call | solution.py:362
  420.9 13.9 %shard_map.499 = (bf16[16,192,512]{2,1,0:T(8,128)(2,1)}, f32[8192,128]{1,0:T(8,128)}) custom-call(s32[8]{0:T(128)S(1)} %bitcast.136, s32[1]{0:T(128)} %constant.117.clone.1.base_ref, bf16[16,192,512]{2,1,0:T(8,128)(2,1)} %copy-done, bf16[16,64,512]{2,1,0:T(8,128)(2,1)S(1)} %copy-done.8, ...), custom_call_target="tpu_custom_call", output_to_operand_aliasing={{0}: (7, {}), {1}: (6, {})} | custom-call | flops 14062499840 | bytes 1572864 | tf_op jit(solution)/shard_map/pallas_call | solution.py:362
  440.4 13.9 %shard_map.500 = (bf16[16,192,512]{2,1,0:T(8,128)(2,1)}, f32[8192,128]{1,0:T(8,128)}) custom-call(s32[8]{0:T(128)S(1)} %bitcast.137, s32[1]{0:T(128)} %constant.117.clone.1.base_ref, bf16[16,192,512]{2,1,0:T(8,128)(2,1)} %copy-done, bf16[16,64,512]{2,1,0:T(8,128)(2,1)S(1)} %copy-done.8, ...), custom_call_target="tpu_custom_call", output_to_operand_aliasing={{0}: (7, {}), {1}: (6, {})} | custom-call | flops 14062499840 | bytes 1572864 | tf_op jit(solution)/shard_map/pallas_call | solution.py:362
  462.4 12.2 %shard_map.501.grad_ref = bf16[16,192,512]{2,1,0:T(8,128)(2,1)} custom-call(s32[8]{0:T(128)S(1)} %bitcast.138, s32[1]{0:T(128)} %constant.117.clone.1.base_ref, bf16[16,192,512]{2,1,0:T(8,128)(2,1)} %copy-done, bf16[16,64,512]{2,1,0:T(8,128)(2,1)S(1)} %copy-done.8, bf16[16,64,512]{2,1,0:T(8,128)(2,1)S(1)} %all-to-all-done.1.refs_1_, ...), custom_call_target="tpu_custom_call", output_to_operand_aliasing={{}: (7, {})} | custom-call | flops 9374999552 | bytes 1048576 | tf_op jit(solution)/shard_map/pallas_call | solution.py:362
  484.0 8.9 %shard_map.502 = f32[192,1024]{1,0:T(8,128)S(1)} custom-call(s32[16]{0:T(128)S(1)} %stack.229.place_ref, bf16[16,192,512]{2,1,0:T(8,128)(2,1)S(1)} %copy-done.1, bf16[512,1024]{1,0:T(8,128)(2,1)} %add_convert_fusion.9.refs_0_, bf16[512,1024]{1,0:T(8,128)(2,1)S(1)} %copy-done.11, bf16[512,1024]{1,0:T(8,128)(2,1)} %collective-permute-done.6.refs_0_.refs_2_, ...), custom_call_target="tpu_custom_call" | custom-call | flops 6442450944 | bytes 16777216 | tf_op jit(solution)/shard_map/pallas_call | solution.py:550
  501.6 8.7 %collective-permute-done.55 = f32[192,512]{1,0:T(8,128)S(1)} collective-permute-done((f32[192,512]{1,0:T(8,128)S(1)}, f32[192,512]{1,0:T(8,128)S(1)}, u32[]{:S(2)}, u32[]{:S(2)}) %collective-permute-start.55) | collective-permute-done | bytes 393248 | tf_op jit(solution)/shard_map/ppermute | solution.py:690
  510.5 8.0 %shard_map.503 = bf16[1024,3072]{1,0:T(8,128)(2,1)} custom-call(s32[8]{0:T(128)} %multiply_add_fusion.2.row_ref, s32[8]{0:T(128)} %broadcast_17_col_ref.2.col_ref, bf16[512,3072]{1,0:T(8,128)(2,1)} %refs_0_.4, bf16[128,3072]{1,0:T(8,128)(2,1)} %collective-permute-done.31.refs_1_, bf16[128,3072]{1,0:T(8,128)(2,1)} %collective-permute-done.34.refs_2_, ...), custom_call_target="tpu_custom_call" | custom-call | bytes 12582912 | tf_op jit(solution)/shard_map/pallas_call | solution.py:432
  528.0 19.0 %collective-permute-done.54.refs_1_ = bf16[256,2560]{1,0:T(8,128)(2,1)} collective-permute-done((bf16[256,2560]{1,0:T(8,128)(2,1)}, bf16[256,2560]{1,0:T(8,128)(2,1)}, u32[]{:S(2)}, u32[]{:S(2)}) %collective-permute-start.54) | collective-permute-done | bytes 1310752 | tf_op jit(solution)/shard_map/ppermute | solution.py:806
  563.1 8.3 %multiply_reduce_fusion.1 = (f32[1024]{0:T(1024)S(1)}, f32[512]{0:T(512)S(1)}, f32[512]{0:T(512)S(1)}, f32[1024]{0:T(1024)S(1)}, f32[512,1024]{1,0:T(8,128)}) fusion(f32[512]{0:T(512)S(1)} %copy-done.68, f32[512]{0:T(512)S(1)} %copy-done.66, bf16[1,512,1024]{2,1,0:T(8,128)(2,1)S(1)} %copy-done.25, bf16[1,512,1024]{2,1,0:T(8,128)(2,1)S(1)} %copy-done.28, ...), kind=kOutput, calls=%fused_computation.22 | convolution fusion | flops 3227513856 | bytes 13651968 | tf_op jit(solution)/shard_map/dot_general | solution.py:621
  587.2 10.8 %collective-permute-done.68.refs_2_ = bf16[192,512]{1,0:T(8,128)(2,1)S(1)} collective-permute-done((bf16[192,512]{1,0:T(8,128)(2,1)S(1)}, bf16[192,512]{1,0:T(8,128)(2,1)S(1)}, u32[]{:S(2)}, u32[]{:S(2)}) %collective-permute-start.68) | collective-permute-done | bytes 196640 | tf_op jit(solution)/shard_map/ppermute | solution.py:1076
  (492 shorter events, 319.1 us)
Async XLA Ops:
  14.3 29.7 %collective-permute-start.4 = (bf16[512,1024]{1,0:T(8,128)(2,1)}, bf16[512,1024]{1,0:T(8,128)(2,1)}, u32[]{:S(2)}, u32[]{:S(2)}) collective-permute-start(bf16[512,1024]{1,0:T(8,128)(2,1)} %add_convert_fusion.9.refs_0_), channel_id=1, source_target_pairs={{0,8},{8,16},{16,24},{1,9},{9,17},{17,25},{2,10},{10,18},{18,26},{... | collective-permute-start | bytes 3145736 | tf_op jit(solution)/shard_map/ppermute | solution.py:899
  85.4 28.9 %collective-permute-start.15 = (bf16[512,1024]{1,0:T(8,128)(2,1)}, bf16[512,1024]{1,0:T(8,128)(2,1)}, u32[]{:S(2)}, u32[]{:S(2)}) collective-permute-start(bf16[512,1024]{1,0:T(8,128)(2,1)} %collective-permute-done.10), channel_id=1, source_target_pairs={{8,0},{9,1},{10,2},{11,3},{12,4},{13,5},{14,6},{15,7}} | collective-permute-start | bytes 3145736 | tf_op jit(solution)/shard_map/ppermute | solution.py:900
  143.2 51.9 %collective-permute-start.28 = (bf16[512,1024]{1,0:T(8,128)(2,1)}, bf16[512,1024]{1,0:T(8,128)(2,1)}, u32[]{:S(2)}, u32[]{:S(2)}) collective-permute-start(bf16[512,1024]{1,0:T(8,128)(2,1)} %shard_map.485), channel_id=1, source_target_pairs={{0,1},{1,0},{2,3},{3,2},{4,5},{5,4},{6,7},{7,6},{8,9},{9,8},{10,11... | collective-permute-start | bytes 3145736 | tf_op jit(solution)/shard_map/ppermute | solution.py:641
  144.6 50.5 %collective-permute-start.27 = (bf16[512,1024]{1,0:T(8,128)(2,1)}, bf16[512,1024]{1,0:T(8,128)(2,1)}, u32[]{:S(2)}, u32[]{:S(2)}) collective-permute-start(bf16[512,1024]{1,0:T(8,128)(2,1)} %shard_map.484), channel_id=1, source_target_pairs={{0,1},{1,0},{2,3},{3,2},{4,5},{5,4},{6,7},{7,6},{8,9},{9,8},{10,11... | collective-permute-start | bytes 3145736 | tf_op jit(solution)/shard_map/ppermute | solution.py:641
  187.9 31.6 %all-to-all-start = ((bf16[16,64,512]{2,1,0:T(8,128)(2,1)}), bf16[16,64,512]{2,1,0:T(8,128)(2,1)S(1)}, u32[]{:S(2)}, u32[]{:S(2)}) async-start(bf16[16,64,512]{2,1,0:T(8,128)(2,1)} %copy-done.7), calls=%async_computation | async-start | bytes 2097152 | tf_op jit(solution)/shard_map/all_to_all | solution.py:993
  198.4 35.7 %collective-permute-start.34 = (bf16[128,3072]{1,0:T(8,128)(2,1)}, bf16[128,3072]{1,0:T(8,128)(2,1)}, u32[]{:S(2)}, u32[]{:S(2)}) collective-permute-start(bf16[128,3072]{1,0:T(8,128)(2,1)} %shard_map.487), channel_id=1, source_target_pairs={{0,1},{1,0},{2,3},{3,2},{4,5},{5,4},{6,7},{7,6},{8,9},{9,8},{10,11... | collective-permute-start | bytes 2359304 | tf_op jit(solution)/shard_map/ppermute | solution.py:641
  236.7 55.6 %collective-permute-start.36 = (bf16[2048,512]{1,0:T(8,128)(2,1)}, bf16[2048,512]{1,0:T(8,128)(2,1)}, u32[]{:S(2)}, u32[]{:S(2)}) collective-permute-start(bf16[2048,512]{1,0:T(8,128)(2,1)} %convolution_convert_fusion.3), channel_id=1, source_target_pairs={{0,2},{2,0},{1,3},{3,1},{4,6},{6,4},{5,7},{7,5},{8,10},{10,8},{9,1... | collective-permute-start | bytes 6291464 | tf_op jit(solution)/shard_map/ppermute | solution.py:641
  274.9 32.6 %collective-permute-start.38 = (bf16[512,2048]{1,0:T(8,128)(2,1)}, bf16[512,2048]{1,0:T(8,128)(2,1)}, u32[]{:S(2)}, u32[]{:S(2)}) collective-permute-start(bf16[512,2048]{1,0:T(8,128)(2,1)} %convolution_convert_fusion.1), channel_id=1, source_target_pairs={{0,2},{2,0},{1,3},{3,1},{4,6},{6,4},{5,7},{7,5},{8,10},{10,8},{9,1... | collective-permute-start | bytes 6291464 | tf_op jit(solution)/shard_map/ppermute | solution.py:641
  275.7 63.2 %collective-permute-start.40 = (bf16[1024,512]{1,0:T(8,128)(2,1)}, bf16[1024,512]{1,0:T(8,128)(2,1)}, u32[]{:S(2)}, u32[]{:S(2)}) collective-permute-start(bf16[1024,512]{1,0:T(8,128)(2,1)} %add_convert_fusion.6), channel_id=1, source_target_pairs={{0,1},{1,0},{2,3},{3,2},{4,5},{5,4},{6,7},{7,6},{8,9},{9,8},{10,11... | collective-permute-start | bytes 3145736 | tf_op jit(solution)/shard_map/ppermute | solution.py:641
  283.9 41.2 %all-to-all-start.1 = ((bf16[16,64,512]{2,1,0:T(8,128)(2,1)}), bf16[16,64,512]{2,1,0:T(8,128)(2,1)S(1)}, u32[]{:S(2)}, u32[]{:S(2)}) async-start(bf16[16,64,512]{2,1,0:T(8,128)(2,1)} %bitcast.160), calls=%async_computation.1 | async-start | bytes 2097152 | tf_op jit(solution)/shard_map/all_to_all | solution.py:1019
  292.4 62.0 %collective-permute-start.44 = (bf16[512,512]{1,0:T(8,128)(2,1)}, bf16[512,512]{1,0:T(8,128)(2,1)}, u32[]{:S(2)}, u32[]{:S(2)}) collective-permute-start(bf16[512,512]{1,0:T(8,128)(2,1)} %convolution_convert_fusion.6), channel_id=1, source_target_pairs={{0,2},{2,0},{1,3},{3,1},{4,6},{6,4},{5,7},{7,5},{8,10},{10,8},{9,1... | collective-permute-start | bytes 1572872 | tf_op jit(solution)/shard_map/ppermute | solution.py:641
  301.4 42.6 %collective-permute-start.42 = (bf16[512,2048]{1,0:T(8,128)(2,1)}, bf16[512,2048]{1,0:T(8,128)(2,1)}, u32[]{:S(2)}, u32[]{:S(2)}) collective-permute-start(bf16[512,2048]{1,0:T(8,128)(2,1)} %convolution_convert_fusion), channel_id=1, source_target_pairs={{0,2},{2,0},{1,3},{3,1},{4,6},{6,4},{5,7},{7,5},{8,10},{10,8},{9,1... | collective-permute-start | bytes 6291464 | tf_op jit(solution)/shard_map/ppermute | solution.py:641
  304.3 31.1 %collective-permute-start.41 = (bf16[1024,512]{1,0:T(8,128)(2,1)}, bf16[1024,512]{1,0:T(8,128)(2,1)}, u32[]{:S(2)}, u32[]{:S(2)}) collective-permute-start(bf16[1024,512]{1,0:T(8,128)(2,1)} %add_convert_fusion.5), channel_id=1, source_target_pairs={{0,4},{4,0},{1,5},{5,1},{2,6},{6,2},{3,7},{7,3},{8,12},{12,8},{9,1... | collective-permute-start | bytes 3145736 | tf_op jit(solution)/shard_map/ppermute | solution.py:770
  310.7 41.3 %collective-permute-start.43 = (bf16[256,2560]{1,0:T(8,128)(2,1)}, bf16[256,2560]{1,0:T(8,128)(2,1)}, u32[]{:S(2)}, u32[]{:S(2)}) collective-permute-start(bf16[256,2560]{1,0:T(8,128)(2,1)} %pad_maximum_fusion), channel_id=1, source_target_pairs={{0,1},{1,0},{2,3},{3,2},{4,5},{5,4},{6,7},{7,6},{8,9},{9,8},{10,11... | collective-permute-start | bytes 3932168 | tf_op jit(solution)/shard_map/ppermute | solution.py:641
  335.4 51.6 %collective-permute-start.46 = (bf16[256,2560]{1,0:T(8,128)(2,1)S(1)}, bf16[256,2560]{1,0:T(8,128)(2,1)}, u32[]{:S(2)}, u32[]{:S(2)}) collective-permute-start(bf16[256,2560]{1,0:T(8,128)(2,1)S(1)} %copy-done.40), channel_id=1, source_target_pairs={{0,1},{1,0},{2,3},{3,2},{4,5},{5,4},{6,7},{7,6},{8,9},{9,8},{10,11... | collective-permute-start | bytes 3932168 | tf_op jit(solution)/shard_map/ppermute | solution.py:641
  342.5 38.4 %collective-permute-start.45 = (bf16[512,512]{1,0:T(8,128)(2,1)}, bf16[512,512]{1,0:T(8,128)(2,1)S(1)}, u32[]{:S(2)}, u32[]{:S(2)}) collective-permute-start(bf16[512,512]{1,0:T(8,128)(2,1)} %dynamic-slice_bitcast_fusion.1), channel_id=1, source_target_pairs={{0,8},{8,0},{16,24},{24,16},{1,9},{9,1},{17,25},{25,17},{2,10},{10... | collective-permute-start | bytes 1572872 | tf_op jit(solution)/shard_map/ppermute | solution.py:784
  356.9 30.1 %collective-permute-start.47 = (bf16[256,2560]{1,0:T(8,128)(2,1)}, bf16[256,2560]{1,0:T(8,128)(2,1)}, u32[]{:S(2)}, u32[]{:S(2)}) collective-permute-start(bf16[256,2560]{1,0:T(8,128)(2,1)} %pad_maximum_fusion.2), channel_id=1, source_target_pairs={{0,4},{4,0},{1,5},{5,1},{2,6},{6,2},{3,7},{7,3},{8,12},{12,8},{9,1... | collective-permute-start | bytes 3932168 | tf_op jit(solution)/shard_map/ppermute | solution.py:770
  381.0 34.3 %collective-permute-start.49 = (bf16[512,512]{1,0:T(8,128)(2,1)S(1)}, bf16[512,512]{1,0:T(8,128)(2,1)S(1)}, u32[]{:S(2)}, u32[]{:S(2)}) collective-permute-start(bf16[512,512]{1,0:T(8,128)(2,1)S(1)} %fusion.22), channel_id=1, source_target_pairs={{0,16},{8,24},{16,0},{24,8},{1,17},{9,25},{17,1},{25,9},{2,18},{10... | collective-permute-start | bytes 1572872 | tf_op jit(solution)/shard_map/ppermute | solution.py:792
  417.3 37.0 %collective-permute-start.50 = (bf16[128,2560]{1,0:T(8,128)(2,1)S(1)}, bf16[128,2560]{1,0:T(8,128)(2,1)S(1)}, u32[]{:S(2)}, u32[]{:S(2)}) collective-permute-start(bf16[128,2560]{1,0:T(8,128)(2,1)S(1)} %fusion.21), channel_id=1, source_target_pairs={{0,16},{8,24},{16,0},{24,8},{1,17},{9,25},{17,1},{25,9},{2,18},{10... | collective-permute-start | bytes 1966088 | tf_op jit(solution)/shard_map/ppermute | solution.py:792
  475.9 84.7 %all-to-all-start.2 = ((bf16[16,192,512]{2,1,0:T(8,128)(2,1)}), bf16[16,192,512]{2,1,0:T(8,128)(2,1)}, u32[]{:S(2)}, u32[]{:S(2)}) async-start(bf16[16,192,512]{2,1,0:T(8,128)(2,1)} %shard_map.501.grad_ref), calls=%async_computation.2 | async-start | bytes 6291456 | tf_op jit(solution)/shard_map/all_to_all | solution.py:1058
  481.0 29.4 %collective-permute-start.56 = (bf16[128,3072]{1,0:T(8,128)(2,1)}, bf16[128,3072]{1,0:T(8,128)(2,1)}, u32[]{:S(2)}, u32[]{:S(2)}) collective-permute-start(bf16[128,3072]{1,0:T(8,128)(2,1)} %collective-permute-done.31.refs_1_), channel_id=1, source_target_pairs={{0,2},{2,0},{1,3},{3,1},{4,6},{6,4},{5,7},{7,5},{8,10},{10,8},{9,1... | collective-permute-start | bytes 2359304 | tf_op jit(solution)/shard_map/ppermute | solution.py:641
  481.5 29.0 %collective-permute-start.57 = (bf16[128,3072]{1,0:T(8,128)(2,1)}, bf16[128,3072]{1,0:T(8,128)(2,1)}, u32[]{:S(2)}, u32[]{:S(2)}) collective-permute-start(bf16[128,3072]{1,0:T(8,128)(2,1)} %collective-permute-done.34.refs_2_), channel_id=1, source_target_pairs={{0,2},{2,0},{1,3},{3,1},{4,6},{6,4},{5,7},{7,5},{8,10},{10,8},{9,1... | collective-permute-start | bytes 2359304 | tf_op jit(solution)/shard_map/ppermute | solution.py:641
  499.7 47.3 %collective-permute-start.54 = (bf16[256,2560]{1,0:T(8,128)(2,1)}, bf16[256,2560]{1,0:T(8,128)(2,1)}, u32[]{:S(2)}, u32[]{:S(2)}) collective-permute-start(bf16[256,2560]{1,0:T(8,128)(2,1)} %bitcast.42.refs_0_), channel_id=1, source_target_pairs={{0,4},{4,0},{1,5},{5,1},{2,6},{6,2},{3,7},{7,3},{8,12},{12,8},{9,1... | collective-permute-start | bytes 3932168 | tf_op jit(solution)/shard_map/ppermute | solution.py:806
  519.5 28.3 %collective-permute-start.60 = (bf16[256,2560]{1,0:T(8,128)(2,1)}, bf16[256,2560]{1,0:T(8,128)(2,1)}, u32[]{:S(2)}, u32[]{:S(2)}) collective-permute-start(bf16[256,2560]{1,0:T(8,128)(2,1)} %bitcast.42.refs_0_), channel_id=1, source_target_pairs={{0,2},{2,0},{1,3},{3,1},{4,6},{6,4},{5,7},{7,5},{8,10},{10,8},{9,1... | collective-permute-start | bytes 3932168 | tf_op jit(solution)/shard_map/ppermute | solution.py:641
  (149 other events, 1619.4 us)

commit v4 on v3

--- a/solution.py
+++ b/solution.py
@@ -17,6 +17,7 @@
 FAR = 1e30
 QB = 512
 KB = 512
+HALF = 256
 CALM_SCORE = 60.0
 FORWARD_COST = 50_000_000_000
 BACKWARD_COST = 75_000_000_000
@@ -50,6 +51,18 @@
     return low, high
 
 
+def over_keys(low, high, step, carry):
+    def whole(j, carry):
+        return step(pl.ds(pl.multiple_of((low + 2 * j) * HALF, HALF), KB), carry)
+
+    def half(j, carry):
+        return step(pl.ds(pl.multiple_of(j * HALF, HALF), HALF), carry)
+
+    pairs = (high - low) // 2
+    carry = lax.fori_loop(0, pairs, whole, carry)
+    return lax.fori_loop(low + 2 * pairs, high, half, carry)
+
+
 def split3(x):
     top = x.astype(jnp.bfloat16)
     rest = x - top.astype(jnp.float32)
@@ -62,12 +75,17 @@
     return [ref.at[:, i * HEAD_DIM : (i + 1) * HEAD_DIM, :] for i in range(ref.shape[1] // HEAD_DIM)]
 
 
-def forward_kernel(count, shift, ends_ref, base_ref, own_ref, *refs):
-    q_ref, k_ref, v_ref = parts_of(own_ref)
+def forward_kernel(count, shift, pieces, ends_ref, base_ref, *refs):
     if shift:
-        k_ref, v_ref = parts_of(refs[0])
-        refs = refs[1:]
-    o_ref, log_ref, qa, kn, va, peak = refs
+        own_ref, window_ref, o_ref, log_ref, qa, kn, va, peak = refs
+        q_ref = parts_of(own_ref)[0]
+        k_ref, v_ref = parts_of(window_ref)
+    else:
+        place_ref, *refs = refs
+        made, (o_ref, log_ref, own_ref, qa, kn, va, peak) = refs[:pieces], refs[pieces:]
+        for i in range(pieces):
+            own_ref[place_ref[i]] = made[i][...]
+        q_ref, k_ref, v_ref = parts_of(own_ref)
     peak[...] = jnp.zeros_like(peak)
     q_blocks = q_ref.shape[0]
     k_blocks = k_ref.shape[0]
@@ -103,8 +121,8 @@
     def span(i):
         first = base + i * QB
         low, high = image_span(ends_ref, count, first, first + QB - 1)
-        low = jnp.maximum(low - base + shift, 0) // KB
-        return low, jnp.minimum(high - base + shift + KB - 1, key_count) // KB
+        low = jnp.maximum(low - base + shift, 0) // HALF
+        return low, jnp.minimum(high - base + shift + HALF - 1, key_count) // HALF
 
     def finish(i, top, acc):
         total = acc[HEAD_DIM : HEAD_DIM + 1]
@@ -121,13 +139,11 @@
         def _(i):
             q_part = qa[:, pl.ds(pl.multiple_of(i * QB, QB), QB)]
 
-            def step(j, acc):
-                at = pl.ds(pl.multiple_of(j * KB, KB), KB)
+            def step(at, acc):
                 weights = jnp.exp(rows_dot(kn[at, :], q_part)).astype(jnp.bfloat16)
                 return acc + rows_dot(va[:, at], weights)
 
-            acc = lax.fori_loop(*span(i), step, jnp.zeros((HEAD_DIM + 16, QB), jnp.float32))
-            finish(i, 0.0, acc)
+            finish(i, 0.0, over_keys(*span(i), step, jnp.zeros((HEAD_DIM + 16, QB), jnp.float32)))
 
     @pl.when(jnp.logical_not(small))
     def _():
@@ -135,9 +151,8 @@
         def _(i):
             q_part = qa[:, pl.ds(pl.multiple_of(i * QB, QB), QB)]
 
-            def step(j, carry):
+            def step(at, carry):
                 top, acc = carry
-                at = pl.ds(pl.multiple_of(j * KB, KB), KB)
                 scores = rows_dot(kn[at, :], q_part)
                 new_top = jnp.maximum(top, jnp.max(scores, axis=0, keepdims=True))
                 weights = jnp.exp(scores - new_top).astype(jnp.bfloat16)
@@ -148,7 +163,7 @@
                 jnp.full((1, QB), -3e38, jnp.float32),
                 jnp.zeros((HEAD_DIM + 16, QB), jnp.float32),
             )
-            finish(i, *lax.fori_loop(*span(i), step, start))
+            finish(i, *over_keys(*span(i), step, start))
 
 
 def backward_kernel(count, shift, first_block, chunk, last, ends_ref, base_ref, own_ref, *refs):
@@ -229,18 +244,17 @@
         d_rows = dn[q_at, :]
         first = start + i * BLOCK
         key_low, key_high = image_span(ends_ref, count, first, first + BLOCK - 1)
-        key_low = jnp.maximum(key_low - base + shift, 0) // BLOCK
-        key_high = jnp.minimum(key_high - base + shift + BLOCK - 1, key_count) // BLOCK
-
-        def step(j, dq):
-            at = block_at(j)
+        key_low = jnp.maximum(key_low - base + shift, 0) // HALF
+        key_high = jnp.minimum(key_high - base + shift + HALF - 1, key_count) // HALF
+
+        def step(at, dq):
             probs = jnp.exp(rows_dot(kn[at, :], q_part))
             score_grad = (probs * rows_dot(vn[at, :], d_part)).astype(jnp.bfloat16)
             sums[at, 0:HEAD_DIM] += rows_dot(score_grad, q_rows)
             sums[at, HEAD_DIM : 2 * HEAD_DIM] += rows_dot(probs.astype(jnp.bfloat16), d_rows)
             return dq + rows_dot(ks[:, at], score_grad)
 
-        dq = lax.fori_loop(key_low, key_high, step, jnp.zeros((HEAD_DIM, BLOCK), jnp.float32))
+        dq = over_keys(key_low, key_high, step, jnp.zeros((HEAD_DIM, BLOCK), jnp.float32))
         dq_part[i] = dq.astype(jnp.bfloat16)
 
     def query_copy(i):
@@ -295,26 +309,34 @@
     return pl.BlockSpec(memory_space=pltpu.SMEM)
 
 
-def attention_forward(ends, base, own, window, shift):
-    blocks = own.shape[0]
+def attention_forward(ends, base, made, places, window, shift):
+    blocks = made[0].shape[0] if shift else len(made)
     tokens, keys = blocks * BLOCK, blocks * BLOCK + 2 * shift
-    arrays = [own] + ([window] if shift else [])
+    low = jnp.bfloat16
+    out_shape = [
+        jax.ShapeDtypeStruct((blocks, HEAD_DIM, BLOCK), low),
+        jax.ShapeDtypeStruct((1, tokens), jnp.float32),
+    ]
+    if shift:
+        arrays, in_specs = [*made, window], [smem_spec()] * 2 + [vmem_spec()] * 2
+    else:
+        arrays, in_specs = [places, *made], [smem_spec()] * 3 + [vmem_spec()] * blocks
+        out_shape.append(jax.ShapeDtypeStruct((blocks, 3 * HEAD_DIM, BLOCK), low))
     return pl.pallas_call(
-        partial(forward_kernel, ends.shape[0], shift),
-        out_shape=(
-            jax.ShapeDtypeStruct((blocks, HEAD_DIM, BLOCK), jnp.bfloat16),
-            jax.ShapeDtypeStruct((1, tokens), jnp.float32),
-        ),
-        in_specs=[smem_spec(), smem_spec()] + [vmem_spec()] * len(arrays),
-        out_specs=(vmem_spec(), vmem_spec()),
+        partial(forward_kernel, ends.shape[0], shift, blocks),
+        out_shape=out_shape,
+        in_specs=in_specs,
+        out_specs=[vmem_spec()] * len(out_shape),
         scratch_shapes=[
-            pltpu.VMEM((HEAD_DIM + 16, tokens), jnp.bfloat16),
-            pltpu.VMEM((keys, HEAD_DIM + 16), jnp.bfloat16),
-            pltpu.VMEM((HEAD_DIM + 16, keys), jnp.bfloat16),
+            pltpu.VMEM((HEAD_DIM + 16, tokens), low),
+            pltpu.VMEM((keys, HEAD_DIM + 16), low),
+            pltpu.VMEM((HEAD_DIM + 16, keys), low),
             pltpu.VMEM((8, BLOCK), jnp.float32),
         ],
         compiler_params=pltpu.CompilerParams(vmem_limit_bytes=48 * 1024 * 1024),
-        cost_estimate=pl.CostEstimate(flops=FORWARD_COST, bytes_accessed=tokens * 512, transcendentals=0),
+        cost_estimate=pl.CostEstimate(
+            flops=FORWARD_COST, bytes_accessed=tokens * 512, transcendentals=0
+        ),
     )(ends, base, *arrays)
 
 
@@ -448,73 +470,87 @@
     )(row_at, col_at, *pieces)
 
 
-def head_columns_kernel(head_ref, q_ref, k_ref, v_ref, out_ref):
-    odd = lax.rem(head_ref[0], 2) == 1
+def plane_columns_kernel(plane_ref, q_ref, k_ref, v_ref, out_ref):
     for part, ref in enumerate((q_ref, k_ref, v_ref)):
-        both = ref[...].astype(jnp.float32).T
-        mine = jnp.where(odd, both[HEAD_DIM:], both[:HEAD_DIM])
-        out_ref[part * HEAD_DIM : (part + 1) * HEAD_DIM] = mine.astype(out_ref.dtype)
-
-
-def head_columns(w, head):
-    rows, pairs = w.shape[0], HEADS // 2
+        cols = ref[...].astype(jnp.float32).T
+        for j in range(4):
+            at = (3 * j + part) * HEAD_DIM
+            out_ref[at : at + HEAD_DIM] = cols[j * HEAD_DIM : (j + 1) * HEAD_DIM].astype(out_ref.dtype)
+
+
+def plane_columns(w, plane):
+    rows = w.shape[0]
 
     def spec(part):
-        return pl.BlockSpec(
-            (rows, 2 * HEAD_DIM), lambda i, head_ref: (0, part * pairs + head_ref[0] // 2)
-        )
+        return pl.BlockSpec((rows, 4 * HEAD_DIM), lambda i, plane_ref: (0, part * (HEADS // 4) + plane_ref[0]))
 
     return pl.pallas_call(
-        head_columns_kernel,
-        out_shape=jax.ShapeDtypeStruct((3 * HEAD_DIM, rows), w.dtype),
+        plane_columns_kernel,
+        out_shape=jax.ShapeDtypeStruct((12 * HEAD_DIM, rows), w.dtype),
         grid_spec=pltpu.PrefetchScalarGridSpec(
             num_scalar_prefetch=1,
             grid=(1,),
             in_specs=[spec(part) for part in range(3)],
-            out_specs=pl.BlockSpec((3 * HEAD_DIM, rows), lambda i, head_ref: (0, 0)),
+            out_specs=pl.BlockSpec((12 * HEAD_DIM, rows), lambda i, plane_ref: (0, 0)),
         ),
-    )(head.astype(jnp.int32).reshape(1), w, w, w)
-
-
-def project_kernel(count, place_ref, w_ref, bias_ref, *refs):
-    blocks, out_ref, made, sem = refs[:count], refs[-3], refs[-2], refs[-1]
-
-    def copy(i):
-        return pltpu.make_async_copy(made.at[i], out_ref.at[place_ref[i]], sem.at[i])
-
+    )(plane.astype(jnp.int32).reshape(1), w, w, w)
+
+
+def project_kernel(head_ref, w_ref, bias_ref, block_ref, *out_refs):
     size = w_ref.shape[2]
-    for i in range(count):
-        total = bias_ref[...]
+    rows = 3 * HEAD_DIM
+    for i, out_ref in enumerate(out_refs):
+        at = pl.ds(pl.multiple_of(head_ref[i] * rows, HEAD_DIM), rows)
+        total = bias_ref[at, :]
         for f in range(w_ref.shape[0]):
             total += lax.dot_general(
-                w_ref[f], blocks[i][:, f * size : (f + 1) * size], (((1,), (1,)), ((), ())),
+                w_ref[f, at, :], block_ref[:, f * size : (f + 1) * size], (((1,), (1,)), ((), ())),
                 preferred_element_type=jnp.float32,
             )
-        made[i] = total.astype(jnp.bfloat16)
+        out_ref[...] = total.astype(jnp.bfloat16)
+
+
+def project(heads, w, bias, block):
+    rows, width = block.shape
+    count = heads.shape[0]
+    shape = jax.ShapeDtypeStruct((3 * HEAD_DIM, rows), jnp.bfloat16)
+    return pl.pallas_call(
+        project_kernel,
+        out_shape=[shape] * count,
+        in_specs=[smem_spec()] + [vmem_spec()] * 3,
+        out_specs=[vmem_spec()] * count,
+        compiler_params=pltpu.CompilerParams(vmem_limit_bytes=24 * 1024 * 1024),
+        cost_estimate=pl.CostEstimate(
+            flops=6 * count * rows * width * 3 * HEAD_DIM, bytes_accessed=rows * width * 2, transcendentals=0
+        ),
+    )(heads, w, bias, block)
+
+
+def assemble_kernel(count, place_ref, *refs):
+    pieces, out_ref, sem = refs[:count], refs[count], refs[count + 1]
+
+    def copy(i):
+        return pltpu.make_async_copy(pieces[i], out_ref.at[place_ref[i]], sem.at[i])
+
+    for i in range(count):
         copy(i).start()
     for i in range(count):
         copy(i).wait()
 
 
-def project(so_far, places, w, bias, blocks):
-    count = len(blocks)
-    rows, width = blocks[0].shape
-    cols = w.shape[1]
-    arrays = [w, bias, *blocks] + ([] if so_far is None else [so_far])
-    specs = [vmem_spec()] * (2 + count) + ([] if so_far is None else [any_spec()])
+def assemble(pieces, places):
+    count = len(pieces)
     return pl.pallas_call(
-        partial(project_kernel, count),
-        out_shape=jax.ShapeDtypeStruct((HEADS, cols, rows), jnp.bfloat16),
-        in_specs=[smem_spec()] + specs,
+        partial(assemble_kernel, count),
+        out_shape=jax.ShapeDtypeStruct((count,) + pieces[0].shape, pieces[0].dtype),
+        in_specs=[smem_spec()] + [vmem_spec()] * count,
         out_specs=any_spec(),
-        scratch_shapes=[
-            pltpu.VMEM((count, cols, rows), jnp.bfloat16),
-            pltpu.SemaphoreType.DMA((count,)),
-        ],
-        input_output_aliases={} if so_far is None else {3 + count: 0},
-        compiler_params=pltpu.CompilerParams(vmem_limit_bytes=24 * 1024 * 1024),
-        cost_estimate=pl.CostEstimate(flops=4 * count * rows * width * cols, bytes_accessed=count * rows * width * 2, transcendentals=0),
-    )(jnp.stack(places).astype(jnp.int32), *arrays)
+        scratch_shapes=[pltpu.SemaphoreType.DMA((count,))],
+        compiler_params=pltpu.CompilerParams(vmem_limit_bytes=16 * 1024 * 1024),
+        cost_estimate=pl.CostEstimate(
+            flops=0, bytes_accessed=4 * count * pieces[0].size, transcendentals=0
+        ),
+    )(places, *pieces)
 
 
 SLOTS = 4
@@ -558,7 +594,7 @@
         ],
         compiler_params=pltpu.CompilerParams(vmem_limit_bytes=24 * 1024 * 1024),
         cost_estimate=pl.CostEstimate(flops=4 * count * rows * width * cols, bytes_accessed=count * rows * width * 2, transcendentals=0),
-    )(jnp.stack(places).astype(jnp.int32), grad, *blocks)
+    )(places, grad, *blocks)
 
 
 def weave_kernel(count, at_ref, *refs):
@@ -750,6 +786,7 @@
             self.joined([self.term(n, core, f) + self.got[f][n].astype(jnp.float32) for n in count])
             for f in range(parts)
         ]
+        self.far = []
         self.total = lax.psum_scatter(jnp.stack(total), "f", scatter_dimension=0, tiled=False)
         return self.total
 
@@ -885,38 +922,35 @@
     return table
 
 
-def gather_group(x, use, beside):
-    z, y, c = (lax.axis_index(axis) for axis in SEQ)
+def gather_planes(x, use, beside, later):
+    z = lax.axis_index("z")
     count = lax.axis_size("z")
     table = arrivals(count)
     up, down = x, x
     hops = {}
-    block, plane = x, z
-    state, items = None, []
-    for t in range(1, count + 1):
-        first = plane * 4
-        if t < count:
-            up = lax.ppermute(up, "z", [(i, i + 1) for i in range(t - 1, count - 1)])
-            down = lax.ppermute(down, "z", [(i, i - 1) for i in range(1, count - t + 1)])
-        near = swap(block, "y")
-        items += [(block, first + 2 * y + c), (swap(block, "c"), first + 2 * y + 1 - c)]
-        across, places = zip(*items)
-        across = lax.optimization_barrier(across)
-        state = use(state, across, places)
-        up, down, near, state, _ = lax.optimization_barrier(
-            (up, down, near, state, beside[t - 1] if t <= len(beside) else [])
+    blocks, planes, used = [x], [z], []
+    for t in range(1, count):
+        up = lax.ppermute(up, "z", [(i, i + 1) for i in range(t - 1, count - 1)])
+        down = lax.ppermute(down, "z", [(i, i - 1) for i in range(1, count - t + 1)])
+        made = use(blocks[-1])
+        before = used.pop() if used else []
+        up, down, before, made[0], extra, _ = lax.optimization_barrier(
+            (up, down, before, made[0], later[t - 1](blocks), beside[t - 1])
         )
-        items = [(near, first + 2 * (1 - y) + c), (swap(near, "c"), first + 2 * (1 - y) + 1 - c)]
-        if t < count:
-            hops["up", t], hops["down", t] = up, down
-            names = sorted({table[i][t - 1] for i in range(count)})
-            block, plane = None, z
-            for name in names:
-                here = [i for i in range(count) if table[i][t - 1] == name]
-                chosen = (z >= here[0]) & (z <= here[-1])
-                block = hops[name] if block is None else jnp.where(chosen, hops[name], block)
-                plane = jnp.where(chosen, z + (-name[1] if name[0] == "up" else name[1]), plane)
-    return use(state, *zip(*items))
+        later[t - 1](blocks, extra)
+        used += [before] * (t > 1) + [made]
+        hops["up", t], hops["down", t] = up, down
+        names = sorted({table[i][t - 1] for i in range(count)})
+        block, plane = None, z
+        for name in names:
+            here = [i for i in range(count) if table[i][t - 1] == name]
+            chosen = (z >= here[0]) & (z <= here[-1])
+            block = hops[name] if block is None else jnp.where(chosen, hops[name], block)
+            plane = jnp.where(chosen, z + (-name[1] if name[0] == "up" else name[1]), plane)
+        blocks.append(block)
+        planes.append(plane)
+    used.append(use(blocks[-1]))
+    return blocks, planes, used
 
 
 def body(
@@ -940,30 +974,48 @@
     normed = normed_pre.astype(low)
 
     shard_rows = w_qkv.shape[0]
-    head_full = join_small(head_columns(w_qkv, head)).reshape(parts, 3 * HEAD_DIM, shard_rows)
-    head_bias = jnp.concatenate(
-        [
-            lax.dynamic_slice_in_dim(qv_bias, head * HEAD_DIM, HEAD_DIM),
-            jnp.zeros((HEAD_DIM,), f32),
-            lax.dynamic_slice_in_dim(qv_bias, width + head * HEAD_DIM, HEAD_DIM),
+    z, y, c = (lax.axis_index(axis) for axis in SEQ)
+    place_in_plane = 2 * y + c
+    plane_weights = join_small(plane_columns(tie(w_qkv, gain_one, bias_one, qv_bias), z)).reshape(parts, 12 * HEAD_DIM, shard_rows)
+    q_bias, v_bias = (
+        lax.dynamic_slice_in_dim(qv_bias, at + z * 4 * HEAD_DIM, 4 * HEAD_DIM).reshape(4, HEAD_DIM)
+        for at in (0, width)
+    )
+    plane_bias = jnp.concatenate([q_bias, jnp.zeros((4, HEAD_DIM), f32), v_bias], axis=1).reshape(-1, 1)
+    others = jnp.array([0, 1, 2, 3], jnp.int32)
+    heads_made = others ^ place_in_plane
+
+    def heads_of(block):
+        own, core, near, far = project(heads_made, plane_weights, plane_bias, block)
+        return [
+            own, swap(core, "c"), swap(near, "y"),
+            lax.ppermute(far, ("y", "c"), [(i, 3 - i) for i in range(4)]),
         ]
-    )[:, None]
-
-    normed = tie(normed, head_bias, head_full)
-    kept_blocks, kept_places = [], []
-
-    def add_blocks(qkv, blocks, places):
-        kept_blocks.extend(blocks)
-        kept_places.extend(places)
-        return project(qkv, places, head_full, head_bias, blocks)
 
     out_taken, out_part = fetch_fsdp(w_out, 1, normed)
     fc1_taken, fc1_part = fetch_fsdp(w_fc1, 2, normed)
     fc2_taken, fc2_part = fetch_fsdp(w_fc2, 2, normed)
     qkv_taken, qkv_part = fetch_fsdp(w_qkv, 2, normed)
     out_full = join_fsdp(w_out, share_cores(out_part))
-    beside = [out_part + out_taken + fc1_taken + fc2_taken + qkv_taken, [], fc1_part[:1], fc1_part[1:] + [out_full]]
-    qkv = gather_group(normed, add_blocks, beside)
+    beside = [
+        out_taken + fc1_taken + fc2_taken + qkv_taken, out_part, fc1_part[:1] + [out_full],
+    ]
+    near_blocks = []
+
+    def swap_later(first):
+        def step(blocks, done=None):
+            if done is None:
+                return [swap(blocks[first], "y")] if first is not None else []
+            near_blocks.extend(done)
+
+        return step
+
+    later = [swap_later(None), swap_later(0), swap_later(1)]
+    blocks, planes, made = gather_planes(normed, heads_of, beside, later)
+    blocks_at = jnp.concatenate([plane * 4 + heads_made for plane in planes])
+    made = [piece for round_made in made for piece in round_made]
+    if groups > 1:
+        qkv = assemble(made, blocks_at)
     ends = jnp.cumsum(lengths[0]).astype(jnp.int32)
     base = (group * (rows * HEADS)).astype(jnp.int32).reshape(1)
     shift, window = 0, None
@@ -976,9 +1028,12 @@
         before = lax.ppermute(both[HEADS - margin :], "g", up)
         after = lax.ppermute(both[:margin], "g", down)
         window = jnp.concatenate([before, both, after], axis=0)
-    attended, log_total = attention_forward(
-        ends, base, qkv, window, shift
-    )
+    if groups > 1:
+        attended, log_total = attention_forward(ends, base, [qkv], None, window, shift)
+    else:
+        attended, log_total, qkv = attention_forward(ends, base, made, blocks_at, None, 0)
+    attended, near_last = lax.optimization_barrier((attended, swap(blocks[2], "y")))
+    near_blocks.append(near_last)
     fc2_part = share_cores(fc2_part, attended)
     fc1_full = join_fsdp(w_fc1, share_cores(fc1_part), attended)
     fc2_full = join_fsdp(w_fc2, fc2_part, attended)
@@ -1008,7 +1063,8 @@
     token = fc2_sum.other_core()
     active_grad = dot(tie(out_cot, token), fc2_full, 1, 1)
     inner_grad = gelu_pull(active_grad)[0].astype(low)
-    token = fc2_sum.other_f(inner_grad)
+    near_blocks.append(swap(tie(blocks[3], fc2_full), "y"))
+    token = fc2_sum.other_f(inner_grad, near_blocks[3])
     norm_two_grad = dot(tie(inner_grad, token), fc1_full, 1, 1)
     gain_two_grad, bias_two_grad, middle_from_norm = norm_backward(
         norm_two_grad, scaled_two, inv_two, gain_two
@@ -1022,9 +1078,10 @@
     rest_sum = WeightSum([(normed_two, inner_grad, 0), (mixed, branch_grad, 1)], scale)
     token = rest_sum.other_core(mixed_grad)
     token = fc2_sum.near_y(token)
-    token = rest_sum.other_f(token)
-    block_out = middle + (dot(tie(active_low, token), fc2_full, 1, 0) + fc2_bias)
-    tokens = [block_out]
+    token = rest_sum.other_f(token, *fc2_sum.far[1:])
+    column = list(blocks)
+    across = [swap(tie(block, mixed_grad), "c") for block in column + near_blocks]
+    tokens = [token] + across
 
     plan = [
         [fc2_sum.near_z, rest_sum.near_y],
@@ -1057,7 +1114,11 @@
         head_grad = jnp.concatenate([head_grad, inner.astype(low)], axis=1)
     token_grad = lax.all_to_all(tie(head_grad, *tokens), SEQ, 0, 0, tiled=True)
 
-    weight_part = head_weight(kept_places, head_grad, kept_blocks)
+    weight_part = head_weight(
+        jnp.concatenate([jnp.stack(planes) * 4 + (place_in_plane ^ k) for k in (0, 2, 1, 3)]).astype(jnp.int32),
+        head_grad,
+        column + near_blocks + across,
+    )
     weight_part = weight_part.reshape(3 * HEAD_DIM, parts, shard_rows).transpose(1, 0, 2)
     if parts == 2:
         weight_part = halve(weight_part, "f")
@@ -1071,7 +1132,7 @@
     (fc2_grad,) = fc2_sum.results(qkv_full)
     fc1_grad, out_weight_grad = rest_sum.results(fc2_grad)
     token_grad = tie(token_grad, fc1_grad, out_weight_grad)
-    z, y, c = (lax.axis_index(axis) for axis in SEQ)
+    block_out = middle + (dot(tie(active_low, weight_part), fc2_full, 1, 0) + fc2_bias)
     hops = [weight_part] + [
         lax.ppermute(weight_part, "z", [(i, (i + k) % 4) for i in range(4)]) for k in range(1, 4)
     ]
@@ -1112,8 +1173,8 @@
     token = late.near_y(token)
     token = late.near_z(token)
     late.far_z(token)
-    planes = lax.rem(z + 4 - jnp.arange(4, dtype=jnp.int32), 4) * 4
-    near_places = [planes + 2 * y + c, planes + 2 * (1 - y) + c]
+    firsts = lax.rem(z + 4 - jnp.arange(4, dtype=jnp.int32), 4) * 4
+    near_places = [firsts + 2 * y + c, firsts + 2 * (1 - y) + c]
     places = jnp.concatenate(near_places + [place_at + 1 - 2 * c for place_at in near_places])
     qkv_weight_grad = weave(pieces, places)
     late.result()

time: 636 us -> 631 us (level)
  waiting for transfers between devices: 148 us -> 126 us
  starting transfers between devices: 86.1 us -> 104 us
  Pallas kernels: 231 us -> 220 us
    ppermute x2, waiting for transfers between devices: 3.52 us -> 14.6 us  [near_y(): self.coming = lax.ppermute(sent, 'y', SWAP)]
    ppermute x3, waiting for transfers between devices: 10.8 us -> 0.01 us  [body(): lax.ppermute(weight_part, 'z', [(i, (i + k) % 4) for i in range(4)])]
    pallas_call x7 -> x6, Pallas kernels: 59.5 us -> 49.4 us  [the longest x1 37.7 us: attention_forward(): pl.pallas_call(partial(forward_kernel, ends.shape[0], shift, blocks), out...]
    ppermute x59 -> x67, starting transfers between devices: 32.9 us -> 40.8 us  [swap(): return lax.ppermute(x, axis, SWAP)]
    ppermute x2, waiting for transfers between devices: 26.8 us -> 19 us  [back_y(): self.near = lax.ppermute(x, 'y', SWAP)]
    unnamed x196 -> x242, local copies, waits for them, and re-layouts: 21.1 us -> 27.3 us
    ppermute x59 -> x67, waiting for transfers between devices: 71.7 us -> 66.6 us  [swap(): return lax.ppermute(x, axis, SWAP)]
    ppermute x6 -> x10, starting transfers between devices: 11.6 us -> 13.4 us  [the longest x3 7.83 us: gather_planes(): up = lax.ppermute(up, 'z', [(i, i + 1) for i in range(t - 1, count - 1)])]
  transfers between devices with their start and end apart: 85 -> 97, of which waited for: 30 -> 30; matrix products, arithmetic and copies ran while one was open for 19% -> 20% of each run, Pallas kernels for 36% -> 34%
where the time goes in v4:
time: 631 us; the launch traced here: 618 us
  Pallas kernels  220 us (35%)
  waiting for transfers between devices  126 us (20%)
  starting transfers between devices  104 us (16%)
  matrix products  95.3 us (15%)
  local copies, waits for them, and re-layouts  38.6 us (6%)
  other arithmetic  31.6 us (5%)
    dot_general x25, matrix products, dot(): lax.dot_general(a, b, (((a_dim,), (b_dim,)), ((), ())), preferred_element...  95.3 us
    pallas_call x6, Pallas kernels, attention_backward(): pl.pallas_call(partial(backward_kernel, ends.shape[0], shift, first_block...  94.1 us
    ppermute x67, waiting for transfers between devices, swap(): return lax.ppermute(x, axis, SWAP)  66.6 us
    pallas_call x7, Pallas kernels, place(): pl.pallas_call(partial(place_kernel, owner), out_shape=jax.ShapeDtypeStru...  46.8 us
    ppermute x67, starting transfers between devices, swap(): return lax.ppermute(x, axis, SWAP)  40.8 us
    pallas_call x1, Pallas kernels, attention_forward(): pl.pallas_call(partial(forward_kernel, ends.shape[0], shift, blocks), out...  37.7 us
    unnamed x242, local copies, waits for them, and re-layouts  27.3 us
    ppermute x2, waiting for transfers between devices, back_y(): self.near = lax.ppermute(x, 'y', SWAP)  19 us
  transfers between devices with their start and end apart: 97, of which 30 were waited for; matrix products, arithmetic and copies ran while one was open for 20% of the time, Pallas kernels for 34%

profile of v4, /device:TPU:0, one launch (start us, length us, event | category | flops | bytes accessed | tf_op | source)
XLA Modules:
  0.0 618.3 jit_solution(17007723370006820221)
XLA Ops:
  48.6 10.0 %collective-permute-done.9.refs_3_ = bf16[192,512]{1,0:T(8,128)(2,1)S(1)} collective-permute-done((bf16[192,512]{1,0:T(8,128)(2,1)}, bf16[192,512]{1,0:T(8,128)(2,1)S(1)}, u32[]{:S(2)}, u32[]{:S(2)}) %collective-permute-start.9) | collective-permute-done | bytes 196640 | tf_op jit(solution)/shard_map/ppermute | solution.py:677
  86.5 16.4 %collective-permute-done.16.refs_7_ = bf16[192,512]{1,0:T(8,128)(2,1)S(1)} collective-permute-done((bf16[192,512]{1,0:T(8,128)(2,1)S(1)}, bf16[192,512]{1,0:T(8,128)(2,1)S(1)}, u32[]{:S(2)}, u32[]{:S(2)}) %collective-permute-start.16) | collective-permute-done | bytes 196640 | tf_op jit(solution)/shard_map/ppermute | solution.py:677
  125.2 37.7 %shard_map.501 = (bf16[16,64,512]{2,1,0:T(8,128)(2,1)}, f32[1,8192]{1,0:T(1,128)S(1)}, bf16[16,192,512]{2,1,0:T(8,128)(2,1)}) custom-call(s32[8]{0:T(128)S(1)} %bitcast.117, s32[1]{0:T(128)} %constant.119.clone.1.base_ref, s32[16]{0:T(128)S(1)} %pad_add_fusion.refs_0_, bf16[192,512]{1,0:T(8,128)(2,1)S(1)} %copy-done.32, ...), custom_call_target="tpu_custom_call" | custom-call | flops 49999998976 | bytes 4194304 | tf_op jit(solution)/shard_map/pallas_call | solution.py:325
  163.7 6.9 %all-to-all-start = ((bf16[16,64,512]{2,1,0:T(8,128)(2,1)}), bf16[16,64,512]{2,1,0:T(8,128)(2,1)}, u32[]{:S(2)}, u32[]{:S(2)}) async-start(bf16[16,64,512]{2,1,0:T(8,128)(2,1)} %get-tuple-element.182.refs_0_), calls=%async_computation | async-start | bytes 2097152 | tf_op jit(solution)/shard_map/all_to_all | solution.py:1048
  174.4 9.5 %collective-permute-done.34.refs_2_ = bf16[128,4096]{1,0:T(8,128)(2,1)S(1)} collective-permute-done((bf16[128,4096]{1,0:T(8,128)(2,1)}, bf16[128,4096]{1,0:T(8,128)(2,1)S(1)}, u32[]{:S(2)}, u32[]{:S(2)}) %collective-permute-start.34) | collective-permute-done | bytes 1048608 | tf_op jit(solution)/shard_map/ppermute | solution.py:677
  188.5 8.9 %shard_map.503 = bf16[1024,4096]{1,0:T(8,128)(2,1)} custom-call(s32[8]{0:T(128)} %multiply_add_fusion.2.row_ref, s32[8]{0:T(128)} %broadcast_17_col_ref.2.col_ref, bf16[512,4096]{1,0:T(8,128)(2,1)} %refs_0_.3, bf16[128,4096]{1,0:T(8,128)(2,1)} %collective-permute-done.19.refs_1_, bf16[128,4096]{1,0:T(8,128)(2,1)} %copy-done.63, ...), custom_call_target="tpu_custom_call" | custom-call | bytes 16777216 | tf_op jit(solution)/shard_map/pallas_call | solution.py:454
  197.4 9.2 %shard_map.502 = bf16[4096,1024]{1,0:T(8,128)(2,1)} custom-call(s32[8]{0:T(128)} %multiply_add_fusion.2.row_ref, s32[8]{0:T(128)} %broadcast_17_col_ref.2.col_ref, bf16[2048,1024]{1,0:T(8,128)(2,1)} %refs_0_.2, bf16[512,1024]{1,0:T(8,128)(2,1)} %collective-permute-done.29.refs_1_, bf16[512,1024]{1,0:T(8,128)(2,1)} %collective-permute-done.30.refs_2_, ...), custom_call_target="tpu_custom_call" | custom-call | bytes 16777216 | tf_op jit(solution)/shard_map/pallas_call | solution.py:454
  215.5 8.5 %multiply_convert_fusion = (bf16[512,4096]{1,0:T(8,128)(2,1)S(1)}, f32[512,4096]{1,0:T(8,128)}) fusion(f32[4096]{0:T(1024)S(1)} %bitcast.154, bf16[512,1024]{1,0:T(8,128)(2,1)S(1)} %add_convert_fusion.8, bf16[1024,4096]{1,0:T(8,128)(2,1)S(1)} %copy-done.56), kind=kOutput, calls=%fused_computation.10 | convolution fusion | flops 4315938816 | bytes 22036480 | tf_op jit(solution)/shard_map/dot_general | solution.py:657
  230.5 12.5 %convert_reduce_fusion = (f32[4096]{0:T(1024)S(1)}, bf16[512,4096]{1,0:T(8,128)(2,1)S(1)}) fusion(f32[512,4096]{1,0:T(8,128)} %get-tuple-element.314, f32[4096]{0:T(1024)S(1)} %bitcast.155, bf16[512,1024]{1,0:T(8,128)(2,1)S(1)} %bitcast.130, bf16[4096,1024]{1,0:T(8,128)(2,1)S(1)} %bitcast.125), kind=kOutput, calls=%fused_computation.9 | convolution fusion | flops 4343197696 | bytes 22052864 | tf_op jit(solution)/shard_map/dot_general | solution.py:657
  251.7 7.6 %multiply_reduce_fusion = (f32[1024]{0:T(1024)S(1)}, f32[512]{0:T(512)S(1)}, f32[512]{0:T(512)S(1)}, f32[1024]{0:T(1024)S(1)}, f32[512,1024]{1,0:T(8,128)S(1)}) fusion(f32[512,1024]{1,0:T(8,128)S(1)} %get-tuple-element.292, f32[512]{0:T(512)S(1)} %add_rsqrt_fusion, f32[512]{0:T(512)S(1)} %broadcast_multiply_fusion.5, f32[1024]{0:T(1024)S(1)} %bitcast.149, ...), kind=kOutput, calls=%fused_computation.22 | convolution fusion | flops 4299682816 | bytes 16797696 | tf_op jit(solution)/shard_map/dot_general | solution.py:657
  273.3 7.0 %all-to-all-start.1 = ((bf16[16,64,512]{2,1,0:T(8,128)(2,1)}), bf16[16,64,512]{2,1,0:T(8,128)(2,1)}, u32[]{:S(2)}, u32[]{:S(2)}) async-start(bf16[16,64,512]{2,1,0:T(8,128)(2,1)} %bitcast.139), calls=%async_computation.1 | async-start | bytes 2097152 | tf_op jit(solution)/shard_map/all_to_all | solution.py:1075
  313.9 12.1 %shard_map.504 = (bf16[16,192,512]{2,1,0:T(8,128)(2,1)}, f32[8192,128]{1,0:T(8,128)}) custom-call(s32[8]{0:T(128)S(1)} %bitcast.118, s32[1]{0:T(128)} %constant.119.clone.1.base_ref, bf16[16,192,512]{2,1,0:T(8,128)(2,1)} %get-tuple-element.216.own_ref, bf16[16,64,512]{2,1,0:T(8,128)(2,1)} %get-tuple-element.182.refs_0_, ...), custom_call_target="tpu_custom_call" | custom-call | flops 9374999552 | bytes 1048576 | tf_op jit(solution)/shard_map/pallas_call | solution.py:384
  347.9 15.6 %shard_map.505 = (bf16[16,192,512]{2,1,0:T(8,128)(2,1)}, f32[8192,128]{1,0:T(8,128)}) custom-call(s32[8]{0:T(128)S(1)} %bitcast.119, s32[1]{0:T(128)} %constant.119.clone.1.base_ref, bf16[16,192,512]{2,1,0:T(8,128)(2,1)} %get-tuple-element.216.own_ref, ...), custom_call_target="tpu_custom_call", output_to_operand_aliasing={{0}: (7, {}), {1}: (6, {})} | custom-call | flops 14062499840 | bytes 1572864 | tf_op jit(solution)/shard_map/pallas_call | solution.py:384
  366.3 10.6 %collective-permute-done.59 = bf16[256,2560]{1,0:T(8,128)(2,1)S(1)} collective-permute-done((bf16[256,2560]{1,0:T(8,128)(2,1)S(1)}, bf16[256,2560]{1,0:T(8,128)(2,1)S(1)}, u32[]{:S(2)}, u32[]{:S(2)}) %collective-permute-start.59) | collective-permute-done | bytes 1310752 | tf_op jit(solution)/shard_map/ppermute | solution.py:807
  383.5 17.3 %shard_map.506 = (bf16[16,192,512]{2,1,0:T(8,128)(2,1)}, f32[8192,128]{1,0:T(8,128)}) custom-call(s32[8]{0:T(128)S(1)} %bitcast.120, s32[1]{0:T(128)} %constant.119.clone.1.base_ref, bf16[16,192,512]{2,1,0:T(8,128)(2,1)} %get-tuple-element.216.own_ref, ...), custom_call_target="tpu_custom_call", output_to_operand_aliasing={{0}: (7, {}), {1}: (6, {})} | custom-call | flops 14062499840 | bytes 1572864 | tf_op jit(solution)/shard_map/pallas_call | solution.py:384
  404.7 17.3 %shard_map.507 = (bf16[16,192,512]{2,1,0:T(8,128)(2,1)}, f32[8192,128]{1,0:T(8,128)}) custom-call(s32[8]{0:T(128)S(1)} %bitcast.121, s32[1]{0:T(128)} %constant.119.clone.1.base_ref, bf16[16,192,512]{2,1,0:T(8,128)(2,1)} %get-tuple-element.216.own_ref, ...), custom_call_target="tpu_custom_call", output_to_operand_aliasing={{0}: (7, {}), {1}: (6, {})} | custom-call | flops 14062499840 | bytes 1572864 | tf_op jit(solution)/shard_map/pallas_call | solution.py:384
  425.0 17.7 %shard_map.508 = (bf16[16,192,512]{2,1,0:T(8,128)(2,1)}, f32[8192,128]{1,0:T(8,128)}) custom-call(s32[8]{0:T(128)S(1)} %bitcast.122, s32[1]{0:T(128)} %constant.119.clone.1.base_ref, bf16[16,192,512]{2,1,0:T(8,128)(2,1)} %get-tuple-element.216.own_ref, ...), custom_call_target="tpu_custom_call", output_to_operand_aliasing={{0}: (7, {}), {1}: (6, {})} | custom-call | flops 14062499840 | bytes 1572864 | tf_op jit(solution)/shard_map/pallas_call | solution.py:384
  448.0 14.2 %shard_map.509.grad_ref = bf16[16,192,512]{2,1,0:T(8,128)(2,1)} custom-call(s32[8]{0:T(128)S(1)} %bitcast.123, s32[1]{0:T(128)} %constant.119.clone.1.base_ref, bf16[16,192,512]{2,1,0:T(8,128)(2,1)} %get-tuple-element.216.own_ref, bf16[16,64,512]{2,1,0:T(8,128)(2,1)} %get-tuple-element.182.refs_0_, ...), custom_call_target="tpu_custom_call", output_to_operand_aliasing={{}: (7, {})} | custom-call | flops 9374999552 | bytes 1048576 | tf_op jit(solution)/shard_map/pallas_call | solution.py:384
  480.2 8.8 %shard_map.510 = f32[192,1024]{1,0:T(8,128)S(1)} custom-call(s32[16]{0:T(128)S(1)} %pad_add_fusion.1.place_ref, bf16[16,192,512]{2,1,0:T(8,128)(2,1)S(1)} %copy-done, bf16[512,1024]{1,0:T(8,128)(2,1)S(1)} %copy-done.5, bf16[512,1024]{1,0:T(8,128)(2,1)} %broadcast_select_fusion.block_ref.refs_1_, bf16[512,1024]{1,0:T(8,128)(2,1)S(1)} %copy-done.2, ...), custom_call_target="tpu_custom_call" | custom-call | flops 6442450944 | bytes 16777216 | tf_op jit(solution)/shard_map/pallas_call | solution.py:586
  499.4 7.8 %collective-permute-done.65 = f32[192,512]{1,0:T(8,128)S(1)} collective-permute-done((f32[192,512]{1,0:T(8,128)S(1)}, f32[192,512]{1,0:T(8,128)S(1)}, u32[]{:S(2)}, u32[]{:S(2)}) %collective-permute-start.65) | collective-permute-done | bytes 393248 | tf_op jit(solution)/shard_map/ppermute | solution.py:726
  507.3 8.0 %shard_map.511 = bf16[1024,3072]{1,0:T(8,128)(2,1)} custom-call(s32[8]{0:T(128)} %multiply_add_fusion.2.row_ref, s32[8]{0:T(128)} %broadcast_17_col_ref.2.col_ref, bf16[512,3072]{1,0:T(8,128)(2,1)} %refs_0_.4, bf16[128,3072]{1,0:T(8,128)(2,1)} %collective-permute-done.33.refs_1_, bf16[128,3072]{1,0:T(8,128)(2,1)} %collective-permute-done.37.refs_2_, ...), custom_call_target="tpu_custom_call" | custom-call | bytes 12582912 | tf_op jit(solution)/shard_map/pallas_call | solution.py:454
  524.8 15.6 %collective-permute-done.67.refs_1_ = bf16[256,2560]{1,0:T(8,128)(2,1)} collective-permute-done((bf16[256,2560]{1,0:T(8,128)(2,1)}, bf16[256,2560]{1,0:T(8,128)(2,1)}, u32[]{:S(2)}, u32[]{:S(2)}) %collective-permute-start.67) | collective-permute-done | bytes 1310752 | tf_op jit(solution)/shard_map/ppermute | solution.py:843
  556.6 9.1 %multiply_reduce_fusion.1 = (f32[1024]{0:T(1024)S(1)}, f32[512]{0:T(512)}, f32[512]{0:T(512)S(1)}, f32[1024]{0:T(1024)S(1)}, f32[512,1024]{1,0:T(8,128)}) fusion(f32[512]{0:T(512)S(1)} %copy-done.89, f32[512]{0:T(512)S(1)} %copy-done.87, bf16[1,512,1024]{2,1,0:T(8,128)(2,1)S(1)} %copy-done.44, bf16[1,512,1024]{2,1,0:T(8,128)(2,1)S(1)} %copy-done.47, ...), kind=kOutput, calls=%fused_computation.24 | convolution fusion | flops 3227513856 | bytes 13651968 | tf_op jit(solution)/shard_map/dot_general | solution.py:657
  579.2 10.3 %fusion.21 = bf16[1,512,1024]{2,1,0:T(8,128)(2,1)} fusion(f32[512,1024]{1,0:T(8,128)S(1)} %copy-done.41, bf16[512,4096]{1,0:T(8,128)(2,1)} %copy-done.65, bf16[4096,1024]{1,0:T(8,128)(2,1)} %shard_map.502, f32[1024]{0:T(1024)S(1)} %bitcast.157), kind=kOutput, calls=%fused_computation.60 | convolution fusion | flops 4296540160 | bytes 15732736 | tf_op jit(solution)/shard_map/dot_general | solution.py:657
  (566 shorter events, 317.0 us)
Async XLA Ops:
  31.5 40.2 %collective-permute-start.11 = (bf16[512,1024]{1,0:T(8,128)(2,1)S(1)}, bf16[512,1024]{1,0:T(8,128)(2,1)}, u32[]{:S(2)}, u32[]{:S(2)}) collective-permute-start(bf16[512,1024]{1,0:T(8,128)(2,1)S(1)} %add_convert_fusion.9.block_ref.refs_0_), channel_id=1, source_target_pairs={{0,4},{4,0},{1,5},{5,1},{2,6},{6,2},{3,7},{7,3},{8,12},{12,8},{9,1... | collective-permute-start | bytes 3145736 | tf_op jit(solution)/shard_map/ppermute | solution.py:677
  47.1 35.6 %collective-permute-start.19 = (bf16[128,4096]{1,0:T(8,128)(2,1)}, bf16[128,4096]{1,0:T(8,128)(2,1)}, u32[]{:S(2)}, u32[]{:S(2)}) collective-permute-start(bf16[128,4096]{1,0:T(8,128)(2,1)} %shard_map.491), channel_id=1, source_target_pairs={{0,1},{1,0},{2,3},{3,2},{4,5},{5,4},{6,7},{7,6},{8,9},{9,8},{10,11... | collective-permute-start | bytes 3145736 | tf_op jit(solution)/shard_map/ppermute | solution.py:677
  72.4 34.2 %collective-permute-start.18 = (bf16[512,1024]{1,0:T(8,128)(2,1)}, bf16[512,1024]{1,0:T(8,128)(2,1)}, u32[]{:S(2)}, u32[]{:S(2)}) collective-permute-start(bf16[512,1024]{1,0:T(8,128)(2,1)} %broadcast_select_fusion.block_ref.refs_1_), channel_id=1, source_target_pairs={{0,4},{4,0},{1,5},{5,1},{2,6},{6,2},{3,7},{7,3},{8,12},{12,8},{9,1... | collective-permute-start | bytes 3145736 | tf_op jit(solution)/shard_map/ppermute | solution.py:677
  72.8 34.7 %collective-permute-start.13 = (bf16[512,1024]{1,0:T(8,128)(2,1)}, bf16[512,1024]{1,0:T(8,128)(2,1)}, u32[]{:S(2)}, u32[]{:S(2)}) collective-permute-start(bf16[512,1024]{1,0:T(8,128)(2,1)} %collective-permute-done.6), channel_id=1, source_target_pairs={{16,24},{17,25},{18,26},{19,27},{20,28},{21,29},{22,30},{23,31}} | collective-permute-start | bytes 3145736 | tf_op jit(solution)/shard_map/ppermute | solution.py:933
  74.4 33.1 %collective-permute-start.14 = (bf16[512,1024]{1,0:T(8,128)(2,1)}, bf16[512,1024]{1,0:T(8,128)(2,1)}, u32[]{:S(2)}, u32[]{:S(2)}) collective-permute-start(bf16[512,1024]{1,0:T(8,128)(2,1)} %collective-permute-done.7), channel_id=1, source_target_pairs={{8,0},{9,1},{10,2},{11,3},{12,4},{13,5},{14,6},{15,7}} | collective-permute-start | bytes 3145736 | tf_op jit(solution)/shard_map/ppermute | solution.py:934
  113.3 70.6 %collective-permute-start.29 = (bf16[512,1024]{1,0:T(8,128)(2,1)}, bf16[512,1024]{1,0:T(8,128)(2,1)}, u32[]{:S(2)}, u32[]{:S(2)}) collective-permute-start(bf16[512,1024]{1,0:T(8,128)(2,1)} %shard_map.493), channel_id=1, source_target_pairs={{0,1},{1,0},{2,3},{3,2},{4,5},{5,4},{6,7},{7,6},{8,9},{9,8},{10,11... | collective-permute-start | bytes 3145736 | tf_op jit(solution)/shard_map/ppermute | solution.py:677
  116.8 67.6 %collective-permute-start.30 = (bf16[512,1024]{1,0:T(8,128)(2,1)}, bf16[512,1024]{1,0:T(8,128)(2,1)}, u32[]{:S(2)}, u32[]{:S(2)}) collective-permute-start(bf16[512,1024]{1,0:T(8,128)(2,1)} %shard_map.494), channel_id=1, source_target_pairs={{0,1},{1,0},{2,3},{3,2},{4,5},{5,4},{6,7},{7,6},{8,9},{9,8},{10,11... | collective-permute-start | bytes 3145736 | tf_op jit(solution)/shard_map/ppermute | solution.py:677
  118.3 65.6 %collective-permute-start.34 = (bf16[128,4096]{1,0:T(8,128)(2,1)}, bf16[128,4096]{1,0:T(8,128)(2,1)S(1)}, u32[]{:S(2)}, u32[]{:S(2)}) collective-permute-start(bf16[128,4096]{1,0:T(8,128)(2,1)} %shard_map.492), channel_id=1, source_target_pairs={{0,1},{1,0},{2,3},{3,2},{4,5},{5,4},{6,7},{7,6},{8,9},{9,8},{10,11... | collective-permute-start | bytes 3145736 | tf_op jit(solution)/shard_map/ppermute | solution.py:677
  121.7 41.9 %collective-permute-start.27 = (bf16[512,1024]{1,0:T(8,128)(2,1)S(1)}, bf16[512,1024]{1,0:T(8,128)(2,1)S(1)}, u32[]{:S(2)}, u32[]{:S(2)}) collective-permute-start(bf16[512,1024]{1,0:T(8,128)(2,1)S(1)} %select_select_fusion.1.block_ref.refs_2_), channel_id=1, source_target_pairs={{0,4},{4,0},{1,5},{5,1},{2,6},{6,2},{3,7},{7,3},{8,12},{12,8},{9,1... | collective-permute-start | bytes 3145736 | tf_op jit(solution)/shard_map/ppermute | solution.py:677
  163.7 44.0 %all-to-all-start = ((bf16[16,64,512]{2,1,0:T(8,128)(2,1)}), bf16[16,64,512]{2,1,0:T(8,128)(2,1)}, u32[]{:S(2)}, u32[]{:S(2)}) async-start(bf16[16,64,512]{2,1,0:T(8,128)(2,1)} %get-tuple-element.182.refs_0_), calls=%async_computation | async-start | bytes 2097152 | tf_op jit(solution)/shard_map/all_to_all | solution.py:1048
  187.4 36.7 %collective-permute-start.37 = (bf16[128,3072]{1,0:T(8,128)(2,1)}, bf16[128,3072]{1,0:T(8,128)(2,1)}, u32[]{:S(2)}, u32[]{:S(2)}) collective-permute-start(bf16[128,3072]{1,0:T(8,128)(2,1)} %shard_map.496), channel_id=1, source_target_pairs={{0,1},{1,0},{2,3},{3,2},{4,5},{5,4},{6,7},{7,6},{8,9},{9,8},{10,11... | collective-permute-start | bytes 2359304 | tf_op jit(solution)/shard_map/ppermute | solution.py:677
  206.6 36.4 %collective-permute-start.38 = (bf16[512,1024]{1,0:T(8,128)(2,1)S(1)}, bf16[512,1024]{1,0:T(8,128)(2,1)}, u32[]{:S(2)}, u32[]{:S(2)}) collective-permute-start(bf16[512,1024]{1,0:T(8,128)(2,1)S(1)} %copy-done.7), channel_id=1, source_target_pairs={{0,4},{4,0},{1,5},{5,1},{2,6},{6,2},{3,7},{7,3},{8,12},{12,8},{9,1... | collective-permute-start | bytes 3145736 | tf_op jit(solution)/shard_map/ppermute | solution.py:677
  226.7 42.6 %collective-permute-start.40 = (bf16[2048,512]{1,0:T(8,128)(2,1)}, bf16[2048,512]{1,0:T(8,128)(2,1)}, u32[]{:S(2)}, u32[]{:S(2)}) collective-permute-start(bf16[2048,512]{1,0:T(8,128)(2,1)} %convolution_convert_fusion.3), channel_id=1, source_target_pairs={{0,2},{2,0},{1,3},{3,1},{4,6},{6,4},{5,7},{7,5},{8,10},{10,8},{9,1... | collective-permute-start | bytes 6291464 | tf_op jit(solution)/shard_map/ppermute | solution.py:677
  266.7 33.0 %collective-permute-start.43 = (bf16[512,2048]{1,0:T(8,128)(2,1)}, bf16[512,2048]{1,0:T(8,128)(2,1)}, u32[]{:S(2)}, u32[]{:S(2)}) collective-permute-start(bf16[512,2048]{1,0:T(8,128)(2,1)} %convolution_convert_fusion.1), channel_id=1, source_target_pairs={{0,2},{2,0},{1,3},{3,1},{4,6},{6,4},{5,7},{7,5},{8,10},{10,8},{9,1... | collective-permute-start | bytes 6291464 | tf_op jit(solution)/shard_map/ppermute | solution.py:677
  273.3 40.6 %all-to-all-start.1 = ((bf16[16,64,512]{2,1,0:T(8,128)(2,1)}), bf16[16,64,512]{2,1,0:T(8,128)(2,1)}, u32[]{:S(2)}, u32[]{:S(2)}) async-start(bf16[16,64,512]{2,1,0:T(8,128)(2,1)} %bitcast.139), calls=%async_computation.1 | async-start | bytes 2097152 | tf_op jit(solution)/shard_map/all_to_all | solution.py:1075
  306.2 38.0 %collective-permute-start.54 = (bf16[512,2048]{1,0:T(8,128)(2,1)}, bf16[512,2048]{1,0:T(8,128)(2,1)}, u32[]{:S(2)}, u32[]{:S(2)}) collective-permute-start(bf16[512,2048]{1,0:T(8,128)(2,1)} %convolution_convert_fusion), channel_id=1, source_target_pairs={{0,2},{2,0},{1,3},{3,1},{4,6},{6,4},{5,7},{7,5},{8,10},{10,8},{9,1... | collective-permute-start | bytes 6291464 | tf_op jit(solution)/shard_map/ppermute | solution.py:677
  310.9 31.9 %collective-permute-start.55 = (bf16[256,2560]{1,0:T(8,128)(2,1)}, bf16[256,2560]{1,0:T(8,128)(2,1)}, u32[]{:S(2)}, u32[]{:S(2)}) collective-permute-start(bf16[256,2560]{1,0:T(8,128)(2,1)} %pad_maximum_fusion), channel_id=1, source_target_pairs={{0,1},{1,0},{2,3},{3,2},{4,5},{5,4},{6,7},{7,6},{8,9},{9,8},{10,11... | collective-permute-start | bytes 3932168 | tf_op jit(solution)/shard_map/ppermute | solution.py:677
  313.4 63.5 %collective-permute-start.58 = (bf16[256,2560]{1,0:T(8,128)(2,1)}, bf16[256,2560]{1,0:T(8,128)(2,1)}, u32[]{:S(2)}, u32[]{:S(2)}) collective-permute-start(bf16[256,2560]{1,0:T(8,128)(2,1)} %pad_maximum_fusion.1), channel_id=1, source_target_pairs={{0,1},{1,0},{2,3},{3,2},{4,5},{5,4},{6,7},{7,6},{8,9},{9,8},{10,11... | collective-permute-start | bytes 3932168 | tf_op jit(solution)/shard_map/ppermute | solution.py:677
  363.6 37.2 %collective-permute-start.61 = (bf16[512,512]{1,0:T(8,128)(2,1)S(1)}, bf16[512,512]{1,0:T(8,128)(2,1)S(1)}, u32[]{:S(2)}, u32[]{:S(2)}) collective-permute-start(bf16[512,512]{1,0:T(8,128)(2,1)S(1)} %fusion.24), channel_id=1, source_target_pairs={{0,16},{8,24},{16,0},{24,8},{1,17},{9,25},{17,1},{25,9},{2,18},{10... | collective-permute-start | bytes 1572872 | tf_op jit(solution)/shard_map/ppermute | solution.py:829
  403.0 39.7 %collective-permute-start.62 = (bf16[128,2560]{1,0:T(8,128)(2,1)S(1)}, bf16[128,2560]{1,0:T(8,128)(2,1)S(1)}, u32[]{:S(2)}, u32[]{:S(2)}) collective-permute-start(bf16[128,2560]{1,0:T(8,128)(2,1)S(1)} %fusion.22), channel_id=1, source_target_pairs={{0,16},{8,24},{16,0},{24,8},{1,17},{9,25},{17,1},{25,9},{2,18},{10... | collective-permute-start | bytes 1966088 | tf_op jit(solution)/shard_map/ppermute | solution.py:829
  463.5 90.6 %all-to-all-start.2 = ((bf16[16,192,512]{2,1,0:T(8,128)(2,1)}), bf16[16,192,512]{2,1,0:T(8,128)(2,1)}, u32[]{:S(2)}, u32[]{:S(2)}) async-start(bf16[16,192,512]{2,1,0:T(8,128)(2,1)} %shard_map.509.grad_ref), calls=%async_computation.2 | async-start | bytes 6291456 | tf_op jit(solution)/shard_map/all_to_all | solution.py:1115
  468.7 38.6 %collective-permute-start.68 = (bf16[128,3072]{1,0:T(8,128)(2,1)}, bf16[128,3072]{1,0:T(8,128)(2,1)}, u32[]{:S(2)}, u32[]{:S(2)}) collective-permute-start(bf16[128,3072]{1,0:T(8,128)(2,1)} %collective-permute-done.33.refs_1_), channel_id=1, source_target_pairs={{0,2},{2,0},{1,3},{3,1},{4,6},{6,4},{5,7},{7,5},{8,10},{10,8},{9,1... | collective-permute-start | bytes 2359304 | tf_op jit(solution)/shard_map/ppermute | solution.py:677
  469.1 38.2 %collective-permute-start.69 = (bf16[128,3072]{1,0:T(8,128)(2,1)}, bf16[128,3072]{1,0:T(8,128)(2,1)}, u32[]{:S(2)}, u32[]{:S(2)}) collective-permute-start(bf16[128,3072]{1,0:T(8,128)(2,1)} %collective-permute-done.37.refs_2_), channel_id=1, source_target_pairs={{0,2},{2,0},{1,3},{3,1},{4,6},{6,4},{5,7},{7,5},{8,10},{10,8},{9,1... | collective-permute-start | bytes 2359304 | tf_op jit(solution)/shard_map/ppermute | solution.py:677
  497.5 42.9 %collective-permute-start.67 = (bf16[256,2560]{1,0:T(8,128)(2,1)}, bf16[256,2560]{1,0:T(8,128)(2,1)}, u32[]{:S(2)}, u32[]{:S(2)}) collective-permute-start(bf16[256,2560]{1,0:T(8,128)(2,1)} %bitcast.30.refs_0_), channel_id=1, source_target_pairs={{0,4},{4,0},{1,5},{5,1},{2,6},{6,2},{3,7},{7,3},{8,12},{12,8},{9,1... | collective-permute-start | bytes 3932168 | tf_op jit(solution)/shard_map/ppermute | solution.py:843
  (184 other events, 2286.3 us)

commit v5 on v4

--- a/solution.py
+++ b/solution.py
@@ -11,7 +11,7 @@
 HEADS = 16
 LONG = 2304
 NORM_EPS = 1e-06
-CHUNKS = (2, 3, 3, 3, 3, 2)
+CHUNKS = (2, 4, 3, 2, 3, 2)
 HEAD_DIM = 64
 BLOCK = 512
 FAR = 1e30
@@ -995,6 +995,8 @@
     out_taken, out_part = fetch_fsdp(w_out, 1, normed)
     fc1_taken, fc1_part = fetch_fsdp(w_fc1, 2, normed)
     fc2_taken, fc2_part = fetch_fsdp(w_fc2, 2, normed)
+    if parts == 2:
+        fc2_part = [swap(tie(part, fc1_part[1]), "f") for part in fc2_taken]
     qkv_taken, qkv_part = fetch_fsdp(w_qkv, 2, normed)
     out_full = join_fsdp(w_out, share_cores(out_part))
     beside = [
@@ -1038,7 +1040,11 @@
     fc1_full = join_fsdp(w_fc1, share_cores(fc1_part), attended)
     fc2_full = join_fsdp(w_fc2, fc2_part, attended)
     small = (b_out, ln2_gain, ln2_bias, b_fc1, b_fc2)
-    packed = join_small(tie(jnp.concatenate(small), normed))
+    packed, at, total = 0.0, 0, sum(vec.shape[0] for vec in small)
+    for vec in small:
+        packed += jnp.pad(vec, (at, total - at - vec.shape[0]))
+        at += vec.shape[0]
+    packed = join_small(tie(packed, normed))
     vectors, at = [], 0
     for vec in small:
         size = vec.shape[0]

time: 631 us -> 624 us (0.989)
  Pallas kernels: 220 us -> 227 us
    unnamed x242 -> x234, local copies, waits for them, and re-layouts: 27.3 us -> 25.7 us
  transfers between devices with their start and end apart: 97 -> 97, of which waited for: 30 -> 30; matrix products, arithmetic and copies ran while one was open for 20% -> 20% of each run, Pallas kernels for 34% -> 36%
where the time goes in v5:
time: 624 us; the launch traced here: 614 us
  Pallas kernels  227 us (36%)
  waiting for transfers between devices  120 us (19%)
  starting transfers between devices  101 us (16%)
  matrix products  95.4 us (15%)
  local copies, waits for them, and re-layouts  36.7 us (6%)
  other arithmetic  31.7 us (5%)
    pallas_call x6, Pallas kernels, attention_backward(): pl.pallas_call(partial(backward_kernel, ends.shape[0], shift, first_block...  98.6 us
    dot_general x25, matrix products, dot(): lax.dot_general(a, b, (((a_dim,), (b_dim,)), ((), ())), preferred_element...  95.4 us
    ppermute x67, waiting for transfers between devices, swap(): return lax.ppermute(x, axis, SWAP)  62.1 us
    pallas_call x7, Pallas kernels, place(): pl.pallas_call(partial(place_kernel, owner), out_shape=jax.ShapeDtypeStru...  46.8 us
    ppermute x67, starting transfers between devices, swap(): return lax.ppermute(x, axis, SWAP)  42.6 us
    pallas_call x1, Pallas kernels, attention_forward(): pl.pallas_call(partial(forward_kernel, ends.shape[0], shift, blocks), out...  39.3 us
    unnamed x234, local copies, waits for them, and re-layouts  25.7 us
    ppermute x2, waiting for transfers between devices, back_y(): self.near = lax.ppermute(x, 'y', SWAP)  17.4 us
  transfers between devices with their start and end apart: 97, of which 30 were waited for; matrix products, arithmetic and copies ran while one was open for 20% of the time, Pallas kernels for 36%

profile of v5, /device:TPU:0, one launch (start us, length us, event | category | flops | bytes accessed | tf_op | source)
XLA Modules:
  0.0 614.3 jit_solution(646860944739337860)
XLA Ops:
  47.5 13.2 %collective-permute-done.9.refs_3_ = bf16[192,512]{1,0:T(8,128)(2,1)S(1)} collective-permute-done((bf16[192,512]{1,0:T(8,128)(2,1)S(1)}, bf16[192,512]{1,0:T(8,128)(2,1)S(1)}, u32[]{:S(2)}, u32[]{:S(2)}) %collective-permute-start.9) | collective-permute-done | bytes 196640 | tf_op jit(solution)/shard_map/ppermute | solution.py:677
  86.7 13.4 %collective-permute-done.16.refs_7_ = bf16[192,512]{1,0:T(8,128)(2,1)S(1)} collective-permute-done((bf16[192,512]{1,0:T(8,128)(2,1)}, bf16[192,512]{1,0:T(8,128)(2,1)S(1)}, u32[]{:S(2)}, u32[]{:S(2)}) %collective-permute-start.16) | collective-permute-done | bytes 196640 | tf_op jit(solution)/shard_map/ppermute | solution.py:677
  126.6 39.3 %shard_map.501 = (bf16[16,64,512]{2,1,0:T(8,128)(2,1)}, f32[1,8192]{1,0:T(1,128)S(1)}, bf16[16,192,512]{2,1,0:T(8,128)(2,1)}) custom-call(s32[8]{0:T(128)S(1)} %bitcast.117, s32[1]{0:T(128)} %constant.120.clone.1.base_ref, s32[16]{0:T(128)S(1)} %pad_add_fusion.1.refs_0_, bf16[192,512]{1,0:T(8,128)(2,1)S(1)} %copy-done.29, ...), custom_call_target="tpu_custom_call" | custom-call | flops 49999998976 | bytes 4194304 | tf_op jit(solution)/shard_map/pallas_call | solution.py:325
  166.6 7.0 %all-to-all-start = ((bf16[16,64,512]{2,1,0:T(8,128)(2,1)}), bf16[16,64,512]{2,1,0:T(8,128)(2,1)}, u32[]{:S(2)}, u32[]{:S(2)}) async-start(bf16[16,64,512]{2,1,0:T(8,128)(2,1)} %get-tuple-element.184.refs_0_), calls=%async_computation | async-start | bytes 2097152 | tf_op jit(solution)/shard_map/all_to_all | solution.py:1054
  180.8 8.9 %shard_map.503 = bf16[1024,4096]{1,0:T(8,128)(2,1)} custom-call(s32[8]{0:T(128)} %multiply_add_fusion.2.row_ref, s32[8]{0:T(128)} %broadcast_17_col_ref.2.col_ref, bf16[512,4096]{1,0:T(8,128)(2,1)} %refs_0_.3, bf16[128,4096]{1,0:T(8,128)(2,1)} %collective-permute-done.19.refs_1_, bf16[128,4096]{1,0:T(8,128)(2,1)} %copy-done.60, ...), custom_call_target="tpu_custom_call" | custom-call | bytes 16777216 | tf_op jit(solution)/shard_map/pallas_call | solution.py:454
  189.7 9.2 %shard_map.502 = bf16[4096,1024]{1,0:T(8,128)(2,1)} custom-call(s32[8]{0:T(128)} %multiply_add_fusion.2.row_ref, s32[8]{0:T(128)} %broadcast_17_col_ref.2.col_ref, bf16[2048,1024]{1,0:T(8,128)(2,1)} %refs_0_.2, bf16[512,1024]{1,0:T(8,128)(2,1)} %collective-permute-done.30.refs_1_, bf16[512,1024]{1,0:T(8,128)(2,1)} %collective-permute-done.31.refs_2_, ...), custom_call_target="tpu_custom_call" | custom-call | bytes 16777216 | tf_op jit(solution)/shard_map/pallas_call | solution.py:454
  208.7 8.5 %multiply_convert_fusion = (bf16[512,4096]{1,0:T(8,128)(2,1)S(1)}, f32[512,4096]{1,0:T(8,128)}) fusion(f32[4096]{0:T(1024)S(1)} %bitcast.154, bf16[512,1024]{1,0:T(8,128)(2,1)S(1)} %add_convert_fusion.8, bf16[1024,4096]{1,0:T(8,128)(2,1)S(1)} %copy-done.53), kind=kOutput, calls=%fused_computation.10 | convolution fusion | flops 4315938816 | bytes 22036480 | tf_op jit(solution)/shard_map/dot_general | solution.py:657
  223.6 12.5 %convert_reduce_fusion = (f32[4096]{0:T(1024)S(1)}, bf16[512,4096]{1,0:T(8,128)(2,1)S(1)}) fusion(f32[512,4096]{1,0:T(8,128)} %get-tuple-element.318, f32[4096]{0:T(1024)S(1)} %bitcast.155, bf16[512,1024]{1,0:T(8,128)(2,1)S(1)} %bitcast.130, bf16[4096,1024]{1,0:T(8,128)(2,1)S(1)} %bitcast.125), kind=kOutput, calls=%fused_computation.9 | convolution fusion | flops 4343197696 | bytes 22052864 | tf_op jit(solution)/shard_map/dot_general | solution.py:657
  244.3 7.6 %multiply_reduce_fusion = (f32[1024]{0:T(1024)S(1)}, f32[512]{0:T(512)S(1)}, f32[512]{0:T(512)S(1)}, f32[1024]{0:T(1024)S(1)}, f32[512,1024]{1,0:T(8,128)S(1)}) fusion(f32[512,1024]{1,0:T(8,128)S(1)} %get-tuple-element.296, f32[512]{0:T(512)S(1)} %add_rsqrt_fusion, f32[512]{0:T(512)S(1)} %broadcast_multiply_fusion.5, f32[1024]{0:T(1024)S(1)} %bitcast.149, ...), kind=kOutput, calls=%fused_computation.22 | convolution fusion | flops 4299682816 | bytes 16797696 | tf_op jit(solution)/shard_map/dot_general | solution.py:657
  280.0 7.6 %collective-permute-done.42 = bf16[1024,512]{1,0:T(8,128)(2,1)} collective-permute-done((bf16[1024,512]{1,0:T(8,128)(2,1)}, bf16[1024,512]{1,0:T(8,128)(2,1)}, u32[]{:S(2)}, u32[]{:S(2)}) %collective-permute-start.42) | collective-permute-done | bytes 1048608 | tf_op jit(solution)/shard_map/ppermute | solution.py:677
  306.4 10.2 %shard_map.504 = (bf16[16,192,512]{2,1,0:T(8,128)(2,1)}, f32[8192,128]{1,0:T(8,128)}) custom-call(s32[8]{0:T(128)S(1)} %bitcast.118, s32[1]{0:T(128)} %constant.120.clone.1.base_ref, bf16[16,192,512]{2,1,0:T(8,128)(2,1)} %get-tuple-element.220.own_ref, bf16[16,64,512]{2,1,0:T(8,128)(2,1)} %get-tuple-element.184.refs_0_, ...), custom_call_target="tpu_custom_call" | custom-call | flops 9374999552 | bytes 1048576 | tf_op jit(solution)/shard_map/pallas_call | solution.py:384
  318.6 6.7 %collective-permute-done.53 = bf16[1024,512]{1,0:T(8,128)(2,1)S(1)} collective-permute-done((bf16[1024,512]{1,0:T(8,128)(2,1)}, bf16[1024,512]{1,0:T(8,128)(2,1)S(1)}, u32[]{:S(2)}, u32[]{:S(2)}) %collective-permute-start.53) | collective-permute-done | bytes 1048608 | tf_op jit(solution)/shard_map/ppermute | solution.py:807
  341.1 20.4 %shard_map.505 = (bf16[16,192,512]{2,1,0:T(8,128)(2,1)}, f32[8192,128]{1,0:T(8,128)}) custom-call(s32[8]{0:T(128)S(1)} %bitcast.119, s32[1]{0:T(128)} %constant.120.clone.1.base_ref, bf16[16,192,512]{2,1,0:T(8,128)(2,1)} %get-tuple-element.220.own_ref, ...), custom_call_target="tpu_custom_call", output_to_operand_aliasing={{0}: (7, {}), {1}: (6, {})} | custom-call | flops 18749999104 | bytes 2097152 | tf_op jit(solution)/shard_map/pallas_call | solution.py:384
  375.3 17.9 %shard_map.506 = (bf16[16,192,512]{2,1,0:T(8,128)(2,1)}, f32[8192,128]{1,0:T(8,128)}) custom-call(s32[8]{0:T(128)S(1)} %bitcast.120, s32[1]{0:T(128)} %constant.120.clone.1.base_ref, bf16[16,192,512]{2,1,0:T(8,128)(2,1)} %get-tuple-element.220.own_ref, ...), custom_call_target="tpu_custom_call", output_to_operand_aliasing={{0}: (7, {}), {1}: (6, {})} | custom-call | flops 14062499840 | bytes 1572864 | tf_op jit(solution)/shard_map/pallas_call | solution.py:384
  393.8 7.2 %collective-permute-done.60 = bf16[128,2560]{1,0:T(8,128)(2,1)S(1)} collective-permute-done((bf16[128,2560]{1,0:T(8,128)(2,1)S(1)}, bf16[128,2560]{1,0:T(8,128)(2,1)S(1)}, u32[]{:S(2)}, u32[]{:S(2)}) %collective-permute-start.60) | collective-permute-done | bytes 655392 | tf_op jit(solution)/shard_map/ppermute | solution.py:821
  402.5 18.4 %shard_map.507 = (bf16[16,192,512]{2,1,0:T(8,128)(2,1)}, f32[8192,128]{1,0:T(8,128)}) custom-call(s32[8]{0:T(128)S(1)} %bitcast.121, s32[1]{0:T(128)} %constant.120.clone.1.base_ref, bf16[16,192,512]{2,1,0:T(8,128)(2,1)} %get-tuple-element.220.own_ref, ...), custom_call_target="tpu_custom_call", output_to_operand_aliasing={{0}: (7, {}), {1}: (6, {})} | custom-call | flops 9374999552 | bytes 1048576 | tf_op jit(solution)/shard_map/pallas_call | solution.py:384
  422.5 17.7 %shard_map.508 = (bf16[16,192,512]{2,1,0:T(8,128)(2,1)}, f32[8192,128]{1,0:T(8,128)}) custom-call(s32[8]{0:T(128)S(1)} %bitcast.122, s32[1]{0:T(128)} %constant.120.clone.1.base_ref, bf16[16,192,512]{2,1,0:T(8,128)(2,1)} %get-tuple-element.220.own_ref, ...), custom_call_target="tpu_custom_call", output_to_operand_aliasing={{0}: (7, {}), {1}: (6, {})} | custom-call | flops 14062499840 | bytes 1572864 | tf_op jit(solution)/shard_map/pallas_call | solution.py:384
  445.7 14.2 %shard_map.509.grad_ref = bf16[16,192,512]{2,1,0:T(8,128)(2,1)} custom-call(s32[8]{0:T(128)S(1)} %bitcast.123, s32[1]{0:T(128)} %constant.120.clone.1.base_ref, bf16[16,192,512]{2,1,0:T(8,128)(2,1)} %get-tuple-element.220.own_ref, bf16[16,64,512]{2,1,0:T(8,128)(2,1)} %get-tuple-element.184.refs_0_, ...), custom_call_target="tpu_custom_call", output_to_operand_aliasing={{}: (7, {})} | custom-call | flops 9374999552 | bytes 1048576 | tf_op jit(solution)/shard_map/pallas_call | solution.py:384
  478.5 8.8 %shard_map.510 = f32[192,1024]{1,0:T(8,128)S(1)} custom-call(s32[16]{0:T(128)S(1)} %pad_add_fusion.2.place_ref, bf16[16,192,512]{2,1,0:T(8,128)(2,1)S(1)} %copy-done, bf16[512,1024]{1,0:T(8,128)(2,1)S(1)} %copy-done.5, bf16[512,1024]{1,0:T(8,128)(2,1)} %broadcast_select_fusion.block_ref.refs_1_, bf16[512,1024]{1,0:T(8,128)(2,1)S(1)} %copy-done.2, ...), custom_call_target="tpu_custom_call" | custom-call | flops 6442450944 | bytes 16777216 | tf_op jit(solution)/shard_map/pallas_call | solution.py:586
  495.2 9.4 %collective-permute-done.65 = f32[192,512]{1,0:T(8,128)S(1)} collective-permute-done((f32[192,512]{1,0:T(8,128)S(1)}, f32[192,512]{1,0:T(8,128)S(1)}, u32[]{:S(2)}, u32[]{:S(2)}) %collective-permute-start.65) | collective-permute-done | bytes 393248 | tf_op jit(solution)/shard_map/ppermute | solution.py:726
  504.8 8.0 %shard_map.511 = bf16[1024,3072]{1,0:T(8,128)(2,1)} custom-call(s32[8]{0:T(128)} %multiply_add_fusion.2.row_ref, s32[8]{0:T(128)} %broadcast_17_col_ref.2.col_ref, bf16[512,3072]{1,0:T(8,128)(2,1)} %refs_0_.4, bf16[128,3072]{1,0:T(8,128)(2,1)} %collective-permute-done.34.refs_1_, bf16[128,3072]{1,0:T(8,128)(2,1)} %collective-permute-done.37.refs_2_, ...), custom_call_target="tpu_custom_call" | custom-call | bytes 12582912 | tf_op jit(solution)/shard_map/pallas_call | solution.py:454
  522.3 14.6 %collective-permute-done.67.refs_1_ = bf16[256,2560]{1,0:T(8,128)(2,1)} collective-permute-done((bf16[256,2560]{1,0:T(8,128)(2,1)}, bf16[256,2560]{1,0:T(8,128)(2,1)}, u32[]{:S(2)}, u32[]{:S(2)}) %collective-permute-start.67) | collective-permute-done | bytes 1310752 | tf_op jit(solution)/shard_map/ppermute | solution.py:843
  553.1 9.1 %multiply_reduce_fusion.1 = (f32[1024]{0:T(1024)S(1)}, f32[512]{0:T(512)}, f32[512]{0:T(512)S(1)}, f32[1024]{0:T(1024)S(1)}, f32[512,1024]{1,0:T(8,128)}) fusion(f32[512]{0:T(512)S(1)} %copy-done.87, f32[512]{0:T(512)S(1)} %copy-done.85, bf16[1,512,1024]{2,1,0:T(8,128)(2,1)S(1)} %copy-done.41, bf16[1,512,1024]{2,1,0:T(8,128)(2,1)S(1)} %copy-done.44, ...), kind=kOutput, calls=%fused_computation.24 | convolution fusion | flops 3227513856 | bytes 13651968 | tf_op jit(solution)/shard_map/dot_general | solution.py:657
  575.0 10.3 %fusion.21 = bf16[1,512,1024]{2,1,0:T(8,128)(2,1)} fusion(f32[512,1024]{1,0:T(8,128)S(1)} %copy-done.38, bf16[512,4096]{1,0:T(8,128)(2,1)} %copy-done.63, bf16[4096,1024]{1,0:T(8,128)(2,1)} %shard_map.502, f32[1024]{0:T(1024)S(1)} %bitcast.157), kind=kOutput, calls=%fused_computation.60 | convolution fusion | flops 4296540160 | bytes 15732736 | tf_op jit(solution)/shard_map/dot_general | solution.py:657
  (557 shorter events, 311.6 us)
Async XLA Ops:
  31.5 38.4 %collective-permute-start.11 = (bf16[512,1024]{1,0:T(8,128)(2,1)S(1)}, bf16[512,1024]{1,0:T(8,128)(2,1)}, u32[]{:S(2)}, u32[]{:S(2)}) collective-permute-start(bf16[512,1024]{1,0:T(8,128)(2,1)S(1)} %add_convert_fusion.9.block_ref.refs_0_), channel_id=1, source_target_pairs={{0,4},{4,0},{1,5},{5,1},{2,6},{6,2},{3,7},{7,3},{8,12},{12,8},{9,1... | collective-permute-start | bytes 3145736 | tf_op jit(solution)/shard_map/ppermute | solution.py:677
  70.5 36.7 %collective-permute-start.18 = (bf16[512,1024]{1,0:T(8,128)(2,1)}, bf16[512,1024]{1,0:T(8,128)(2,1)}, u32[]{:S(2)}, u32[]{:S(2)}) collective-permute-start(bf16[512,1024]{1,0:T(8,128)(2,1)} %broadcast_select_fusion.block_ref.refs_1_), channel_id=1, source_target_pairs={{0,4},{4,0},{1,5},{5,1},{2,6},{6,2},{3,7},{7,3},{8,12},{12,8},{9,1... | collective-permute-start | bytes 3145736 | tf_op jit(solution)/shard_map/ppermute | solution.py:677
  72.1 36.1 %collective-permute-start.13 = (bf16[512,1024]{1,0:T(8,128)(2,1)}, bf16[512,1024]{1,0:T(8,128)(2,1)}, u32[]{:S(2)}, u32[]{:S(2)}) collective-permute-start(bf16[512,1024]{1,0:T(8,128)(2,1)} %collective-permute-done.6), channel_id=1, source_target_pairs={{16,24},{17,25},{18,26},{19,27},{20,28},{21,29},{22,30},{23,31}} | collective-permute-start | bytes 3145736 | tf_op jit(solution)/shard_map/ppermute | solution.py:933
  73.7 35.3 %collective-permute-start.14 = (bf16[512,1024]{1,0:T(8,128)(2,1)}, bf16[512,1024]{1,0:T(8,128)(2,1)}, u32[]{:S(2)}, u32[]{:S(2)}) collective-permute-start(bf16[512,1024]{1,0:T(8,128)(2,1)} %collective-permute-done.7), channel_id=1, source_target_pairs={{8,0},{9,1},{10,2},{11,3},{12,4},{13,5},{14,6},{15,7}} | collective-permute-start | bytes 3145736 | tf_op jit(solution)/shard_map/ppermute | solution.py:934
  81.3 31.7 %collective-permute-start.29 = (bf16[128,4096]{1,0:T(8,128)(2,1)}, bf16[128,4096]{1,0:T(8,128)(2,1)S(1)}, u32[]{:S(2)}, u32[]{:S(2)}) collective-permute-start(bf16[128,4096]{1,0:T(8,128)(2,1)} %shard_map.492), channel_id=1, source_target_pairs={{0,1},{1,0},{2,3},{3,2},{4,5},{5,4},{6,7},{7,6},{8,9},{9,8},{10,11... | collective-permute-start | bytes 3145736 | tf_op jit(solution)/shard_map/ppermute | solution.py:677
  115.0 59.3 %collective-permute-start.30 = (bf16[512,1024]{1,0:T(8,128)(2,1)}, bf16[512,1024]{1,0:T(8,128)(2,1)}, u32[]{:S(2)}, u32[]{:S(2)}) collective-permute-start(bf16[512,1024]{1,0:T(8,128)(2,1)} %shard_map.493), channel_id=1, source_target_pairs={{0,1},{1,0},{2,3},{3,2},{4,5},{5,4},{6,7},{7,6},{8,9},{9,8},{10,11... | collective-permute-start | bytes 3145736 | tf_op jit(solution)/shard_map/ppermute | solution.py:677
  118.1 56.6 %collective-permute-start.31 = (bf16[512,1024]{1,0:T(8,128)(2,1)}, bf16[512,1024]{1,0:T(8,128)(2,1)}, u32[]{:S(2)}, u32[]{:S(2)}) collective-permute-start(bf16[512,1024]{1,0:T(8,128)(2,1)} %shard_map.494), channel_id=1, source_target_pairs={{0,1},{1,0},{2,3},{3,2},{4,5},{5,4},{6,7},{7,6},{8,9},{9,8},{10,11... | collective-permute-start | bytes 3145736 | tf_op jit(solution)/shard_map/ppermute | solution.py:677
  119.6 46.9 %collective-permute-start.27 = (bf16[512,1024]{1,0:T(8,128)(2,1)S(1)}, bf16[512,1024]{1,0:T(8,128)(2,1)S(1)}, u32[]{:S(2)}, u32[]{:S(2)}) collective-permute-start(bf16[512,1024]{1,0:T(8,128)(2,1)S(1)} %select_select_fusion.1.block_ref.refs_2_), channel_id=1, source_target_pairs={{0,4},{4,0},{1,5},{5,1},{2,6},{6,2},{3,7},{7,3},{8,12},{12,8},{9,1... | collective-permute-start | bytes 3145736 | tf_op jit(solution)/shard_map/ppermute | solution.py:677
  166.6 34.2 %all-to-all-start = ((bf16[16,64,512]{2,1,0:T(8,128)(2,1)}), bf16[16,64,512]{2,1,0:T(8,128)(2,1)}, u32[]{:S(2)}, u32[]{:S(2)}) async-start(bf16[16,64,512]{2,1,0:T(8,128)(2,1)} %get-tuple-element.184.refs_0_), calls=%async_computation | async-start | bytes 2097152 | tf_op jit(solution)/shard_map/all_to_all | solution.py:1054
  178.3 38.9 %collective-permute-start.37 = (bf16[128,3072]{1,0:T(8,128)(2,1)}, bf16[128,3072]{1,0:T(8,128)(2,1)}, u32[]{:S(2)}, u32[]{:S(2)}) collective-permute-start(bf16[128,3072]{1,0:T(8,128)(2,1)} %shard_map.496), channel_id=1, source_target_pairs={{0,1},{1,0},{2,3},{3,2},{4,5},{5,4},{6,7},{7,6},{8,9},{9,8},{10,11... | collective-permute-start | bytes 2359304 | tf_op jit(solution)/shard_map/ppermute | solution.py:677
  198.9 37.3 %collective-permute-start.38 = (bf16[512,1024]{1,0:T(8,128)(2,1)S(1)}, bf16[512,1024]{1,0:T(8,128)(2,1)}, u32[]{:S(2)}, u32[]{:S(2)}) collective-permute-start(bf16[512,1024]{1,0:T(8,128)(2,1)S(1)} %copy-done.7), channel_id=1, source_target_pairs={{0,4},{4,0},{1,5},{5,1},{2,6},{6,2},{3,7},{7,3},{8,12},{12,8},{9,1... | collective-permute-start | bytes 3145736 | tf_op jit(solution)/shard_map/ppermute | solution.py:677
  219.8 42.6 %collective-permute-start.40 = (bf16[2048,512]{1,0:T(8,128)(2,1)}, bf16[2048,512]{1,0:T(8,128)(2,1)}, u32[]{:S(2)}, u32[]{:S(2)}) collective-permute-start(bf16[2048,512]{1,0:T(8,128)(2,1)} %convolution_convert_fusion.3), channel_id=1, source_target_pairs={{0,2},{2,0},{1,3},{3,1},{4,6},{6,4},{5,7},{7,5},{8,10},{10,8},{9,1... | collective-permute-start | bytes 6291464 | tf_op jit(solution)/shard_map/ppermute | solution.py:677
  259.3 33.5 %collective-permute-start.43 = (bf16[512,2048]{1,0:T(8,128)(2,1)}, bf16[512,2048]{1,0:T(8,128)(2,1)}, u32[]{:S(2)}, u32[]{:S(2)}) collective-permute-start(bf16[512,2048]{1,0:T(8,128)(2,1)} %convolution_convert_fusion.1), channel_id=1, source_target_pairs={{0,2},{2,0},{1,3},{3,1},{4,6},{6,4},{5,7},{7,5},{8,10},{10,8},{9,1... | collective-permute-start | bytes 6291464 | tf_op jit(solution)/shard_map/ppermute | solution.py:677
  265.7 40.7 %all-to-all-start.1 = ((bf16[16,64,512]{2,1,0:T(8,128)(2,1)}), bf16[16,64,512]{2,1,0:T(8,128)(2,1)}, u32[]{:S(2)}, u32[]{:S(2)}) async-start(bf16[16,64,512]{2,1,0:T(8,128)(2,1)} %bitcast.139), calls=%async_computation.1 | async-start | bytes 2097152 | tf_op jit(solution)/shard_map/all_to_all | solution.py:1081
  299.4 37.3 %collective-permute-start.54 = (bf16[512,2048]{1,0:T(8,128)(2,1)}, bf16[512,2048]{1,0:T(8,128)(2,1)}, u32[]{:S(2)}, u32[]{:S(2)}) collective-permute-start(bf16[512,2048]{1,0:T(8,128)(2,1)} %convolution_convert_fusion), channel_id=1, source_target_pairs={{0,2},{2,0},{1,3},{3,1},{4,6},{6,4},{5,7},{7,5},{8,10},{10,8},{9,1... | collective-permute-start | bytes 6291464 | tf_op jit(solution)/shard_map/ppermute | solution.py:677
  303.4 31.9 %collective-permute-start.55 = (bf16[256,2560]{1,0:T(8,128)(2,1)}, bf16[256,2560]{1,0:T(8,128)(2,1)}, u32[]{:S(2)}, u32[]{:S(2)}) collective-permute-start(bf16[256,2560]{1,0:T(8,128)(2,1)} %pad_maximum_fusion), channel_id=1, source_target_pairs={{0,1},{1,0},{2,3},{3,2},{4,5},{5,4},{6,7},{7,6},{8,9},{9,8},{10,11... | collective-permute-start | bytes 3932168 | tf_op jit(solution)/shard_map/ppermute | solution.py:677
  305.6 63.7 %collective-permute-start.58 = (bf16[256,2560]{1,0:T(8,128)(2,1)}, bf16[256,2560]{1,0:T(8,128)(2,1)}, u32[]{:S(2)}, u32[]{:S(2)}) collective-permute-start(bf16[256,2560]{1,0:T(8,128)(2,1)} %pad_maximum_fusion.1), channel_id=1, source_target_pairs={{0,1},{1,0},{2,3},{3,2},{4,5},{5,4},{6,7},{7,6},{8,9},{9,8},{10,11... | collective-permute-start | bytes 3932168 | tf_op jit(solution)/shard_map/ppermute | solution.py:677
  327.6 33.8 %collective-permute-start.57 = (bf16[512,512]{1,0:T(8,128)(2,1)S(1)}, bf16[512,512]{1,0:T(8,128)(2,1)S(1)}, u32[]{:S(2)}, u32[]{:S(2)}) collective-permute-start(bf16[512,512]{1,0:T(8,128)(2,1)S(1)} %dynamic-slice_bitcast_fusion.1), channel_id=1, source_target_pairs={{0,8},{8,0},{16,24},{24,16},{1,9},{9,1},{17,25},{25,17},{2,10},{10... | collective-permute-start | bytes 1572872 | tf_op jit(solution)/shard_map/ppermute | solution.py:821
  361.6 31.6 %collective-permute-start.61 = (bf16[512,512]{1,0:T(8,128)(2,1)S(1)}, bf16[512,512]{1,0:T(8,128)(2,1)S(1)}, u32[]{:S(2)}, u32[]{:S(2)}) collective-permute-start(bf16[512,512]{1,0:T(8,128)(2,1)S(1)} %fusion.24), channel_id=1, source_target_pairs={{0,16},{8,24},{16,0},{24,8},{1,17},{9,25},{17,1},{25,9},{2,18},{10... | collective-permute-start | bytes 1572872 | tf_op jit(solution)/shard_map/ppermute | solution.py:829
  401.1 39.1 %collective-permute-start.62 = (bf16[128,2560]{1,0:T(8,128)(2,1)S(1)}, bf16[128,2560]{1,0:T(8,128)(2,1)S(1)}, u32[]{:S(2)}, u32[]{:S(2)}) collective-permute-start(bf16[128,2560]{1,0:T(8,128)(2,1)S(1)} %fusion.22), channel_id=1, source_target_pairs={{0,16},{8,24},{16,0},{24,8},{1,17},{9,25},{17,1},{25,9},{2,18},{10... | collective-permute-start | bytes 1966088 | tf_op jit(solution)/shard_map/ppermute | solution.py:829
  461.2 89.5 %all-to-all-start.2 = ((bf16[16,192,512]{2,1,0:T(8,128)(2,1)}), bf16[16,192,512]{2,1,0:T(8,128)(2,1)}, u32[]{:S(2)}, u32[]{:S(2)}) async-start(bf16[16,192,512]{2,1,0:T(8,128)(2,1)} %shard_map.509.grad_ref), calls=%async_computation.2 | async-start | bytes 6291456 | tf_op jit(solution)/shard_map/all_to_all | solution.py:1121
  466.9 37.9 %collective-permute-start.68 = (bf16[128,3072]{1,0:T(8,128)(2,1)}, bf16[128,3072]{1,0:T(8,128)(2,1)}, u32[]{:S(2)}, u32[]{:S(2)}) collective-permute-start(bf16[128,3072]{1,0:T(8,128)(2,1)} %collective-permute-done.34.refs_1_), channel_id=1, source_target_pairs={{0,2},{2,0},{1,3},{3,1},{4,6},{6,4},{5,7},{7,5},{8,10},{10,8},{9,1... | collective-permute-start | bytes 2359304 | tf_op jit(solution)/shard_map/ppermute | solution.py:677
  467.4 37.4 %collective-permute-start.69 = (bf16[128,3072]{1,0:T(8,128)(2,1)}, bf16[128,3072]{1,0:T(8,128)(2,1)}, u32[]{:S(2)}, u32[]{:S(2)}) collective-permute-start(bf16[128,3072]{1,0:T(8,128)(2,1)} %collective-permute-done.37.refs_2_), channel_id=1, source_target_pairs={{0,2},{2,0},{1,3},{3,1},{4,6},{6,4},{5,7},{7,5},{8,10},{10,8},{9,1... | collective-permute-start | bytes 2359304 | tf_op jit(solution)/shard_map/ppermute | solution.py:677
  493.2 43.7 %collective-permute-start.67 = (bf16[256,2560]{1,0:T(8,128)(2,1)}, bf16[256,2560]{1,0:T(8,128)(2,1)}, u32[]{:S(2)}, u32[]{:S(2)}) collective-permute-start(bf16[256,2560]{1,0:T(8,128)(2,1)} %bitcast.30.refs_0_), channel_id=1, source_target_pairs={{0,4},{4,0},{1,5},{5,1},{2,6},{6,2},{3,7},{7,3},{8,12},{12,8},{9,1... | collective-permute-start | bytes 3932168 | tf_op jit(solution)/shard_map/ppermute | solution.py:843
  (182 other events, 2218.4 us)

commit v6 on v5

--- a/solution.py
+++ b/solution.py
@@ -1125,6 +1125,8 @@
         head_grad,
         column + near_blocks + across,
     )
+    block_out = dot(tie(active_low, weight_part), fc2_full, 1, 0) + fc2_bias
+    block_out = (middle + block_out).astype(low)
     weight_part = weight_part.reshape(3 * HEAD_DIM, parts, shard_rows).transpose(1, 0, 2)
     if parts == 2:
         weight_part = halve(weight_part, "f")
@@ -1134,14 +1136,15 @@
         weight_part = lax.psum(weight_part, "g")
 
     weight_part = (weight_part * scale).astype(low)
-    qkv_full = join_fsdp(w_qkv, qkv_part, weight_part)
+    qkv_full = join_fsdp(w_qkv, qkv_part, weight_part, block_out)
     (fc2_grad,) = fc2_sum.results(qkv_full)
     fc1_grad, out_weight_grad = rest_sum.results(fc2_grad)
-    token_grad = tie(token_grad, fc1_grad, out_weight_grad)
-    block_out = middle + (dot(tie(active_low, weight_part), fc2_full, 1, 0) + fc2_bias)
     hops = [weight_part] + [
         lax.ppermute(weight_part, "z", [(i, (i + k) % 4) for i in range(4)]) for k in range(1, 4)
     ]
+    token_grad, fc1_grad, out_weight_grad, *hops = lax.optimization_barrier(
+        (token_grad, fc1_grad, out_weight_grad, *hops)
+    )
 
     token_grad = (
         tie(token_grad, fc2_grad).reshape(HEADS, 3, HEAD_DIM, rows).transpose(1, 0, 2, 3).reshape(3 * width, rows)
@@ -1171,11 +1174,10 @@
         ),
         scale,
     )
-    hops = [tie(piece, gain_one_grad) for piece in hops]
     token = late.core()
     token = late.other_f(token)
     pieces = hops + [swap(piece, "y") for piece in hops]
-    pieces += [swap(tie(piece, token), "c") for piece in pieces]
+    pieces += [swap(tie(piece, gain_one_grad), "c") for piece in pieces]
     token = late.near_y(token)
     token = late.near_z(token)
     late.far_z(token)
@@ -1189,7 +1191,7 @@
         ln2_gain_sum, ln2_bias_sum, fc1_bias_sum, fc2_bias_sum,
     ) = late.vectors()
     return (
-        block_out.astype(low)[None],
+        block_out[None],
         patch_grad[None],
         ln1_gain_sum,
         ln1_bias_sum,

time: 624 us -> 615 us (0.986)
  Pallas kernels: 227 us -> 215 us
  starting transfers between devices: 101 us -> 113 us
  waiting for transfers between devices: 120 us -> 110 us
    ppermute x1, waiting for transfers between devices: 9.42 us -> 0.01 us  [halve(): got = lax.ppermute(pick(x, 1 - here), axis, pairs)]
    pallas_call x6, Pallas kernels: 98.6 us -> 90.1 us  [attention_backward(): pl.pallas_call(partial(backward_kernel, ends.shape[0], shift, first_block...]
    unnamed x234 -> x228, local copies, waits for them, and re-layouts: 25.7 us -> 25.5 us
  transfers between devices with their start and end apart: 97 -> 97, of which waited for: 30 -> 26; matrix products, arithmetic and copies ran while one was open for 20% -> 21% of each run, Pallas kernels for 36% -> 34%
where the time goes in v6:
time: 615 us; the launch traced here: 604 us
  Pallas kernels  215 us (35%)
  starting transfers between devices  113 us (18%)
  waiting for transfers between devices  110 us (18%)
  matrix products  94.5 us (15%)
  local copies, waits for them, and re-layouts  37 us (6%)
  other arithmetic  32.8 us (5%)
    dot_general x25, matrix products, dot(): lax.dot_general(a, b, (((a_dim,), (b_dim,)), ((), ())), preferred_element...  94.5 us
    pallas_call x6, Pallas kernels, attention_backward(): pl.pallas_call(partial(backward_kernel, ends.shape[0], shift, first_block...  90.1 us
    ppermute x67, waiting for transfers between devices, swap(): return lax.ppermute(x, axis, SWAP)  60.3 us
    pallas_call x7, Pallas kernels, place(): pl.pallas_call(partial(place_kernel, owner), out_shape=jax.ShapeDtypeStru...  46.7 us
    ppermute x67, starting transfers between devices, swap(): return lax.ppermute(x, axis, SWAP)  46.4 us
    pallas_call x1, Pallas kernels, attention_forward(): pl.pallas_call(partial(forward_kernel, ends.shape[0], shift, blocks), out...  35.5 us
    unnamed x228, local copies, waits for them, and re-layouts  25.5 us
    ppermute x2, waiting for transfers between devices, back_y(): self.near = lax.ppermute(x, 'y', SWAP)  19.5 us
  transfers between devices with their start and end apart: 97, of which 26 were waited for; matrix products, arithmetic and copies ran while one was open for 21% of the time, Pallas kernels for 34%

profile of v6, /device:TPU:0, one launch (start us, length us, event | category | flops | bytes accessed | tf_op | source)
XLA Modules:
  0.0 604.1 jit_solution(17220913695215875399)
XLA Ops:
  47.5 13.3 %collective-permute-done.9.refs_3_ = bf16[192,512]{1,0:T(8,128)(2,1)S(1)} collective-permute-done((bf16[192,512]{1,0:T(8,128)(2,1)S(1)}, bf16[192,512]{1,0:T(8,128)(2,1)S(1)}, u32[]{:S(2)}, u32[]{:S(2)}) %collective-permute-start.9) | collective-permute-done | bytes 196640 | tf_op jit(solution)/shard_map/ppermute | solution.py:677
  86.7 13.4 %collective-permute-done.16.refs_7_ = bf16[192,512]{1,0:T(8,128)(2,1)S(1)} collective-permute-done((bf16[192,512]{1,0:T(8,128)(2,1)}, bf16[192,512]{1,0:T(8,128)(2,1)S(1)}, u32[]{:S(2)}, u32[]{:S(2)}) %collective-permute-start.16) | collective-permute-done | bytes 196640 | tf_op jit(solution)/shard_map/ppermute | solution.py:677
  126.7 35.5 %shard_map.501 = (bf16[16,64,512]{2,1,0:T(8,128)(2,1)}, f32[1,8192]{1,0:T(1,128)S(1)}, bf16[16,192,512]{2,1,0:T(8,128)(2,1)}) custom-call(s32[8]{0:T(128)S(1)} %bitcast.116, s32[1]{0:T(128)} %constant.120.clone.1.base_ref, s32[16]{0:T(128)S(1)} %pad_add_fusion.1.refs_0_, bf16[192,512]{1,0:T(8,128)(2,1)S(1)} %copy-done.29, ...), custom_call_target="tpu_custom_call" | custom-call | flops 49999998976 | bytes 4194304 | tf_op jit(solution)/shard_map/pallas_call | solution.py:325
  162.8 7.1 %all-to-all-start = ((bf16[16,64,512]{2,1,0:T(8,128)(2,1)}), bf16[16,64,512]{2,1,0:T(8,128)(2,1)}, u32[]{:S(2)}, u32[]{:S(2)}) async-start(bf16[16,64,512]{2,1,0:T(8,128)(2,1)} %get-tuple-element.186.refs_0_), calls=%async_computation | async-start | bytes 2097152 | tf_op jit(solution)/shard_map/all_to_all | solution.py:1054
  179.2 8.9 %shard_map.503 = bf16[1024,4096]{1,0:T(8,128)(2,1)} custom-call(s32[8]{0:T(128)} %multiply_add_fusion.2.row_ref, s32[8]{0:T(128)} %broadcast_17_col_ref.2.col_ref, bf16[512,4096]{1,0:T(8,128)(2,1)} %refs_0_.3, bf16[128,4096]{1,0:T(8,128)(2,1)} %collective-permute-done.19.refs_1_, bf16[128,4096]{1,0:T(8,128)(2,1)} %copy-done.58, ...), custom_call_target="tpu_custom_call" | custom-call | bytes 16777216 | tf_op jit(solution)/shard_map/pallas_call | solution.py:454
  188.1 9.1 %shard_map.502 = bf16[4096,1024]{1,0:T(8,128)(2,1)} custom-call(s32[8]{0:T(128)} %multiply_add_fusion.2.row_ref, s32[8]{0:T(128)} %broadcast_17_col_ref.2.col_ref, bf16[2048,1024]{1,0:T(8,128)(2,1)} %refs_0_.2, bf16[512,1024]{1,0:T(8,128)(2,1)} %collective-permute-done.30.refs_1_, bf16[512,1024]{1,0:T(8,128)(2,1)} %collective-permute-done.31.refs_2_, ...), custom_call_target="tpu_custom_call" | custom-call | bytes 16777216 | tf_op jit(solution)/shard_map/pallas_call | solution.py:454
  207.0 8.5 %multiply_convert_fusion = (bf16[512,4096]{1,0:T(8,128)(2,1)S(1)}, f32[512,4096]{1,0:T(8,128)}) fusion(f32[4096]{0:T(1024)S(1)} %bitcast.160, bf16[512,1024]{1,0:T(8,128)(2,1)S(1)} %add_convert_fusion.8, bf16[1024,4096]{1,0:T(8,128)(2,1)S(1)} %copy-done.52), kind=kOutput, calls=%fused_computation.10 | convolution fusion | flops 4315938816 | bytes 22036480 | tf_op jit(solution)/shard_map/dot_general | solution.py:657
  222.0 12.5 %convert_reduce_fusion = (f32[4096]{0:T(1024)S(1)}, bf16[512,4096]{1,0:T(8,128)(2,1)S(1)}) fusion(f32[512,4096]{1,0:T(8,128)} %get-tuple-element.322, f32[4096]{0:T(1024)S(1)} %bitcast.161, bf16[512,1024]{1,0:T(8,128)(2,1)S(1)} %bitcast.136, bf16[4096,1024]{1,0:T(8,128)(2,1)S(1)} %bitcast.128), kind=kOutput, calls=%fused_computation.9 | convolution fusion | flops 4343197696 | bytes 22052864 | tf_op jit(solution)/shard_map/dot_general | solution.py:657
  242.8 7.6 %multiply_reduce_fusion = (f32[1024]{0:T(1024)S(1)}, f32[512]{0:T(512)S(1)}, f32[512]{0:T(512)S(1)}, f32[1024]{0:T(1024)S(1)}, f32[512,1024]{1,0:T(8,128)S(1)}) fusion(f32[512,1024]{1,0:T(8,128)S(1)} %get-tuple-element.300, f32[512]{0:T(512)S(1)} %add_rsqrt_fusion, f32[512]{0:T(512)S(1)} %broadcast_multiply_fusion.5, f32[1024]{0:T(1024)S(1)} %bitcast.155, ...), kind=kOutput, calls=%fused_computation.22 | convolution fusion | flops 4299682816 | bytes 16797696 | tf_op jit(solution)/shard_map/dot_general | solution.py:657
  278.6 7.4 %collective-permute-done.42 = bf16[1024,512]{1,0:T(8,128)(2,1)} collective-permute-done((bf16[1024,512]{1,0:T(8,128)(2,1)}, bf16[1024,512]{1,0:T(8,128)(2,1)}, u32[]{:S(2)}, u32[]{:S(2)}) %collective-permute-start.42) | collective-permute-done | bytes 1048608 | tf_op jit(solution)/shard_map/ppermute | solution.py:677
  304.9 12.1 %shard_map.504 = (bf16[16,192,512]{2,1,0:T(8,128)(2,1)}, f32[8192,128]{1,0:T(8,128)}) custom-call(s32[8]{0:T(128)S(1)} %bitcast.117, s32[1]{0:T(128)} %constant.120.clone.1.base_ref, bf16[16,192,512]{2,1,0:T(8,128)(2,1)} %get-tuple-element.222.own_ref, bf16[16,64,512]{2,1,0:T(8,128)(2,1)} %get-tuple-element.186.refs_0_, ...), custom_call_target="tpu_custom_call" | custom-call | flops 9374999552 | bytes 1048576 | tf_op jit(solution)/shard_map/pallas_call | solution.py:384
  339.5 20.2 %shard_map.505 = (bf16[16,192,512]{2,1,0:T(8,128)(2,1)}, f32[8192,128]{1,0:T(8,128)}) custom-call(s32[8]{0:T(128)S(1)} %bitcast.118, s32[1]{0:T(128)} %constant.120.clone.1.base_ref, bf16[16,192,512]{2,1,0:T(8,128)(2,1)} %get-tuple-element.222.own_ref, ...), custom_call_target="tpu_custom_call", output_to_operand_aliasing={{0}: (7, {}), {1}: (6, {})} | custom-call | flops 18749999104 | bytes 2097152 | tf_op jit(solution)/shard_map/pallas_call | solution.py:384
  373.8 17.8 %shard_map.506 = (bf16[16,192,512]{2,1,0:T(8,128)(2,1)}, f32[8192,128]{1,0:T(8,128)}) custom-call(s32[8]{0:T(128)S(1)} %bitcast.119, s32[1]{0:T(128)} %constant.120.clone.1.base_ref, bf16[16,192,512]{2,1,0:T(8,128)(2,1)} %get-tuple-element.222.own_ref, ...), custom_call_target="tpu_custom_call", output_to_operand_aliasing={{0}: (7, {}), {1}: (6, {})} | custom-call | flops 14062499840 | bytes 1572864 | tf_op jit(solution)/shard_map/pallas_call | solution.py:384
  392.2 6.9 %collective-permute-done.60 = bf16[128,2560]{1,0:T(8,128)(2,1)S(1)} collective-permute-done((bf16[128,2560]{1,0:T(8,128)(2,1)S(1)}, bf16[128,2560]{1,0:T(8,128)(2,1)S(1)}, u32[]{:S(2)}, u32[]{:S(2)}) %collective-permute-start.60) | collective-permute-done | bytes 655392 | tf_op jit(solution)/shard_map/ppermute | solution.py:821
  400.7 13.4 %shard_map.507 = (bf16[16,192,512]{2,1,0:T(8,128)(2,1)}, f32[8192,128]{1,0:T(8,128)}) custom-call(s32[8]{0:T(128)S(1)} %bitcast.120, s32[1]{0:T(128)} %constant.120.clone.1.base_ref, bf16[16,192,512]{2,1,0:T(8,128)(2,1)} %get-tuple-element.222.own_ref, ...), custom_call_target="tpu_custom_call", output_to_operand_aliasing={{0}: (7, {}), {1}: (6, {})} | custom-call | flops 9374999552 | bytes 1048576 | tf_op jit(solution)/shard_map/pallas_call | solution.py:384
  415.5 14.5 %shard_map.508 = (bf16[16,192,512]{2,1,0:T(8,128)(2,1)}, f32[8192,128]{1,0:T(8,128)}) custom-call(s32[8]{0:T(128)S(1)} %bitcast.121, s32[1]{0:T(128)} %constant.120.clone.1.base_ref, bf16[16,192,512]{2,1,0:T(8,128)(2,1)} %get-tuple-element.222.own_ref, ...), custom_call_target="tpu_custom_call", output_to_operand_aliasing={{0}: (7, {}), {1}: (6, {})} | custom-call | flops 14062499840 | bytes 1572864 | tf_op jit(solution)/shard_map/pallas_call | solution.py:384
  438.3 11.9 %shard_map.509.grad_ref = bf16[16,192,512]{2,1,0:T(8,128)(2,1)} custom-call(s32[8]{0:T(128)S(1)} %bitcast.122, s32[1]{0:T(128)} %constant.120.clone.1.base_ref, bf16[16,192,512]{2,1,0:T(8,128)(2,1)} %get-tuple-element.222.own_ref, bf16[16,64,512]{2,1,0:T(8,128)(2,1)} %get-tuple-element.186.refs_0_, ...), custom_call_target="tpu_custom_call", output_to_operand_aliasing={{}: (7, {})} | custom-call | flops 9374999552 | bytes 1048576 | tf_op jit(solution)/shard_map/pallas_call | solution.py:384
  469.0 8.7 %shard_map.510 = f32[192,1024]{1,0:T(8,128)S(1)} custom-call(s32[16]{0:T(128)S(1)} %pad_add_fusion.2.place_ref, bf16[16,192,512]{2,1,0:T(8,128)(2,1)S(1)} %copy-done, bf16[512,1024]{1,0:T(8,128)(2,1)S(1)} %copy-done.5, bf16[512,1024]{1,0:T(8,128)(2,1)} %broadcast_select_fusion.block_ref.refs_1_, bf16[512,1024]{1,0:T(8,128)(2,1)S(1)} %copy-done.2, ...), custom_call_target="tpu_custom_call" | custom-call | flops 6442450944 | bytes 16777216 | tf_op jit(solution)/shard_map/pallas_call | solution.py:586
  488.3 10.1 %add_convert_fusion = bf16[512,1024]{1,0:T(8,128)(2,1)} fusion(f32[512,1024]{1,0:T(8,128)S(1)} %copy-done.38, bf16[512,4096]{1,0:T(8,128)(2,1)} %copy-done.61, bf16[4096,1024]{1,0:T(8,128)(2,1)} %shard_map.502, f32[1024]{0:T(1024)S(1)} %bitcast.163), kind=kOutput, calls=%fused_computation.27 | convolution fusion | flops 4296540160 | bytes 15732736 | tf_op jit(solution)/shard_map/dot_general | solution.py:657
  498.6 8.0 %shard_map.511 = bf16[1024,3072]{1,0:T(8,128)(2,1)} custom-call(s32[8]{0:T(128)} %multiply_add_fusion.2.row_ref, s32[8]{0:T(128)} %broadcast_17_col_ref.2.col_ref, bf16[512,3072]{1,0:T(8,128)(2,1)} %refs_0_.4, bf16[128,3072]{1,0:T(8,128)(2,1)} %collective-permute-done.34.refs_1_, bf16[128,3072]{1,0:T(8,128)(2,1)} %collective-permute-done.37.refs_2_, ...), custom_call_target="tpu_custom_call" | custom-call | bytes 12582912 | tf_op jit(solution)/shard_map/pallas_call | solution.py:454
  509.6 6.5 %shard_map.512 = f32[2048,1024]{1,0:T(8,128)} custom-call(s32[4]{0:T(128)} %multiply_add_fusion.1.row_ref, s32[4]{0:T(128)} %multiply_add_fusion.col_ref, bf16[1024,512]{1,0:T(8,128)(2,1)} %bitcast.133, bf16[1024,512]{1,0:T(8,128)(2,1)} %copy-done.60, bf16[1024,512]{1,0:T(8,128)(2,1)} %collective-permute-done.70.refs_2_, ...), custom_call_target="tpu_custom_call" | custom-call | bytes 12582912 | tf_op jit(solution)/shard_map/pallas_call | solution.py:454
  516.1 13.4 %collective-permute-done.66.refs_1_ = bf16[256,2560]{1,0:T(8,128)(2,1)} collective-permute-done((bf16[256,2560]{1,0:T(8,128)(2,1)}, bf16[256,2560]{1,0:T(8,128)(2,1)}, u32[]{:S(2)}, u32[]{:S(2)}) %collective-permute-start.66) | collective-permute-done | bytes 1310752 | tf_op jit(solution)/shard_map/ppermute | solution.py:843
  540.7 6.5 %shard_map.513 = f32[512,4096]{1,0:T(8,128)} custom-call(s32[4]{0:T(128)} %multiply_add_fusion.1.row_ref, s32[4]{0:T(128)} %multiply_add_fusion.col_ref, bf16[256,2560]{1,0:T(8,128)(2,1)} %bitcast.125, bf16[256,2560]{1,0:T(8,128)(2,1)} %collective-permute-done.66.refs_1_, bf16[256,2560]{1,0:T(8,128)(2,1)} %collective-permute-done.72.refs_2_, ...), custom_call_target="tpu_custom_call" | custom-call | bytes 12582912 | tf_op jit(solution)/shard_map/pallas_call | solution.py:454
  553.7 8.3 %multiply_reduce_fusion.1 = (f32[1024]{0:T(1024)S(1)}, f32[512]{0:T(512)S(1)}, f32[512]{0:T(512)S(1)}, f32[1024]{0:T(1024)S(1)}, f32[512,1024]{1,0:T(8,128)}) fusion(f32[512]{0:T(512)S(1)} %copy-done.85, f32[512]{0:T(512)S(1)} %copy-done.83, bf16[1,512,1024]{2,1,0:T(8,128)(2,1)S(1)} %copy-done.41, bf16[1,512,1024]{2,1,0:T(8,128)(2,1)S(1)} %copy-done.44, ...), kind=kOutput, calls=%fused_computation.24 | convolution fusion | flops 3227513856 | bytes 13651968 | tf_op jit(solution)/shard_map/dot_general | solution.py:657
  (551 shorter events, 319.3 us)
Async XLA Ops:
  31.6 38.4 %collective-permute-start.11 = (bf16[512,1024]{1,0:T(8,128)(2,1)S(1)}, bf16[512,1024]{1,0:T(8,128)(2,1)}, u32[]{:S(2)}, u32[]{:S(2)}) collective-permute-start(bf16[512,1024]{1,0:T(8,128)(2,1)S(1)} %add_convert_fusion.9.block_ref.refs_0_), channel_id=1, source_target_pairs={{0,4},{4,0},{1,5},{5,1},{2,6},{6,2},{3,7},{7,3},{8,12},{12,8},{9,1... | collective-permute-start | bytes 3145736 | tf_op jit(solution)/shard_map/ppermute | solution.py:677
  70.6 36.7 %collective-permute-start.18 = (bf16[512,1024]{1,0:T(8,128)(2,1)}, bf16[512,1024]{1,0:T(8,128)(2,1)}, u32[]{:S(2)}, u32[]{:S(2)}) collective-permute-start(bf16[512,1024]{1,0:T(8,128)(2,1)} %broadcast_select_fusion.block_ref.refs_1_), channel_id=1, source_target_pairs={{0,4},{4,0},{1,5},{5,1},{2,6},{6,2},{3,7},{7,3},{8,12},{12,8},{9,1... | collective-permute-start | bytes 3145736 | tf_op jit(solution)/shard_map/ppermute | solution.py:677
  72.1 36.1 %collective-permute-start.13 = (bf16[512,1024]{1,0:T(8,128)(2,1)}, bf16[512,1024]{1,0:T(8,128)(2,1)}, u32[]{:S(2)}, u32[]{:S(2)}) collective-permute-start(bf16[512,1024]{1,0:T(8,128)(2,1)} %collective-permute-done.6), channel_id=1, source_target_pairs={{16,24},{17,25},{18,26},{19,27},{20,28},{21,29},{22,30},{23,31}} | collective-permute-start | bytes 3145736 | tf_op jit(solution)/shard_map/ppermute | solution.py:933
  73.8 35.3 %collective-permute-start.14 = (bf16[512,1024]{1,0:T(8,128)(2,1)}, bf16[512,1024]{1,0:T(8,128)(2,1)}, u32[]{:S(2)}, u32[]{:S(2)}) collective-permute-start(bf16[512,1024]{1,0:T(8,128)(2,1)} %collective-permute-done.7), channel_id=1, source_target_pairs={{8,0},{9,1},{10,2},{11,3},{12,4},{13,5},{14,6},{15,7}} | collective-permute-start | bytes 3145736 | tf_op jit(solution)/shard_map/ppermute | solution.py:934
  115.1 58.6 %collective-permute-start.30 = (bf16[512,1024]{1,0:T(8,128)(2,1)}, bf16[512,1024]{1,0:T(8,128)(2,1)}, u32[]{:S(2)}, u32[]{:S(2)}) collective-permute-start(bf16[512,1024]{1,0:T(8,128)(2,1)} %shard_map.493), channel_id=1, source_target_pairs={{0,1},{1,0},{2,3},{3,2},{4,5},{5,4},{6,7},{7,6},{8,9},{9,8},{10,11... | collective-permute-start | bytes 3145736 | tf_op jit(solution)/shard_map/ppermute | solution.py:677
  118.2 55.5 %collective-permute-start.31 = (bf16[512,1024]{1,0:T(8,128)(2,1)}, bf16[512,1024]{1,0:T(8,128)(2,1)}, u32[]{:S(2)}, u32[]{:S(2)}) collective-permute-start(bf16[512,1024]{1,0:T(8,128)(2,1)} %shard_map.494), channel_id=1, source_target_pairs={{0,1},{1,0},{2,3},{3,2},{4,5},{5,4},{6,7},{7,6},{8,9},{9,8},{10,11... | collective-permute-start | bytes 3145736 | tf_op jit(solution)/shard_map/ppermute | solution.py:677
  119.7 43.1 %collective-permute-start.27 = (bf16[512,1024]{1,0:T(8,128)(2,1)S(1)}, bf16[512,1024]{1,0:T(8,128)(2,1)S(1)}, u32[]{:S(2)}, u32[]{:S(2)}) collective-permute-start(bf16[512,1024]{1,0:T(8,128)(2,1)S(1)} %select_select_fusion.1.block_ref.refs_2_), channel_id=1, source_target_pairs={{0,4},{4,0},{1,5},{5,1},{2,6},{6,2},{3,7},{7,3},{8,12},{12,8},{9,1... | collective-permute-start | bytes 3145736 | tf_op jit(solution)/shard_map/ppermute | solution.py:677
  162.8 36.3 %all-to-all-start = ((bf16[16,64,512]{2,1,0:T(8,128)(2,1)}), bf16[16,64,512]{2,1,0:T(8,128)(2,1)}, u32[]{:S(2)}, u32[]{:S(2)}) async-start(bf16[16,64,512]{2,1,0:T(8,128)(2,1)} %get-tuple-element.186.refs_0_), calls=%async_computation | async-start | bytes 2097152 | tf_op jit(solution)/shard_map/all_to_all | solution.py:1054
  177.6 37.9 %collective-permute-start.37 = (bf16[128,3072]{1,0:T(8,128)(2,1)}, bf16[128,3072]{1,0:T(8,128)(2,1)}, u32[]{:S(2)}, u32[]{:S(2)}) collective-permute-start(bf16[128,3072]{1,0:T(8,128)(2,1)} %shard_map.496), channel_id=1, source_target_pairs={{0,1},{1,0},{2,3},{3,2},{4,5},{5,4},{6,7},{7,6},{8,9},{9,8},{10,11... | collective-permute-start | bytes 2359304 | tf_op jit(solution)/shard_map/ppermute | solution.py:677
  197.3 37.2 %collective-permute-start.38 = (bf16[512,1024]{1,0:T(8,128)(2,1)S(1)}, bf16[512,1024]{1,0:T(8,128)(2,1)}, u32[]{:S(2)}, u32[]{:S(2)}) collective-permute-start(bf16[512,1024]{1,0:T(8,128)(2,1)S(1)} %copy-done.7), channel_id=1, source_target_pairs={{0,4},{4,0},{1,5},{5,1},{2,6},{6,2},{3,7},{7,3},{8,12},{12,8},{9,1... | collective-permute-start | bytes 3145736 | tf_op jit(solution)/shard_map/ppermute | solution.py:677
  218.2 42.5 %collective-permute-start.40 = (bf16[2048,512]{1,0:T(8,128)(2,1)}, bf16[2048,512]{1,0:T(8,128)(2,1)}, u32[]{:S(2)}, u32[]{:S(2)}) collective-permute-start(bf16[2048,512]{1,0:T(8,128)(2,1)} %convolution_convert_fusion.3), channel_id=1, source_target_pairs={{0,2},{2,0},{1,3},{3,1},{4,6},{6,4},{5,7},{7,5},{8,10},{10,8},{9,1... | collective-permute-start | bytes 6291464 | tf_op jit(solution)/shard_map/ppermute | solution.py:677
  257.8 33.6 %collective-permute-start.43 = (bf16[512,2048]{1,0:T(8,128)(2,1)}, bf16[512,2048]{1,0:T(8,128)(2,1)}, u32[]{:S(2)}, u32[]{:S(2)}) collective-permute-start(bf16[512,2048]{1,0:T(8,128)(2,1)} %convolution_convert_fusion.1), channel_id=1, source_target_pairs={{0,2},{2,0},{1,3},{3,1},{4,6},{6,4},{5,7},{7,5},{8,10},{10,8},{9,1... | collective-permute-start | bytes 6291464 | tf_op jit(solution)/shard_map/ppermute | solution.py:677
  264.4 40.6 %all-to-all-start.1 = ((bf16[16,64,512]{2,1,0:T(8,128)(2,1)}), bf16[16,64,512]{2,1,0:T(8,128)(2,1)}, u32[]{:S(2)}, u32[]{:S(2)}) async-start(bf16[16,64,512]{2,1,0:T(8,128)(2,1)} %bitcast.145), calls=%async_computation.1 | async-start | bytes 2097152 | tf_op jit(solution)/shard_map/all_to_all | solution.py:1081
  297.9 37.4 %collective-permute-start.54 = (bf16[512,2048]{1,0:T(8,128)(2,1)}, bf16[512,2048]{1,0:T(8,128)(2,1)}, u32[]{:S(2)}, u32[]{:S(2)}) collective-permute-start(bf16[512,2048]{1,0:T(8,128)(2,1)} %convolution_convert_fusion), channel_id=1, source_target_pairs={{0,2},{2,0},{1,3},{3,1},{4,6},{6,4},{5,7},{7,5},{8,10},{10,8},{9,1... | collective-permute-start | bytes 6291464 | tf_op jit(solution)/shard_map/ppermute | solution.py:677
  301.9 31.9 %collective-permute-start.55 = (bf16[256,2560]{1,0:T(8,128)(2,1)}, bf16[256,2560]{1,0:T(8,128)(2,1)}, u32[]{:S(2)}, u32[]{:S(2)}) collective-permute-start(bf16[256,2560]{1,0:T(8,128)(2,1)} %pad_maximum_fusion), channel_id=1, source_target_pairs={{0,1},{1,0},{2,3},{3,2},{4,5},{5,4},{6,7},{7,6},{8,9},{9,8},{10,11... | collective-permute-start | bytes 3932168 | tf_op jit(solution)/shard_map/ppermute | solution.py:677
  303.7 64.1 %collective-permute-start.58 = (bf16[256,2560]{1,0:T(8,128)(2,1)}, bf16[256,2560]{1,0:T(8,128)(2,1)}, u32[]{:S(2)}, u32[]{:S(2)}) collective-permute-start(bf16[256,2560]{1,0:T(8,128)(2,1)} %pad_maximum_fusion.1), channel_id=1, source_target_pairs={{0,1},{1,0},{2,3},{3,2},{4,5},{5,4},{6,7},{7,6},{8,9},{9,8},{10,11... | collective-permute-start | bytes 3932168 | tf_op jit(solution)/shard_map/ppermute | solution.py:677
  326.1 33.6 %collective-permute-start.57 = (bf16[512,512]{1,0:T(8,128)(2,1)S(1)}, bf16[512,512]{1,0:T(8,128)(2,1)S(1)}, u32[]{:S(2)}, u32[]{:S(2)}) collective-permute-start(bf16[512,512]{1,0:T(8,128)(2,1)S(1)} %dynamic-slice_bitcast_fusion.1), channel_id=1, source_target_pairs={{0,8},{8,0},{16,24},{24,16},{1,9},{9,1},{17,25},{25,17},{2,10},{10... | collective-permute-start | bytes 1572872 | tf_op jit(solution)/shard_map/ppermute | solution.py:821
  359.9 31.8 %collective-permute-start.61 = (bf16[512,512]{1,0:T(8,128)(2,1)S(1)}, bf16[512,512]{1,0:T(8,128)(2,1)S(1)}, u32[]{:S(2)}, u32[]{:S(2)}) collective-permute-start(bf16[512,512]{1,0:T(8,128)(2,1)S(1)} %fusion.23), channel_id=1, source_target_pairs={{0,16},{8,24},{16,0},{24,8},{1,17},{9,25},{17,1},{25,9},{2,18},{10... | collective-permute-start | bytes 1572872 | tf_op jit(solution)/shard_map/ppermute | solution.py:829
  451.6 99.4 %all-to-all-start.2 = ((bf16[16,192,512]{2,1,0:T(8,128)(2,1)}), bf16[16,192,512]{2,1,0:T(8,128)(2,1)}, u32[]{:S(2)}, u32[]{:S(2)}) async-start(bf16[16,192,512]{2,1,0:T(8,128)(2,1)} %shard_map.509.grad_ref), calls=%async_computation.2 | async-start | bytes 6291456 | tf_op jit(solution)/shard_map/all_to_all | solution.py:1121
  456.9 41.7 %collective-permute-start.68 = (bf16[128,3072]{1,0:T(8,128)(2,1)}, bf16[128,3072]{1,0:T(8,128)(2,1)}, u32[]{:S(2)}, u32[]{:S(2)}) collective-permute-start(bf16[128,3072]{1,0:T(8,128)(2,1)} %collective-permute-done.34.refs_1_), channel_id=1, source_target_pairs={{0,2},{2,0},{1,3},{3,1},{4,6},{6,4},{5,7},{7,5},{8,10},{10,8},{9,1... | collective-permute-start | bytes 2359304 | tf_op jit(solution)/shard_map/ppermute | solution.py:677
  457.5 41.1 %collective-permute-start.69 = (bf16[128,3072]{1,0:T(8,128)(2,1)}, bf16[128,3072]{1,0:T(8,128)(2,1)}, u32[]{:S(2)}, u32[]{:S(2)}) collective-permute-start(bf16[128,3072]{1,0:T(8,128)(2,1)} %collective-permute-done.37.refs_2_), channel_id=1, source_target_pairs={{0,2},{2,0},{1,3},{3,1},{4,6},{6,4},{5,7},{7,5},{8,10},{10,8},{9,1... | collective-permute-start | bytes 2359304 | tf_op jit(solution)/shard_map/ppermute | solution.py:677
  457.5 50.6 %collective-permute-start.70 = (bf16[1024,512]{1,0:T(8,128)(2,1)}, bf16[1024,512]{1,0:T(8,128)(2,1)}, u32[]{:S(2)}, u32[]{:S(2)}) collective-permute-start(bf16[1024,512]{1,0:T(8,128)(2,1)} %bitcast.132), channel_id=1, source_target_pairs={{0,2},{2,0},{1,3},{3,1},{4,6},{6,4},{5,7},{7,5},{8,10},{10,8},{9,1... | collective-permute-start | bytes 3145736 | tf_op jit(solution)/shard_map/ppermute | solution.py:677
  486.6 42.9 %collective-permute-start.66 = (bf16[256,2560]{1,0:T(8,128)(2,1)}, bf16[256,2560]{1,0:T(8,128)(2,1)}, u32[]{:S(2)}, u32[]{:S(2)}) collective-permute-start(bf16[256,2560]{1,0:T(8,128)(2,1)} %bitcast.123), channel_id=1, source_target_pairs={{0,4},{4,0},{1,5},{5,1},{2,6},{6,2},{3,7},{7,3},{8,12},{12,8},{9,1... | collective-permute-start | bytes 3932168 | tf_op jit(solution)/shard_map/ppermute | solution.py:843
  507.6 33.1 %collective-permute-start.72 = (bf16[256,2560]{1,0:T(8,128)(2,1)}, bf16[256,2560]{1,0:T(8,128)(2,1)}, u32[]{:S(2)}, u32[]{:S(2)}) collective-permute-start(bf16[256,2560]{1,0:T(8,128)(2,1)} %bitcast.124), channel_id=1, source_target_pairs={{0,2},{2,0},{1,3},{3,1},{4,6},{6,4},{5,7},{7,5},{8,10},{10,8},{9,1... | collective-permute-start | bytes 3932168 | tf_op jit(solution)/shard_map/ppermute | solution.py:677
  (179 other events, 2218.6 us)
